TPU v7x, 256 devices: a whole 4x4x8 slice. The times are simulated.
256 devices in a mesh: rows: 32 (over x, z_lo, y), dates: 8 (over z_hi, core).
Axes of the slice: x: 4, y: 4, z: 8 (z_hi: 4, z_lo: 2; z = z_hi * 2 + z_lo), core: 2. Of those that a mesh axis runs over, the one named last changes fastest.
Arguments:
- reflectance: float32 [32, 7, 1024, 1024], P('dates', None, 'rows'), may hold values from 0.05 to 0.9
- sun_zenith: float32 [32, 1024, 1024], P('dates', 'rows'), may hold values from 0.35 to 1
- view_zenith: float32 [32, 1024, 1024], P('dates', 'rows'), may hold values from 0 to 0.2
- rel_azimuth: float32 [32, 1024, 1024], P('dates', 'rows'), may hold values from -3.140625 to 3.140625
- flags: int32 [32, 1024, 1024], P('dates', 'rows'), may hold values from 0 to 3
- nadir_sun: float32 [1024, 1024], P('rows'), may hold values from 0.5 to 0.8
Outputs:
- normalized: float32 [32, 7, 1024, 1024], P('dates', None, 'rows')
All inputs are finite; a program needn't handle non-finite values.
Results may differ from a plain program's by a relative error of at most 0.0003.
Values sent between devices are 32-bit elements; how exact they have to be, the bound alone decides.
No kernel may reach another device: no remote copies, remote signals or barrier semaphores. Data moves between devices by JAX's collectives and lax.ppermute only.
A program may use at most 128 MiB of HBM per device.

v0:
```python
import math

import jax
import jax.numpy as jnp
from jax import lax
from jax.experimental import pallas as pl
from jax.experimental.pallas import tpu as pltpu
from jax.sharding import PartitionSpec as P

ridge_weight = 0.5
model_floor = 0.35
LANES = 128
SUB = 8
VMEM = pl.BlockSpec(memory_space=pltpu.VMEM)


SIN_SUN = (1.0, -0.1666666643, 0.008333314069, -0.0001983586641, 2.693759761e-06)
COS_SUN = (1.0, -0.4999999999, 0.04166666582, -0.001388885292, 2.479463838e-05, -2.693749222e-07)
SIN_VIEW = (1.0, -0.1666664847, 0.008321317392)
COS_VIEW = (1.0, -0.4999987263, 0.04158257081)
SIN_HALF = (1.0, -0.1666666662, 0.008333330977, -0.0001984086155, 2.752528678e-06, -2.388949223e-08)
GEO_POLY = (
    1.570796328, -1.214602072, -0.4109448018, 0.07413550608, -0.02841817795,
    0.01338202682, -0.005993092577, 0.001966222815, -0.0003219403671,
)
VOL_POLY = (
    0.999999995, -1.070795655, 0.08958698627, -0.02642109245, 0.01117480515,
    -0.004945099414, 0.001698688062, -0.0002986314728,
)


def poly(x, coefs):
    total = jnp.full_like(x, coefs[-1])
    for c in coefs[-2::-1]:
        total = total * x + c
    return total


def sin_cos_sun(sun):
    sq = sun * sun
    return sun * poly(sq, SIN_SUN), poly(sq, COS_SUN)


def shadow_term(cos_shadow):
    return jnp.sqrt(1.0 - cos_shadow) * poly(cos_shadow, GEO_POLY)


def ross_li(sun, view, azim):
    sin_s, cos_s = sin_cos_sun(sun)
    view_sq = view * view
    sin_v = view * poly(view_sq, SIN_VIEW)
    cos_v = poly(view_sq, COS_VIEW)
    half = 0.5 * azim
    sin_h = half * poly(half * half, SIN_HALF)
    half_sq = sin_h * sin_h
    cos_a = 1.0 - 2.0 * half_sq
    sin_a_sq = 4.0 * half_sq * (1.0 - half_sq)
    cos_cos = cos_s * cos_v
    sin_sin = sin_s * sin_v
    cos_phase = jnp.clip(cos_cos + sin_sin * cos_a, -1.0, 1.0)
    cos_sum = cos_s + cos_v
    inv = 1.0 / (cos_cos * cos_sum)
    sec_sec = cos_sum * inv
    inv_sum = cos_cos * inv
    kvol = (
        (0.5 * math.pi) * cos_phase + jnp.sqrt(1.0 - cos_phase) * poly(cos_phase, VOL_POLY)
    ) * inv_sum - 0.25 * math.pi
    tan_s = sin_s * cos_v
    tan_v = sin_v * cos_s
    dist_sq = jnp.maximum(tan_s * tan_s + tan_v * tan_v - 2.0 * tan_s * tan_v * cos_a, 0.0)
    cross_sq = sin_sin * sin_sin * sin_a_sq
    cos_shadow = jnp.clip(2.0 * jnp.sqrt(dist_sq + cross_sq) * inv_sum, -1.0, 1.0)
    kgeo = sec_sec * (
        cos_sum * (shadow_term(cos_shadow) * (1.0 / math.pi) - 1.0) + 0.5 * (1.0 + cos_phase)
    )
    return kvol, kgeo


def ross_li_nadir(sun):
    sin_s, cos_s = sin_cos_sun(sun)
    cos_sum = cos_s + 1.0
    inv = 1.0 / (cos_s * cos_sum)
    sec_s = cos_sum * inv
    inv_sum = cos_s * inv
    kvol = ((0.5 * math.pi - sun) * cos_s + sin_s) * inv_sum - 0.25 * math.pi
    cos_shadow = jnp.clip(2.0 * sin_s * inv_sum, -1.0, 1.0)
    kgeo = sec_s * (
        cos_sum * (shadow_term(cos_shadow) * (1.0 / math.pi) - 1.0) + 0.5 * (1.0 + cos_s)
    )
    return kvol, kgeo


def ring_place():
    index = lax.axis_index("dates")
    core = lax.rem(index, 2)
    return lax.div(index, 2), core, 1 - 2 * core


def part_at(place, core, ring):
    return core * ring + lax.rem(place + 2 * ring, ring)


def sums_part(i, flip, ring):
    place, core, way = ring_place()
    if flip:
        core, way = 1 - core, -way
    by = jnp.where(i == 0, 0, jnp.where(i == 3, 2, way))
    return part_at(place + by, jnp.where(i == 2, 1 - core, core), ring)


def lanes_of(part):
    return pl.ds(pl.multiple_of(part * LANES, LANES), LANES)


def weight_of(f):
    weight = jnp.where(f == 1, 0.3, jnp.where(f == 2, 0.7, jnp.where(f == 3, 1.0, 0.0)))
    return weight.astype(jnp.float32)


def add_dates(sums, part, block, refl, flags, kernel_of):
    dates, bands, rows, _ = refl.shape
    lanes = lanes_of(block)
    for g in range(rows // SUB):
        r = slice(g * SUB, (g + 1) * SUB)
        acc = [None] * (6 + 3 * bands)

        def add(i, x):
            acc[i] = x if acc[i] is None else acc[i] + x

        for t in range(dates):
            kvol, kgeo = kernel_of(t, r)
            weight = weight_of(flags[t, r, lanes])
            wvol = weight * kvol
            wgeo = weight * kgeo
            for i, x in enumerate((weight, wvol, wgeo, wvol * kvol, wvol * kgeo, wgeo * kgeo)):
                add(i, x)
            for b in range(bands):
                x = refl[t, b, r, lanes]
                add(6 + b, weight * x)
                add(6 + bands + b, wvol * x)
                add(6 + 2 * bands + b, wgeo * x)
        for i, x in enumerate(acc):
            sums[part, i, r] = x


def other_kernel(*refs):
    sources, (sums, kernels), held, sems = refs[:5], refs[5:7], refs[7:12], refs[12]
    refl, sun, view, azim, flags = held
    dates, _, rows, _ = refl.shape
    ring = sums.shape[0]
    copies = [
        [pltpu.make_async_copy(sources[k].at[t], held[k].at[t], sems.at[k, t]) for t in range(dates)]
        for k in range(5)
    ]
    for t in range(dates):
        for k in range(1, 5):
            copies[k][t].start()
    for t in range(dates):
        copies[0][t].start()
    for t in range(dates):
        for k in range(1, 4):
            copies[k][t].wait()

        def angles(i, carry):
            block = sums_part(i, True, ring)
            lanes = lanes_of(block)
            for g in range(rows // SUB):
                r = slice(g * SUB, (g + 1) * SUB)
                kvol, kgeo = ross_li(sun[t, r, lanes], view[t, r, lanes], azim[t, r, lanes])
                kernels[block, t, 0, r] = kvol
                kernels[block, t, 1, r] = kgeo
            return carry

        lax.fori_loop(0, ring, angles, 0)
    for t in range(dates):
        copies[4][t].wait()
        copies[0][t].wait()

    def one(i, carry):
        block = sums_part(i, True, ring)
        add_dates(sums, i, block, refl, flags, lambda t, r: (kernels[block, t, 0, r], kernels[block, t, 1, r]))
        return carry

    lax.fori_loop(0, ring, one, 0)


def own_kernel(refl, sun, view, azim, flags, _, sums, kernels):
    ring = sums.shape[0]

    def one(i, carry):
        block = sums_part(i, False, ring)
        lanes = lanes_of(block)

        def kernel_of(t, r):
            kvol, kgeo = ross_li(sun[t, r, lanes], view[t, r, lanes], azim[t, r, lanes])
            kernels[block, t, 0, r] = kvol
            kernels[block, t, 1, r] = kgeo
            return kvol, kgeo

        add_dates(sums, i, block, refl, flags, kernel_of)
        return carry

    lax.fori_loop(0, ring, one, 0)


def sums_shapes(refl):
    dates, bands, rows, cols = refl.shape
    parts = cols // LANES
    return [
        jax.ShapeDtypeStruct((parts // 2, 6 + 3 * bands, rows, LANES), jnp.float32),
        jax.ShapeDtypeStruct((parts, dates, 2, rows, LANES), jnp.float32),
    ]


def other_sums(*inputs):
    held = [jax.ShapeDtypeStruct(x.shape, x.dtype) for x in inputs]
    return pl.pallas_call(
        other_kernel,
        in_specs=[pl.BlockSpec(memory_space=pltpu.HBM)] * 5,
        out_specs=[VMEM] * 7,
        out_shape=sums_shapes(inputs[0]) + held,
        scratch_shapes=[pltpu.SemaphoreType.DMA((5, inputs[0].shape[0]))],
        compiler_params=pltpu.CompilerParams(vmem_limit_bytes=16 << 20),
        name="other_sums",
    )(*(pltpu.with_memory_space_constraint(x, pltpu.HBM) for x in inputs))


def own_sums(inputs, kernels):
    return pl.pallas_call(
        own_kernel,
        in_specs=[VMEM] * 6,
        out_specs=[VMEM] * 2,
        out_shape=sums_shapes(inputs[0]),
        input_output_aliases={5: 1},
        compiler_params=pltpu.CompilerParams(vmem_limit_bytes=16 << 20),
        name="own_sums",
    )(*inputs, kernels)


def solve_kernel(own_a, own_b, near, far, smooth, above, below):
    planes, rows, _ = smooth.shape
    bands = planes // 3
    groups = rows // SUB
    for g in range(groups):
        r = slice(g * SUB, (g + 1) * SUB)

        def total(i):
            return (own_a[0, i, r] + own_b[0, i, r]) + (near[i, r] + far[i, r])

        n00 = total(0) + ridge_weight
        n01 = total(1)
        n02 = total(2)
        n11 = total(3) + ridge_weight
        n12 = total(4)
        n22 = total(5) + ridge_weight
        c00 = n11 * n22 - n12 * n12
        c01 = n02 * n12 - n01 * n22
        c02 = n01 * n12 - n02 * n11
        c11 = n00 * n22 - n02 * n02
        c12 = n01 * n02 - n00 * n12
        c22 = n00 * n11 - n01 * n01
        inv_det = 1.0 / (n00 * c00 + n01 * c01 + n02 * c02)
        for b in range(bands):
            x, y, z = total(6 + b), total(6 + bands + b), total(6 + 2 * bands + b)
            smooth[b, r] = (c00 * x + c01 * y + c02 * z) * inv_det
            smooth[bands + b, r] = (c01 * x + c11 * y + c12 * z) * inv_det
            smooth[2 * bands + b, r] = (c02 * x + c12 * y + c22 * z) * inv_det
    row = lax.broadcasted_iota(jnp.int32, (SUB, LANES), 0)
    first, last = row == 0, row == SUB - 1
    zero = jnp.zeros((SUB, LANES), jnp.float32)
    above[...] = jnp.zeros(above.shape, jnp.float32)
    below[...] = jnp.zeros(below.shape, jnp.float32)
    for p in range(planes):
        x = [smooth[p, g * SUB : (g + 1) * SUB] for g in range(groups)]
        below[0, p : p + 1] = x[0][:1] * 0.25
        above[0, p : p + 1] = x[-1][SUB - 1 :] * 0.25
        for g in range(groups):
            prior = jnp.where(last, x[g - 1] if g else zero, x[g])
            later = jnp.where(first, x[g + 1] if g < groups - 1 else zero, x[g])
            y = (pltpu.roll(prior, 1, 0) + 2.0 * x[g] + pltpu.roll(later, SUB - 1, 0)) * 0.25
            smooth[p, g * SUB : (g + 1) * SUB] = y


def solve(own_a, own_b, near, far, bands):
    rows = own_a.shape[2]
    shape = lambda *dims: jax.ShapeDtypeStruct(dims, jnp.float32)
    return pl.pallas_call(
        solve_kernel,
        in_specs=[VMEM] * 4,
        out_specs=[VMEM] * 3,
        out_shape=[shape(3 * bands, rows, LANES)] + [shape(1, rows, LANES)] * 2,
        compiler_params=pltpu.CompilerParams(vmem_limit_bytes=16 << 20),
        name="solve",
    )(own_a, own_b, near, far)


def correct_kernel(refl, kernels, nadir, above, below, *rest):
    (own, partner, near_a, far_a, end_a, near_b, far_b, end_b), (out, strip) = rest[:-2], rest[-2:]
    step = pl.program_id(0)
    parts = pl.num_programs(0)
    dates, bands, rows, _ = out.shape
    planes, ring = 3 * bands, parts // 2

    @pl.when(step == 0)
    def _():
        strip[0] = jnp.zeros(strip.shape[1:], jnp.float32)
        strip[parts + 1] = jnp.zeros(strip.shape[1:], jnp.float32)
        place, core, way = ring_place()
        halo = lambda ref, at: (ref.at[at], ref.at[at + 1])
        for by, flip, piece, (top, bottom) in (
            (0, 0, own, (above.at[0], below.at[0])),
            (0, 1, partner, halo(partner, planes)),
            (-way, 0, near_a, halo(far_a, planes + 2)),
            (-way, 1, far_a, halo(far_a, planes)),
            (-2 * way, 1, end_a, halo(end_a, planes)),
            (way, 1, near_b, halo(far_b, planes + 2)),
            (way, 0, far_b, halo(far_b, planes)),
            (2 * way, 0, end_b, halo(end_b, planes)),
        ):
            spot = part_at(place + by, 1 - core if flip else core, ring) + 1
            for p in range(planes):
                strip[spot, p] = piece[p]
                strip[spot, p, :1] += top[p : p + 1]
                strip[spot, p, rows - 1 :] += bottom[p : p + 1]

    lanes = lanes_of(step)
    lane = lax.broadcasted_iota(jnp.int32, (SUB, LANES), 1)
    first, last = lane == 0, lane == LANES - 1
    for g in range(rows // SUB):
        r = slice(g * SUB, (g + 1) * SUB)
        kvol_n, kgeo_n = ross_li_nadir(nadir[r, lanes])

        def smooth(p):
            x = strip[step + 1, p, r]
            prior = pltpu.roll(jnp.where(last, strip[step, p, r], x), 1, 1)
            later = pltpu.roll(jnp.where(first, strip[step + 2, p, r], x), LANES - 1, 1)
            return (prior + 2.0 * x + later) * 0.25

        for b in range(bands):
            iso, vol, geo = smooth(b), smooth(bands + b), smooth(2 * bands + b)
            model_n = iso + vol * kvol_n + geo * kgeo_n
            for t in range(dates):
                model = iso + vol * kernels[step, t, 0, r] + geo * kernels[step, t, 1, r]
                out[t, b, r] = refl[t, b, r, lanes] * model_n / jnp.maximum(model, model_floor)


def correct(refl, kernels, nadir, *pieces):
    dates, bands, rows, cols = refl.shape
    parts = cols // LANES
    return pl.pallas_call(
        correct_kernel,
        grid=(parts,),
        in_specs=[VMEM] * (3 + len(pieces)),
        out_specs=pl.BlockSpec((dates, bands, rows, LANES), lambda i: (0, 0, 0, i)),
        scratch_shapes=[pltpu.VMEM((parts + 2, 3 * bands, rows, LANES), jnp.float32)],
        out_shape=jax.ShapeDtypeStruct(refl.shape, jnp.float32),
        compiler_params=pltpu.CompilerParams(vmem_limit_bytes=24 << 20),
        name="correct",
    )(refl, kernels, nadir, *pieces)


def per_device(reflectance, sun_zenith, view_zenith, rel_azimuth, flags, nadir_sun):
    devices = lax.axis_size("dates")
    bands = reflectance.shape[1]

    def onward(x):
        pairs = [(i, (i + 2 - 4 * (i % 2)) % devices) for i in range(devices)]
        return lax.ppermute(x, "dates", pairs)

    def swap(x):
        return lax.ppermute(x, "dates", [(i, i ^ 1) for i in range(devices)])

    other, kernels, *held = other_sums(reflectance, sun_zenith, view_zenith, rel_azimuth, flags)
    other = swap(other)
    mine, kernels = own_sums(held, kernels)
    far = onward(mine[3] + other[3])
    near = onward(mine[2] + other[2])
    far = onward(mine[1] + other[1] + far)
    near = swap(near)
    own, above, below = solve(mine, other, near, far, bands)

    near = onward(own)
    blocks = lax.axis_size("rows")
    above = lax.ppermute(above, "rows", [(i, i + 1) for i in range(blocks - 1)])
    below = lax.ppermute(below, "rows", [(i + 1, i) for i in range(blocks - 1)])
    partner = swap(jnp.concatenate([own, above, below], 0))
    far = onward(jnp.concatenate([partner, above, below], 0))
    end = onward(far[: 3 * bands + 2])
    pieces = (own, partner, near, far, end)
    pieces += (swap(near), swap(far), swap(end))
    return correct(held[0], kernels, nadir_sun, above, below, *pieces)


def solution(mesh):
    in_specs = (
        P("dates", None, "rows", None),
        P("dates", "rows", None),
        P("dates", "rows", None),
        P("dates", "rows", None),
        P("dates", "rows", None),
        P("rows", None),
    )
    out_specs = P("dates", None, "rows", None)

    return jax.shard_map(
        per_device, mesh=mesh, in_specs=in_specs, out_specs=out_specs, check_vma=False
    )
```

profile of v0, /device:TPU:189, one launch (start us, length us, event | category | flops | bytes accessed | tf_op | source)
XLA Modules:
  0.0 97.0 jit_solution(17723446780962101950)
XLA Ops:
  0.0 3.6 %other_sums.1 = (f32[4,27,32,128]{3,2,1,0:T(8,128)S(1)}, f32[8,4,2,32,128]{4,3,2,1,0:T(8,128)S(1)}, f32[4,7,32,1024]{3,2,1,0:T(8,128)S(1)}, f32[4,32,1024]{2,1,0...) custom-call(f32[4,7,32,1024]{3,2,1,0:T(8,128)} %refs_0_.1, ...), custom_call_target="tpu_custom_call" | custom-call | tf_op jit(solution)/shard_map/other_sums/pallas_call | solution.py:217
  3.6 0.8 collective-permute-start
  4.4 1.7 %own_sums.1 = (f32[4,27,32,128]{3,2,1,0:T(8,128)S(1)}, f32[8,4,2,32,128]{4,3,2,1,0:T(8,128)S(1)}) custom-call(f32[4,7,32,1024]{3,2,1,0:T(8,128)S(1)} %get-tuple-element.17.refl, f32[4,32,1024]{2,1,0:T(8,128)S(1)} %get-tuple-element.18.sun, f32[4,32,1024]{2,1,0:T(8,128)S(1)} %get-tuple-element.19.view, ...), custom_call_target="tpu_custom_call", output_to_operand_aliasing={{1}: (5, {})} | custom-call | tf_op jit(solution)/shard_map/own_sums/pallas_call | solution.py:229
  6.1 1.6 %collective-permute-done.own_b = f32[4,27,32,128]{3,2,1,0:T(8,128)S(1)} collective-permute-done((f32[4,27,32,128]{3,2,1,0:T(8,128)S(1)}, f32[4,27,32,128]{3,2,1,0:T(8,128)S(1)}, u32[]{:S(2)}, u32[]{:S(2)}) %collective-permute-start) | collective-permute-done | bytes 1769504 | tf_op jit(solution)/shard_map/ppermute | solution.py:371
  7.7 0.2 fusion
  7.9 0.3 collective-permute-start.3
  8.2 0.1 collective-permute-start.1
  8.3 9.8 %collective-permute-done.3 = f32[27,32,128]{2,1,0:T(8,128)S(1)} collective-permute-done((f32[27,32,128]{2,1,0:T(8,128)S(1)}, f32[27,32,128]{2,1,0:T(8,128)S(1)}, u32[]{:S(2)}, u32[]{:S(2)}) %collective-permute-start.3) | collective-permute-done | bytes 442400 | tf_op jit(solution)/shard_map/ppermute | solution.py:368
  18.2 0.1 fusion.2
  18.3 1.4 %collective-permute-start.4 = (f32[27,32,128]{2,1,0:T(8,128)S(1)}, f32[27,32,128]{2,1,0:T(8,128)S(1)}, u32[]{:S(2)}, u32[]{:S(2)}) collective-permute-start(f32[27,32,128]{2,1,0:T(8,128)S(1)} %fusion.2), channel_id=1, source_target_pairs={{0,2},{1,7},{2,4},{3,1},{4,6},{5,3},{6,0},{7,5},{8,10},{9,15},{10,... | collective-permute-start | bytes 1327112 | tf_op jit(solution)/shard_map/ppermute | solution.py:368
  19.7 6.4 %collective-permute-done.1 = f32[27,32,128]{2,1,0:T(8,128)S(1)} collective-permute-done((f32[27,32,128]{2,1,0:T(8,128)S(1)}, f32[27,32,128]{2,1,0:T(8,128)S(1)}, u32[]{:S(2)}, u32[]{:S(2)}) %collective-permute-start.1) | collective-permute-done | bytes 442400 | tf_op jit(solution)/shard_map/ppermute | solution.py:368
  26.0 9.8 %collective-permute-start.2 = (f32[27,32,128]{2,1,0:T(8,128)S(1)}, f32[27,32,128]{2,1,0:T(8,128)S(1)}, u32[]{:S(2)}, u32[]{:S(2)}) collective-permute-start(f32[27,32,128]{2,1,0:T(8,128)S(1)} %collective-permute-done.1), channel_id=1, source_target_pairs={{0,1},{1,0},{2,3},{3,2},{4,5},{5,4},{6,7},{7,6},{8,9},{9,8},{10,11... | collective-permute-start | bytes 1327112 | tf_op jit(solution)/shard_map/ppermute | solution.py:371
  35.8 3.4 %collective-permute-done.4.far = f32[27,32,128]{2,1,0:T(8,128)S(1)} collective-permute-done((f32[27,32,128]{2,1,0:T(8,128)S(1)}, f32[27,32,128]{2,1,0:T(8,128)S(1)}, u32[]{:S(2)}, u32[]{:S(2)}) %collective-permute-start.4) | collective-permute-done | bytes 442400 | tf_op jit(solution)/shard_map/ppermute | solution.py:368
  39.2 0.0 collective-permute-done.2.near
  39.2 0.3 solve.1
  39.5 0.0 copy-start
  39.5 3.9 %collective-permute-start.5 = (f32[1,32,128]{2,1,0:T(8,128)S(1)}, f32[1,32,128]{2,1,0:T(8,128)S(1)}, u32[]{:S(2)}, u32[]{:S(2)}) collective-permute-start(f32[1,32,128]{2,1,0:T(8,128)S(1)} %get-tuple-element.26), channel_id=1, source_target_pairs={{0,8},{8,16},{16,24},{24,32},{32,40},{40,48},{48,56},{56,64},{64,7... | collective-permute-start | bytes 49160 | tf_op jit(solution)/shard_map/ppermute | solution.py:384
  43.4 1.9 %collective-permute-start.6 = (f32[1,32,128]{2,1,0:T(8,128)S(1)}, f32[1,32,128]{2,1,0:T(8,128)S(1)}, u32[]{:S(2)}, u32[]{:S(2)}) collective-permute-start(f32[1,32,128]{2,1,0:T(8,128)S(1)} %get-tuple-element.27), channel_id=1, source_target_pairs={{8,0},{16,8},{24,16},{32,24},{40,32},{48,40},{56,48},{64,56},{72,6... | collective-permute-start | bytes 49160 | tf_op jit(solution)/shard_map/ppermute | solution.py:385
  45.3 0.0 collective-permute-done.5.above
  45.3 5.6 %collective-permute-done.6.below = f32[1,32,128]{2,1,0:T(8,128)S(1)} collective-permute-done((f32[1,32,128]{2,1,0:T(8,128)S(1)}, f32[1,32,128]{2,1,0:T(8,128)S(1)}, u32[]{:S(2)}, u32[]{:S(2)}) %collective-permute-start.6) | collective-permute-done | bytes 16416 | tf_op jit(solution)/shard_map/ppermute | solution.py:385
  50.9 3.9 %collective-permute-start.7 = (f32[23,32,128]{2,1,0:T(8,128)S(1)}, f32[23,32,128]{2,1,0:T(8,128)S(1)}, u32[]{:S(2)}, u32[]{:S(2)}) collective-permute-start(f32[23,32,128]{2,1,0:T(8,128)S(1)} %pad_maximum_fusion.1), channel_id=1, source_target_pairs={{0,1},{1,0},{2,3},{3,2},{4,5},{5,4},{6,7},{7,6},{8,9},{9,8},{10,11... | collective-permute-start | bytes 1130504 | tf_op jit(solution)/shard_map/ppermute | solution.py:371
  54.8 1.3 %collective-permute-done.7.rest_1_ = f32[23,32,128]{2,1,0:T(8,128)S(1)} collective-permute-done((f32[23,32,128]{2,1,0:T(8,128)S(1)}, f32[23,32,128]{2,1,0:T(8,128)S(1)}, u32[]{:S(2)}, u32[]{:S(2)}) %collective-permute-start.7) | collective-permute-done | bytes 376864 | tf_op jit(solution)/shard_map/ppermute | solution.py:371
  56.1 0.1 collective-permute-start.9
  56.2 11.1 %collective-permute-done.9.rest_3_ = f32[25,32,128]{2,1,0:T(8,128)S(1)} collective-permute-done((f32[25,32,128]{2,1,0:T(8,128)S(1)}, f32[25,32,128]{2,1,0:T(8,128)S(1)}, u32[]{:S(2)}, u32[]{:S(2)}) %collective-permute-start.9) | collective-permute-done | bytes 409632 | tf_op jit(solution)/shard_map/ppermute | solution.py:368
  67.4 1.8 %collective-permute-start.10 = (f32[23,32,128]{2,1,0:T(8,128)S(1)}, f32[23,32,128]{2,1,0:T(8,128)S(1)}, u32[]{:S(2)}, u32[]{:S(2)}) collective-permute-start(f32[23,32,128]{2,1,0:T(8,128)S(1)} %slice.31), channel_id=1, source_target_pairs={{0,2},{1,7},{2,4},{3,1},{4,6},{5,3},{6,0},{7,5},{8,10},{9,15},{10,... | collective-permute-start | bytes 1130504 | tf_op jit(solution)/shard_map/ppermute | solution.py:368
  69.1 6.3 %collective-permute-start.8 = (f32[21,32,128]{2,1,0:T(8,128)S(1)}, f32[21,32,128]{2,1,0:T(8,128)S(1)}, u32[]{:S(2)}, u32[]{:S(2)}) collective-permute-start(f32[21,32,128]{2,1,0:T(8,128)S(1)} %get-tuple-element.28.rest_0_), channel_id=1, source_target_pairs={{0,2},{1,7},{2,4},{3,1},{4,6},{5,3},{6,0},{7,5},{8,10},{9,15},{10,... | collective-permute-start | bytes 1032200 | tf_op jit(solution)/shard_map/ppermute | solution.py:368
  75.5 0.0 collective-permute-start.12
  75.5 5.7 %collective-permute-done.10.rest_4_ = f32[23,32,128]{2,1,0:T(8,128)S(1)} collective-permute-done((f32[23,32,128]{2,1,0:T(8,128)S(1)}, f32[23,32,128]{2,1,0:T(8,128)S(1)}, u32[]{:S(2)}, u32[]{:S(2)}) %collective-permute-start.10) | collective-permute-done | bytes 376864 | tf_op jit(solution)/shard_map/ppermute | solution.py:368
  81.2 2.6 %collective-permute-start.13 = (f32[23,32,128]{2,1,0:T(8,128)S(1)}, f32[23,32,128]{2,1,0:T(8,128)S(1)}, u32[]{:S(2)}, u32[]{:S(2)}) collective-permute-start(f32[23,32,128]{2,1,0:T(8,128)S(1)} %collective-permute-done.10.rest_4_), channel_id=1, source_target_pairs={{0,1},{1,0},{2,3},{3,2},{4,5},{5,4},{6,7},{7,6},{8,9},{9,8},{10,11... | collective-permute-start | bytes 1130504 | tf_op jit(solution)/shard_map/ppermute | solution.py:371
  83.8 1.1 %collective-permute-done.8.rest_2_ = f32[21,32,128]{2,1,0:T(8,128)S(1)} collective-permute-done((f32[21,32,128]{2,1,0:T(8,128)S(1)}, f32[21,32,128]{2,1,0:T(8,128)S(1)}, u32[]{:S(2)}, u32[]{:S(2)}) %collective-permute-start.8) | collective-permute-done | bytes 344096 | tf_op jit(solution)/shard_map/ppermute | solution.py:368
  84.9 5.7 %collective-permute-start.11 = (f32[21,32,128]{2,1,0:T(8,128)S(1)}, f32[21,32,128]{2,1,0:T(8,128)S(1)}, u32[]{:S(2)}, u32[]{:S(2)}) collective-permute-start(f32[21,32,128]{2,1,0:T(8,128)S(1)} %collective-permute-done.8.rest_2_), channel_id=1, source_target_pairs={{0,1},{1,0},{2,3},{3,2},{4,5},{5,4},{6,7},{7,6},{8,9},{9,8},{10,11... | collective-permute-start | bytes 1032200 | tf_op jit(solution)/shard_map/ppermute | solution.py:371
  90.6 1.3 %collective-permute-done.11.rest_5_ = f32[21,32,128]{2,1,0:T(8,128)S(1)} collective-permute-done((f32[21,32,128]{2,1,0:T(8,128)S(1)}, f32[21,32,128]{2,1,0:T(8,128)S(1)}, u32[]{:S(2)}, u32[]{:S(2)}) %collective-permute-start.11) | collective-permute-done | bytes 344096 | tf_op jit(solution)/shard_map/ppermute | solution.py:371
  91.8 0.0 collective-permute-done.12.rest_6_
  91.9 0.0 collective-permute-done.13.rest_7_
  91.9 0.0 copy-done
  91.9 5.2 %correct.1 = f32[4,7,32,1024]{3,2,1,0:T(8,128)} custom-call(f32[4,7,32,1024]{3,2,1,0:T(8,128)S(1)} %get-tuple-element.17.refl, f32[8,4,2,32,128]{4,3,2,1,0:T(8,128)S(1)} %get-tuple-element.23.kernels, f32[32,1024]{1,0:T(8,128)S(1)} %copy-done, f32[1,32,128]{2,1,0:T(8,128)S(1)} %collective-permute-done.5.above, ...), custom_call_target="tpu_custom_call" | custom-call | tf_op jit(solution)/shard_map/correct/pallas_call | solution.py:350
  (3 shorter events, 0.1 us)
Async XLA Ops:
  3.6 4.1 %collective-permute-start = (f32[4,27,32,128]{3,2,1,0:T(8,128)S(1)}, f32[4,27,32,128]{3,2,1,0:T(8,128)S(1)}, u32[]{:S(2)}, u32[]{:S(2)}) collective-permute-start(f32[4,27,32,128]{3,2,1,0:T(8,128)S(1)} %get-tuple-element.25), channel_id=1, source_target_pairs={{0,1},{1,0},{2,3},{3,2},{4,5},{5,4},{6,7},{7,6},{8,9},{9,8},{10,11... | collective-permute-start | bytes 5308424 | tf_op jit(solution)/shard_map/ppermute | solution.py:371
  7.9 10.3 %collective-permute-start.3 = (f32[27,32,128]{2,1,0:T(8,128)S(1)}, f32[27,32,128]{2,1,0:T(8,128)S(1)}, u32[]{:S(2)}, u32[]{:S(2)}) collective-permute-start(f32[27,32,128]{2,1,0:T(8,128)S(1)} %get-tuple-element.29), channel_id=1, source_target_pairs={{0,2},{1,7},{2,4},{3,1},{4,6},{5,3},{6,0},{7,5},{8,10},{9,15},{10,... | collective-permute-start | bytes 1327112 | tf_op jit(solution)/shard_map/ppermute | solution.py:368
  8.2 17.8 %collective-permute-start.1 = (f32[27,32,128]{2,1,0:T(8,128)S(1)}, f32[27,32,128]{2,1,0:T(8,128)S(1)}, u32[]{:S(2)}, u32[]{:S(2)}) collective-permute-start(f32[27,32,128]{2,1,0:T(8,128)S(1)} %get-tuple-element.30), channel_id=1, source_target_pairs={{0,2},{1,7},{2,4},{3,1},{4,6},{5,3},{6,0},{7,5},{8,10},{9,15},{10,... | collective-permute-start | bytes 1327112 | tf_op jit(solution)/shard_map/ppermute | solution.py:368
  18.3 20.9 %collective-permute-start.4 = (f32[27,32,128]{2,1,0:T(8,128)S(1)}, f32[27,32,128]{2,1,0:T(8,128)S(1)}, u32[]{:S(2)}, u32[]{:S(2)}) collective-permute-start(f32[27,32,128]{2,1,0:T(8,128)S(1)} %fusion.2), channel_id=1, source_target_pairs={{0,2},{1,7},{2,4},{3,1},{4,6},{5,3},{6,0},{7,5},{8,10},{9,15},{10,... | collective-permute-start | bytes 1327112 | tf_op jit(solution)/shard_map/ppermute | solution.py:368
  26.0 13.2 %collective-permute-start.2 = (f32[27,32,128]{2,1,0:T(8,128)S(1)}, f32[27,32,128]{2,1,0:T(8,128)S(1)}, u32[]{:S(2)}, u32[]{:S(2)}) collective-permute-start(f32[27,32,128]{2,1,0:T(8,128)S(1)} %collective-permute-done.1), channel_id=1, source_target_pairs={{0,1},{1,0},{2,3},{3,2},{4,5},{5,4},{6,7},{7,6},{8,9},{9,8},{10,11... | collective-permute-start | bytes 1327112 | tf_op jit(solution)/shard_map/ppermute | solution.py:371
  39.5 52.4 %copy-start = (f32[32,1024]{1,0:T(8,128)S(1)}, f32[32,1024]{1,0:T(8,128)}, u32[]{:S(2)}) copy-start(f32[32,1024]{1,0:T(8,128)} %nadir.1) | copy-start | bytes 393220
  39.5 5.8 %collective-permute-start.5 = (f32[1,32,128]{2,1,0:T(8,128)S(1)}, f32[1,32,128]{2,1,0:T(8,128)S(1)}, u32[]{:S(2)}, u32[]{:S(2)}) collective-permute-start(f32[1,32,128]{2,1,0:T(8,128)S(1)} %get-tuple-element.26), channel_id=1, source_target_pairs={{0,8},{8,16},{16,24},{24,32},{32,40},{40,48},{48,56},{56,64},{64,7... | collective-permute-start | bytes 49160 | tf_op jit(solution)/shard_map/ppermute | solution.py:384
  43.4 7.5 %collective-permute-start.6 = (f32[1,32,128]{2,1,0:T(8,128)S(1)}, f32[1,32,128]{2,1,0:T(8,128)S(1)}, u32[]{:S(2)}, u32[]{:S(2)}) collective-permute-start(f32[1,32,128]{2,1,0:T(8,128)S(1)} %get-tuple-element.27), channel_id=1, source_target_pairs={{8,0},{16,8},{24,16},{32,24},{40,32},{48,40},{56,48},{64,56},{72,6... | collective-permute-start | bytes 49160 | tf_op jit(solution)/shard_map/ppermute | solution.py:385
  50.9 5.2 %collective-permute-start.7 = (f32[23,32,128]{2,1,0:T(8,128)S(1)}, f32[23,32,128]{2,1,0:T(8,128)S(1)}, u32[]{:S(2)}, u32[]{:S(2)}) collective-permute-start(f32[23,32,128]{2,1,0:T(8,128)S(1)} %pad_maximum_fusion.1), channel_id=1, source_target_pairs={{0,1},{1,0},{2,3},{3,2},{4,5},{5,4},{6,7},{7,6},{8,9},{9,8},{10,11... | collective-permute-start | bytes 1130504 | tf_op jit(solution)/shard_map/ppermute | solution.py:371
  56.1 11.2 %collective-permute-start.9 = (f32[25,32,128]{2,1,0:T(8,128)S(1)}, f32[25,32,128]{2,1,0:T(8,128)S(1)}, u32[]{:S(2)}, u32[]{:S(2)}) collective-permute-start(f32[25,32,128]{2,1,0:T(8,128)S(1)} %pad_maximum_fusion), channel_id=1, source_target_pairs={{0,2},{1,7},{2,4},{3,1},{4,6},{5,3},{6,0},{7,5},{8,10},{9,15},{10,... | collective-permute-start | bytes 1228808 | tf_op jit(solution)/shard_map/ppermute | solution.py:368
  67.4 13.8 %collective-permute-start.10 = (f32[23,32,128]{2,1,0:T(8,128)S(1)}, f32[23,32,128]{2,1,0:T(8,128)S(1)}, u32[]{:S(2)}, u32[]{:S(2)}) collective-permute-start(f32[23,32,128]{2,1,0:T(8,128)S(1)} %slice.31), channel_id=1, source_target_pairs={{0,2},{1,7},{2,4},{3,1},{4,6},{5,3},{6,0},{7,5},{8,10},{9,15},{10,... | collective-permute-start | bytes 1130504 | tf_op jit(solution)/shard_map/ppermute | solution.py:368
  69.1 15.7 %collective-permute-start.8 = (f32[21,32,128]{2,1,0:T(8,128)S(1)}, f32[21,32,128]{2,1,0:T(8,128)S(1)}, u32[]{:S(2)}, u32[]{:S(2)}) collective-permute-start(f32[21,32,128]{2,1,0:T(8,128)S(1)} %get-tuple-element.28.rest_0_), channel_id=1, source_target_pairs={{0,2},{1,7},{2,4},{3,1},{4,6},{5,3},{6,0},{7,5},{8,10},{9,15},{10,... | collective-permute-start | bytes 1032200 | tf_op jit(solution)/shard_map/ppermute | solution.py:368
  75.5 16.4 %collective-permute-start.12 = (f32[25,32,128]{2,1,0:T(8,128)S(1)}, f32[25,32,128]{2,1,0:T(8,128)S(1)}, u32[]{:S(2)}, u32[]{:S(2)}) collective-permute-start(f32[25,32,128]{2,1,0:T(8,128)S(1)} %collective-permute-done.9.rest_3_), channel_id=1, source_target_pairs={{0,1},{1,0},{2,3},{3,2},{4,5},{5,4},{6,7},{7,6},{8,9},{9,8},{10,11... | collective-permute-start | bytes 1228808 | tf_op jit(solution)/shard_map/ppermute | solution.py:371
  81.2 10.6 %collective-permute-start.13 = (f32[23,32,128]{2,1,0:T(8,128)S(1)}, f32[23,32,128]{2,1,0:T(8,128)S(1)}, u32[]{:S(2)}, u32[]{:S(2)}) collective-permute-start(f32[23,32,128]{2,1,0:T(8,128)S(1)} %collective-permute-done.10.rest_4_), channel_id=1, source_target_pairs={{0,1},{1,0},{2,3},{3,2},{4,5},{5,4},{6,7},{7,6},{8,9},{9,8},{10,11... | collective-permute-start | bytes 1130504 | tf_op jit(solution)/shard_map/ppermute | solution.py:371
  84.9 7.0 %collective-permute-start.11 = (f32[21,32,128]{2,1,0:T(8,128)S(1)}, f32[21,32,128]{2,1,0:T(8,128)S(1)}, u32[]{:S(2)}, u32[]{:S(2)}) collective-permute-start(f32[21,32,128]{2,1,0:T(8,128)S(1)} %collective-permute-done.8.rest_2_), channel_id=1, source_target_pairs={{0,1},{1,0},{2,3},{3,2},{4,5},{5,4},{6,7},{7,6},{8,9},{9,8},{10,11... | collective-permute-start | bytes 1032200 | tf_op jit(solution)/shard_map/ppermute | solution.py:371
where the time goes:
time: 97.1 us; the launch traced here: 97 us
  waiting for transfers between devices  47.3 us (49%)
  starting transfers between devices  38.5 us (40%)
  Pallas kernels  10.8 us (11%)
    ppermute x6, waiting for transfers between devices, onward(): return lax.ppermute(x, 'dates', pairs)  37.5 us
    ppermute x6, starting transfers between devices, swap(): return lax.ppermute(x, 'dates', [(i, i ^ 1) for i in range(devices)])  22.7 us
    ppermute x6, starting transfers between devices, onward(): return lax.ppermute(x, 'dates', pairs)  10 us
    ppermute x1, waiting for transfers between devices, per_device(): below = lax.ppermute(below, 'rows', [(i + 1, i) for i in range(blocks - 1)])  5.55 us
    pallas_call x1, Pallas kernels, correct(): pl.pallas_call(correct_kernel, grid=(parts,), in_specs=[VMEM] * (3 + len(...  5.16 us
    ppermute x6, waiting for transfers between devices, swap(): return lax.ppermute(x, 'dates', [(i, i ^ 1) for i in range(devices)])  4.2 us
    ppermute x1, starting transfers between devices, per_device(): above = lax.ppermute(above, 'rows', [(i, i + 1) for i in range(blocks - 1)])  3.87 us
    pallas_call x1, Pallas kernels, other_sums(): pl.pallas_call(other_kernel, in_specs=[pl.BlockSpec(memory_space=pltpu.HB...  3.62 us
  transfers between devices with their start and end apart: 14, of which 10 were waited for; matrix products, arithmetic and copies ran while one was open for 0% of the time, Pallas kernels for 2%

commit v1 on v0

--- a/solution.py
+++ b/solution.py
@@ -294,8 +294,8 @@
     )(own_a, own_b, near, far)
 
 
-def correct_kernel(refl, kernels, nadir, above, below, *rest):
-    (own, partner, near_a, far_a, end_a, near_b, far_b, end_b), (out, strip) = rest[:-2], rest[-2:]
+def correct_kernel(refl, kernels, nadir, *rest):
+    (halos, pieces), (out, strip) = (rest[:5], rest[5:-2]), rest[-2:]
     step = pl.program_id(0)
     parts = pl.num_programs(0)
     dates, bands, rows, _ = out.shape
@@ -306,22 +306,23 @@
         strip[0] = jnp.zeros(strip.shape[1:], jnp.float32)
         strip[parts + 1] = jnp.zeros(strip.shape[1:], jnp.float32)
         place, core, way = ring_place()
-        halo = lambda ref, at: (ref.at[at], ref.at[at + 1])
-        for by, flip, piece, (top, bottom) in (
-            (0, 0, own, (above.at[0], below.at[0])),
-            (0, 1, partner, halo(partner, planes)),
-            (-way, 0, near_a, halo(far_a, planes + 2)),
-            (-way, 1, far_a, halo(far_a, planes)),
-            (-2 * way, 1, end_a, halo(end_a, planes)),
-            (way, 1, near_b, halo(far_b, planes + 2)),
-            (way, 0, far_b, halo(far_b, planes)),
-            (2 * way, 0, end_b, halo(end_b, planes)),
+        own, partner, behind, ahead, beyond = halos
+        for (by, flip), piece, (halo, at) in zip(
+            (
+                (0, 0), (-way, 0), (-way, 1), (-2 * way, 0),
+                (0, 1), (way, 1), (way, 0), (2 * way, 1),
+            ),
+            pieces,
+            (
+                (own, 0), (behind, 0), (behind, 2), (beyond, 0),
+                (partner, 0), (ahead, 0), (ahead, 2), (beyond, 2),
+            ),
         ):
             spot = part_at(place + by, 1 - core if flip else core, ring) + 1
             for p in range(planes):
                 strip[spot, p] = piece[p]
-                strip[spot, p, :1] += top[p : p + 1]
-                strip[spot, p, rows - 1 :] += bottom[p : p + 1]
+                strip[spot, p, :1] += halo[at, p : p + 1]
+                strip[spot, p, rows - 1 :] += halo[at + 1, p : p + 1]
 
     lanes = lanes_of(step)
     lane = lax.broadcasted_iota(jnp.int32, (SUB, LANES), 1)
@@ -344,19 +345,19 @@
                 out[t, b, r] = refl[t, b, r, lanes] * model_n / jnp.maximum(model, model_floor)
 
 
-def correct(refl, kernels, nadir, *pieces):
+def correct(refl, kernels, nadir, halos, pieces):
     dates, bands, rows, cols = refl.shape
     parts = cols // LANES
     return pl.pallas_call(
         correct_kernel,
         grid=(parts,),
-        in_specs=[VMEM] * (3 + len(pieces)),
+        in_specs=[VMEM] * (3 + len(halos) + len(pieces)),
         out_specs=pl.BlockSpec((dates, bands, rows, LANES), lambda i: (0, 0, 0, i)),
         scratch_shapes=[pltpu.VMEM((parts + 2, 3 * bands, rows, LANES), jnp.float32)],
         out_shape=jax.ShapeDtypeStruct(refl.shape, jnp.float32),
         compiler_params=pltpu.CompilerParams(vmem_limit_bytes=24 << 20),
         name="correct",
-    )(refl, kernels, nadir, *pieces)
+    )(refl, kernels, nadir, *halos, *pieces)
 
 
 def per_device(reflectance, sun_zenith, view_zenith, rel_azimuth, flags, nadir_sun):
@@ -379,16 +380,25 @@
     near = swap(near)
     own, above, below = solve(mine, other, near, far, bands)
 
-    near = onward(own)
+    behind = onward(own)
+    partner = swap(own)
+    behind_partner = onward(partner)
+    relayed = onward(behind)
+    pieces = (own, behind, behind_partner, relayed, partner)
+    pieces += (swap(behind), swap(behind_partner), swap(relayed))
+
     blocks = lax.axis_size("rows")
     above = lax.ppermute(above, "rows", [(i, i + 1) for i in range(blocks - 1)])
     below = lax.ppermute(below, "rows", [(i + 1, i) for i in range(blocks - 1)])
-    partner = swap(jnp.concatenate([own, above, below], 0))
-    far = onward(jnp.concatenate([partner, above, below], 0))
-    end = onward(far[: 3 * bands + 2])
-    pieces = (own, partner, near, far, end)
-    pieces += (swap(near), swap(far), swap(end))
-    return correct(held[0], kernels, nadir_sun, above, below, *pieces)
+    halo = jnp.concatenate([above, below], 0)
+    halo_partner = swap(halo)
+    halo_both = jnp.concatenate([halo, halo_partner], 0)
+    halo_behind = onward(halo_both)
+    halo_far = lax.ppermute(
+        halo_both, "dates", [(i, (i + devices // 2) % devices) for i in range(devices)]
+    )
+    halos = (halo, halo_partner, halo_behind, swap(halo_behind), halo_far)
+    return correct(held[0], kernels, nadir_sun, halos, pieces)
 
 
 def solution(mesh):

time: 97.1 us -> 92.9 us (0.957)
  the two profiles are of different devices: /device:TPU:189 before, /device:TPU:6 now
where the time goes in v1:
time: 92.9 us; the launch traced here: 92.8 us
  starting transfers between devices  51 us (55%)
  waiting for transfers between devices  30.6 us (33%)
  Pallas kernels  10.8 us (12%)
    ppermute x7, waiting for transfers between devices, onward(): return lax.ppermute(x, 'dates', pairs)  20.7 us
    ppermute x7, starting transfers between devices, onward(): return lax.ppermute(x, 'dates', pairs)  19.9 us
    ppermute x8, starting transfers between devices, swap(): return lax.ppermute(x, 'dates', [(i, i ^ 1) for i in range(devices)])  19.9 us
    ppermute x1, starting transfers between devices, per_device(): below = lax.ppermute(below, 'rows', [(i + 1, i) for i in range(blocks - 1)])  5.37 us
    pallas_call x1, Pallas kernels, correct(): pl.pallas_call(correct_kernel, grid=(parts,), in_specs=[VMEM] * (3 + len(...  5.16 us
    ppermute x8, waiting for transfers between devices, swap(): return lax.ppermute(x, 'dates', [(i, i ^ 1) for i in range(devices)])  4.92 us
    ppermute x1, waiting for transfers between devices, per_device(): lax.ppermute(halo_both, 'dates', [(i, (i + devices // 2) % devices) for i...  4.45 us
    pallas_call x1, Pallas kernels, other_sums(): pl.pallas_call(other_kernel, in_specs=[pl.BlockSpec(memory_space=pltpu.HB...  3.63 us
  transfers between devices with their start and end apart: 18, of which 9 were waited for; matrix products, arithmetic and copies ran while one was open for 0% of the time, Pallas kernels for 2%

profile of v1, /device:TPU:6, one launch (start us, length us, event | category | flops | bytes accessed | tf_op | source)
XLA Modules:
  0.0 92.8 jit_solution(14649482562577822311)
XLA Ops:
  0.0 3.6 %other_sums.1 = (f32[4,27,32,128]{3,2,1,0:T(8,128)S(1)}, f32[8,4,2,32,128]{4,3,2,1,0:T(8,128)S(1)}, f32[4,7,32,1024]{3,2,1,0:T(8,128)S(1)}, f32[4,32,1024]{2,1,0...) custom-call(f32[4,7,32,1024]{3,2,1,0:T(8,128)} %refs_0_.1, ...), custom_call_target="tpu_custom_call" | custom-call | tf_op jit(solution)/shard_map/other_sums/pallas_call | solution.py:217
  3.6 0.1 collective-permute-start
  3.7 1.7 %own_sums.1 = (f32[4,27,32,128]{3,2,1,0:T(8,128)S(1)}, f32[8,4,2,32,128]{4,3,2,1,0:T(8,128)S(1)}) custom-call(f32[4,7,32,1024]{3,2,1,0:T(8,128)S(1)} %get-tuple-element.17.refl, f32[4,32,1024]{2,1,0:T(8,128)S(1)} %get-tuple-element.18.sun, f32[4,32,1024]{2,1,0:T(8,128)S(1)} %get-tuple-element.19.view, ...), custom_call_target="tpu_custom_call", output_to_operand_aliasing={{1}: (5, {})} | custom-call | tf_op jit(solution)/shard_map/own_sums/pallas_call | solution.py:229
  5.5 1.9 %collective-permute-done.own_b = f32[4,27,32,128]{3,2,1,0:T(8,128)S(1)} collective-permute-done((f32[4,27,32,128]{3,2,1,0:T(8,128)S(1)}, f32[4,27,32,128]{3,2,1,0:T(8,128)S(1)}, u32[]{:S(2)}, u32[]{:S(2)}) %collective-permute-start) | collective-permute-done | bytes 1769504 | tf_op jit(solution)/shard_map/ppermute | solution.py:372
  7.4 0.2 fusion
  7.6 3.3 %collective-permute-start.3 = (f32[27,32,128]{2,1,0:T(8,128)S(1)}, f32[27,32,128]{2,1,0:T(8,128)S(1)}, u32[]{:S(2)}, u32[]{:S(2)}) collective-permute-start(f32[27,32,128]{2,1,0:T(8,128)S(1)} %get-tuple-element.29), channel_id=1, source_target_pairs={{0,2},{1,7},{2,4},{3,1},{4,6},{5,3},{6,0},{7,5},{8,10},{9,15},{10,... | collective-permute-start | bytes 1327112 | tf_op jit(solution)/shard_map/ppermute | solution.py:369
  10.9 4.5 %collective-permute-start.1 = (f32[27,32,128]{2,1,0:T(8,128)S(1)}, f32[27,32,128]{2,1,0:T(8,128)S(1)}, u32[]{:S(2)}, u32[]{:S(2)}) collective-permute-start(f32[27,32,128]{2,1,0:T(8,128)S(1)} %get-tuple-element.30), channel_id=1, source_target_pairs={{0,2},{1,7},{2,4},{3,1},{4,6},{5,3},{6,0},{7,5},{8,10},{9,15},{10,... | collective-permute-start | bytes 1327112 | tf_op jit(solution)/shard_map/ppermute | solution.py:369
  15.4 6.4 %collective-permute-done.3 = f32[27,32,128]{2,1,0:T(8,128)S(1)} collective-permute-done((f32[27,32,128]{2,1,0:T(8,128)S(1)}, f32[27,32,128]{2,1,0:T(8,128)S(1)}, u32[]{:S(2)}, u32[]{:S(2)}) %collective-permute-start.3) | collective-permute-done | bytes 442400 | tf_op jit(solution)/shard_map/ppermute | solution.py:369
  21.8 0.1 fusion.2
  21.9 0.0 copy-start
  21.9 1.6 %collective-permute-start.4 = (f32[27,32,128]{2,1,0:T(8,128)S(1)}, f32[27,32,128]{2,1,0:T(8,128)S(1)}, u32[]{:S(2)}, u32[]{:S(2)}) collective-permute-start(f32[27,32,128]{2,1,0:T(8,128)S(1)} %fusion.2), channel_id=1, source_target_pairs={{0,2},{1,7},{2,4},{3,1},{4,6},{5,3},{6,0},{7,5},{8,10},{9,15},{10,... | collective-permute-start | bytes 1327112 | tf_op jit(solution)/shard_map/ppermute | solution.py:369
  23.5 4.9 %collective-permute-done.1 = f32[27,32,128]{2,1,0:T(8,128)S(1)} collective-permute-done((f32[27,32,128]{2,1,0:T(8,128)S(1)}, f32[27,32,128]{2,1,0:T(8,128)S(1)}, u32[]{:S(2)}, u32[]{:S(2)}) %collective-permute-start.1) | collective-permute-done | bytes 442400 | tf_op jit(solution)/shard_map/ppermute | solution.py:369
  28.4 7.4 %collective-permute-start.2 = (f32[27,32,128]{2,1,0:T(8,128)S(1)}, f32[27,32,128]{2,1,0:T(8,128)S(1)}, u32[]{:S(2)}, u32[]{:S(2)}) collective-permute-start(f32[27,32,128]{2,1,0:T(8,128)S(1)} %collective-permute-done.1), channel_id=1, source_target_pairs={{0,1},{1,0},{2,3},{3,2},{4,5},{5,4},{6,7},{7,6},{8,9},{9,8},{10,11... | collective-permute-start | bytes 1327112 | tf_op jit(solution)/shard_map/ppermute | solution.py:372
  35.8 0.0 collective-permute-done.4.far
  35.8 1.4 %collective-permute-done.2.near = f32[27,32,128]{2,1,0:T(8,128)S(1)} collective-permute-done((f32[27,32,128]{2,1,0:T(8,128)S(1)}, f32[27,32,128]{2,1,0:T(8,128)S(1)}, u32[]{:S(2)}, u32[]{:S(2)}) %collective-permute-start.2) | collective-permute-done | bytes 442400 | tf_op jit(solution)/shard_map/ppermute | solution.py:372
  37.2 0.3 solve.1
  37.5 5.6 %collective-permute-start.12 = (f32[21,32,128]{2,1,0:T(8,128)S(1)}, f32[21,32,128]{2,1,0:T(8,128)S(1)}, u32[]{:S(2)}, u32[]{:S(2)}) collective-permute-start(f32[21,32,128]{2,1,0:T(8,128)S(1)} %get-tuple-element.28.rest_5_), channel_id=1, source_target_pairs={{0,1},{1,0},{2,3},{3,2},{4,5},{5,4},{6,7},{7,6},{8,9},{9,8},{10,11... | collective-permute-start | bytes 1032200 | tf_op jit(solution)/shard_map/ppermute | solution.py:372
  43.2 2.2 %collective-permute-start.11 = (f32[21,32,128]{2,1,0:T(8,128)S(1)}, f32[21,32,128]{2,1,0:T(8,128)S(1)}, u32[]{:S(2)}, u32[]{:S(2)}) collective-permute-start(f32[21,32,128]{2,1,0:T(8,128)S(1)} %get-tuple-element.28.rest_5_), channel_id=1, source_target_pairs={{0,2},{1,7},{2,4},{3,1},{4,6},{5,3},{6,0},{7,5},{8,10},{9,15},{10,... | collective-permute-start | bytes 1032200 | tf_op jit(solution)/shard_map/ppermute | solution.py:369
  45.3 0.0 collective-permute-done.12.rest_9_
  45.3 4.6 %collective-permute-start.13 = (f32[21,32,128]{2,1,0:T(8,128)S(1)}, f32[21,32,128]{2,1,0:T(8,128)S(1)}, u32[]{:S(2)}, u32[]{:S(2)}) collective-permute-start(f32[21,32,128]{2,1,0:T(8,128)S(1)} %collective-permute-done.12.rest_9_), channel_id=1, source_target_pairs={{0,2},{1,7},{2,4},{3,1},{4,6},{5,3},{6,0},{7,5},{8,10},{9,15},{10,... | collective-permute-start | bytes 1032200 | tf_op jit(solution)/shard_map/ppermute | solution.py:369
  49.9 7.0 %collective-permute-done.11.rest_6_ = f32[21,32,128]{2,1,0:T(8,128)S(1)} collective-permute-done((f32[21,32,128]{2,1,0:T(8,128)S(1)}, f32[21,32,128]{2,1,0:T(8,128)S(1)}, u32[]{:S(2)}, u32[]{:S(2)}) %collective-permute-start.11) | collective-permute-done | bytes 344096 | tf_op jit(solution)/shard_map/ppermute | solution.py:369
  56.9 2.1 %collective-permute-start.14 = (f32[21,32,128]{2,1,0:T(8,128)S(1)}, f32[21,32,128]{2,1,0:T(8,128)S(1)}, u32[]{:S(2)}, u32[]{:S(2)}) collective-permute-start(f32[21,32,128]{2,1,0:T(8,128)S(1)} %collective-permute-done.11.rest_6_), channel_id=1, source_target_pairs={{0,2},{1,7},{2,4},{3,1},{4,6},{5,3},{6,0},{7,5},{8,10},{9,15},{10,... | collective-permute-start | bytes 1032200 | tf_op jit(solution)/shard_map/ppermute | solution.py:369
  59.0 3.5 %collective-permute-start.5 = (f32[1,32,128]{2,1,0:T(8,128)S(1)}, f32[1,32,128]{2,1,0:T(8,128)S(1)}, u32[]{:S(2)}, u32[]{:S(2)}) collective-permute-start(f32[1,32,128]{2,1,0:T(8,128)S(1)} %get-tuple-element.26), channel_id=1, source_target_pairs={{0,8},{8,16},{16,24},{24,32},{32,40},{40,48},{48,56},{56,64},{64,7... | collective-permute-start | bytes 49160 | tf_op jit(solution)/shard_map/ppermute | solution.py:391
  62.5 5.4 %collective-permute-start.6 = (f32[1,32,128]{2,1,0:T(8,128)S(1)}, f32[1,32,128]{2,1,0:T(8,128)S(1)}, u32[]{:S(2)}, u32[]{:S(2)}) collective-permute-start(f32[1,32,128]{2,1,0:T(8,128)S(1)} %get-tuple-element.27), channel_id=1, source_target_pairs={{8,0},{16,8},{24,16},{32,24},{40,32},{48,40},{56,48},{64,56},{72,6... | collective-permute-start | bytes 49160 | tf_op jit(solution)/shard_map/ppermute | solution.py:392
  67.9 0.5 collective-permute-done.5
  68.3 6.1 %collective-permute-start.15 = (f32[21,32,128]{2,1,0:T(8,128)S(1)}, f32[21,32,128]{2,1,0:T(8,128)S(1)}, u32[]{:S(2)}, u32[]{:S(2)}) collective-permute-start(f32[21,32,128]{2,1,0:T(8,128)S(1)} %collective-permute-done.11.rest_6_), channel_id=1, source_target_pairs={{0,1},{1,0},{2,3},{3,2},{4,5},{5,4},{6,7},{7,6},{8,9},{9,8},{10,11... | collective-permute-start | bytes 1032200 | tf_op jit(solution)/shard_map/ppermute | solution.py:372
  74.4 0.0 collective-permute-done.13.rest_7_
  74.4 0.1 collective-permute-start.16
  74.5 0.0 collective-permute-done.14.rest_8_
  74.5 0.4 collective-permute-start.17
  74.9 0.0 collective-permute-done.6
  74.9 0.2 collective-permute-start.7
  75.2 1.6 %collective-permute-done.7.rest_1_ = f32[2,32,128]{2,1,0:T(8,128)S(1)} collective-permute-done((f32[2,32,128]{2,1,0:T(8,128)S(1)}, f32[2,32,128]{2,1,0:T(8,128)S(1)}, u32[]{:S(2)}, u32[]{:S(2)}) %collective-permute-start.7) | collective-permute-done | bytes 32800 | tf_op jit(solution)/shard_map/ppermute | solution.py:372
  76.7 1.7 %collective-permute-start.8 = (f32[4,32,128]{2,1,0:T(8,128)S(1)}, f32[4,32,128]{2,1,0:T(8,128)S(1)}, u32[]{:S(2)}, u32[]{:S(2)}) collective-permute-start(f32[4,32,128]{2,1,0:T(8,128)S(1)} %constant_dynamic-update-slice_fusion.2), channel_id=1, source_target_pairs={{0,2},{1,7},{2,4},{3,1},{4,6},{5,3},{6,0},{7,5},{8,10},{9,15},{10,... | collective-permute-start | bytes 196616 | tf_op jit(solution)/shard_map/ppermute | solution.py:369
  78.4 2.3 %collective-permute-start.10 = (f32[4,32,128]{2,1,0:T(8,128)S(1)}, f32[4,32,128]{2,1,0:T(8,128)S(1)}, u32[]{:S(2)}, u32[]{:S(2)}) collective-permute-start(f32[4,32,128]{2,1,0:T(8,128)S(1)} %constant_dynamic-update-slice_fusion.2), channel_id=1, source_target_pairs={{0,4},{1,5},{2,6},{3,7},{4,0},{5,1},{6,2},{7,3},{8,12},{9,13},{10,... | collective-permute-start | bytes 196616 | tf_op jit(solution)/shard_map/ppermute | solution.py:397
  80.7 2.4 %collective-permute-done.8.rest_2_ = f32[4,32,128]{2,1,0:T(8,128)S(1)} collective-permute-done((f32[4,32,128]{2,1,0:T(8,128)S(1)}, f32[4,32,128]{2,1,0:T(8,128)S(1)}, u32[]{:S(2)}, u32[]{:S(2)}) %collective-permute-start.8) | collective-permute-done | bytes 65568 | tf_op jit(solution)/shard_map/ppermute | solution.py:369
  83.1 0.0 collective-permute-start.9
  83.1 4.5 %collective-permute-done.10.rest_4_ = f32[4,32,128]{2,1,0:T(8,128)S(1)} collective-permute-done((f32[4,32,128]{2,1,0:T(8,128)S(1)}, f32[4,32,128]{2,1,0:T(8,128)S(1)}, u32[]{:S(2)}, u32[]{:S(2)}) %collective-permute-start.10) | collective-permute-done | bytes 65568 | tf_op jit(solution)/shard_map/ppermute | solution.py:397
  87.6 0.0 collective-permute-done.9.rest_3_
  87.6 0.0 collective-permute-done.15.rest_10_
  87.6 0.0 collective-permute-done.16.rest_11_
  87.6 0.0 collective-permute-done.17.rest_12_
  87.6 0.0 copy-done
  87.6 5.2 %correct.1 = f32[4,7,32,1024]{3,2,1,0:T(8,128)} custom-call(f32[4,7,32,1024]{3,2,1,0:T(8,128)S(1)} %get-tuple-element.17.refl, f32[8,4,2,32,128]{4,3,2,1,0:T(8,128)S(1)} %get-tuple-element.23.kernels, f32[32,1024]{1,0:T(8,128)S(1)} %copy-done, f32[2,32,128]{2,1,0:T(8,128)S(1)} %get-tuple-element.32.rest_0_, ...), custom_call_target="tpu_custom_call" | custom-call | tf_op jit(solution)/shard_map/correct/pallas_call | solution.py:351
  (3 shorter events, 0.0 us)
Async XLA Ops:
  3.6 3.8 %collective-permute-start = (f32[4,27,32,128]{3,2,1,0:T(8,128)S(1)}, f32[4,27,32,128]{3,2,1,0:T(8,128)S(1)}, u32[]{:S(2)}, u32[]{:S(2)}) collective-permute-start(f32[4,27,32,128]{3,2,1,0:T(8,128)S(1)} %get-tuple-element.25), channel_id=1, source_target_pairs={{0,1},{1,0},{2,3},{3,2},{4,5},{5,4},{6,7},{7,6},{8,9},{9,8},{10,11... | collective-permute-start | bytes 5308424 | tf_op jit(solution)/shard_map/ppermute | solution.py:372
  7.6 14.2 %collective-permute-start.3 = (f32[27,32,128]{2,1,0:T(8,128)S(1)}, f32[27,32,128]{2,1,0:T(8,128)S(1)}, u32[]{:S(2)}, u32[]{:S(2)}) collective-permute-start(f32[27,32,128]{2,1,0:T(8,128)S(1)} %get-tuple-element.29), channel_id=1, source_target_pairs={{0,2},{1,7},{2,4},{3,1},{4,6},{5,3},{6,0},{7,5},{8,10},{9,15},{10,... | collective-permute-start | bytes 1327112 | tf_op jit(solution)/shard_map/ppermute | solution.py:369
  10.9 17.5 %collective-permute-start.1 = (f32[27,32,128]{2,1,0:T(8,128)S(1)}, f32[27,32,128]{2,1,0:T(8,128)S(1)}, u32[]{:S(2)}, u32[]{:S(2)}) collective-permute-start(f32[27,32,128]{2,1,0:T(8,128)S(1)} %get-tuple-element.30), channel_id=1, source_target_pairs={{0,2},{1,7},{2,4},{3,1},{4,6},{5,3},{6,0},{7,5},{8,10},{9,15},{10,... | collective-permute-start | bytes 1327112 | tf_op jit(solution)/shard_map/ppermute | solution.py:369
  21.9 65.7 %copy-start = (f32[32,1024]{1,0:T(8,128)S(1)}, f32[32,1024]{1,0:T(8,128)}, u32[]{:S(2)}) copy-start(f32[32,1024]{1,0:T(8,128)} %nadir.1) | copy-start | bytes 393220
  21.9 13.9 %collective-permute-start.4 = (f32[27,32,128]{2,1,0:T(8,128)S(1)}, f32[27,32,128]{2,1,0:T(8,128)S(1)}, u32[]{:S(2)}, u32[]{:S(2)}) collective-permute-start(f32[27,32,128]{2,1,0:T(8,128)S(1)} %fusion.2), channel_id=1, source_target_pairs={{0,2},{1,7},{2,4},{3,1},{4,6},{5,3},{6,0},{7,5},{8,10},{9,15},{10,... | collective-permute-start | bytes 1327112 | tf_op jit(solution)/shard_map/ppermute | solution.py:369
  28.4 8.8 %collective-permute-start.2 = (f32[27,32,128]{2,1,0:T(8,128)S(1)}, f32[27,32,128]{2,1,0:T(8,128)S(1)}, u32[]{:S(2)}, u32[]{:S(2)}) collective-permute-start(f32[27,32,128]{2,1,0:T(8,128)S(1)} %collective-permute-done.1), channel_id=1, source_target_pairs={{0,1},{1,0},{2,3},{3,2},{4,5},{5,4},{6,7},{7,6},{8,9},{9,8},{10,11... | collective-permute-start | bytes 1327112 | tf_op jit(solution)/shard_map/ppermute | solution.py:372
  37.5 7.8 %collective-permute-start.12 = (f32[21,32,128]{2,1,0:T(8,128)S(1)}, f32[21,32,128]{2,1,0:T(8,128)S(1)}, u32[]{:S(2)}, u32[]{:S(2)}) collective-permute-start(f32[21,32,128]{2,1,0:T(8,128)S(1)} %get-tuple-element.28.rest_5_), channel_id=1, source_target_pairs={{0,1},{1,0},{2,3},{3,2},{4,5},{5,4},{6,7},{7,6},{8,9},{9,8},{10,11... | collective-permute-start | bytes 1032200 | tf_op jit(solution)/shard_map/ppermute | solution.py:372
  43.2 13.8 %collective-permute-start.11 = (f32[21,32,128]{2,1,0:T(8,128)S(1)}, f32[21,32,128]{2,1,0:T(8,128)S(1)}, u32[]{:S(2)}, u32[]{:S(2)}) collective-permute-start(f32[21,32,128]{2,1,0:T(8,128)S(1)} %get-tuple-element.28.rest_5_), channel_id=1, source_target_pairs={{0,2},{1,7},{2,4},{3,1},{4,6},{5,3},{6,0},{7,5},{8,10},{9,15},{10,... | collective-permute-start | bytes 1032200 | tf_op jit(solution)/shard_map/ppermute | solution.py:369
  45.3 29.1 %collective-permute-start.13 = (f32[21,32,128]{2,1,0:T(8,128)S(1)}, f32[21,32,128]{2,1,0:T(8,128)S(1)}, u32[]{:S(2)}, u32[]{:S(2)}) collective-permute-start(f32[21,32,128]{2,1,0:T(8,128)S(1)} %collective-permute-done.12.rest_9_), channel_id=1, source_target_pairs={{0,2},{1,7},{2,4},{3,1},{4,6},{5,3},{6,0},{7,5},{8,10},{9,15},{10,... | collective-permute-start | bytes 1032200 | tf_op jit(solution)/shard_map/ppermute | solution.py:369
  56.9 17.6 %collective-permute-start.14 = (f32[21,32,128]{2,1,0:T(8,128)S(1)}, f32[21,32,128]{2,1,0:T(8,128)S(1)}, u32[]{:S(2)}, u32[]{:S(2)}) collective-permute-start(f32[21,32,128]{2,1,0:T(8,128)S(1)} %collective-permute-done.11.rest_6_), channel_id=1, source_target_pairs={{0,2},{1,7},{2,4},{3,1},{4,6},{5,3},{6,0},{7,5},{8,10},{9,15},{10,... | collective-permute-start | bytes 1032200 | tf_op jit(solution)/shard_map/ppermute | solution.py:369
  59.0 9.3 %collective-permute-start.5 = (f32[1,32,128]{2,1,0:T(8,128)S(1)}, f32[1,32,128]{2,1,0:T(8,128)S(1)}, u32[]{:S(2)}, u32[]{:S(2)}) collective-permute-start(f32[1,32,128]{2,1,0:T(8,128)S(1)} %get-tuple-element.26), channel_id=1, source_target_pairs={{0,8},{8,16},{16,24},{24,32},{32,40},{40,48},{48,56},{56,64},{64,7... | collective-permute-start | bytes 49160 | tf_op jit(solution)/shard_map/ppermute | solution.py:391
  62.5 12.4 %collective-permute-start.6 = (f32[1,32,128]{2,1,0:T(8,128)S(1)}, f32[1,32,128]{2,1,0:T(8,128)S(1)}, u32[]{:S(2)}, u32[]{:S(2)}) collective-permute-start(f32[1,32,128]{2,1,0:T(8,128)S(1)} %get-tuple-element.27), channel_id=1, source_target_pairs={{8,0},{16,8},{24,16},{32,24},{40,32},{48,40},{56,48},{64,56},{72,6... | collective-permute-start | bytes 49160 | tf_op jit(solution)/shard_map/ppermute | solution.py:392
  68.3 19.2 %collective-permute-start.15 = (f32[21,32,128]{2,1,0:T(8,128)S(1)}, f32[21,32,128]{2,1,0:T(8,128)S(1)}, u32[]{:S(2)}, u32[]{:S(2)}) collective-permute-start(f32[21,32,128]{2,1,0:T(8,128)S(1)} %collective-permute-done.11.rest_6_), channel_id=1, source_target_pairs={{0,1},{1,0},{2,3},{3,2},{4,5},{5,4},{6,7},{7,6},{8,9},{9,8},{10,11... | collective-permute-start | bytes 1032200 | tf_op jit(solution)/shard_map/ppermute | solution.py:372
  74.4 13.2 %collective-permute-start.16 = (f32[21,32,128]{2,1,0:T(8,128)S(1)}, f32[21,32,128]{2,1,0:T(8,128)S(1)}, u32[]{:S(2)}, u32[]{:S(2)}) collective-permute-start(f32[21,32,128]{2,1,0:T(8,128)S(1)} %collective-permute-done.13.rest_7_), channel_id=1, source_target_pairs={{0,1},{1,0},{2,3},{3,2},{4,5},{5,4},{6,7},{7,6},{8,9},{9,8},{10,11... | collective-permute-start | bytes 1032200 | tf_op jit(solution)/shard_map/ppermute | solution.py:372
  74.5 13.0 %collective-permute-start.17 = (f32[21,32,128]{2,1,0:T(8,128)S(1)}, f32[21,32,128]{2,1,0:T(8,128)S(1)}, u32[]{:S(2)}, u32[]{:S(2)}) collective-permute-start(f32[21,32,128]{2,1,0:T(8,128)S(1)} %collective-permute-done.14.rest_8_), channel_id=1, source_target_pairs={{0,1},{1,0},{2,3},{3,2},{4,5},{5,4},{6,7},{7,6},{8,9},{9,8},{10,11... | collective-permute-start | bytes 1032200 | tf_op jit(solution)/shard_map/ppermute | solution.py:372
  74.9 1.8 %collective-permute-start.7 = (f32[2,32,128]{2,1,0:T(8,128)S(1)}, f32[2,32,128]{2,1,0:T(8,128)S(1)}, u32[]{:S(2)}, u32[]{:S(2)}) collective-permute-start(f32[2,32,128]{2,1,0:T(8,128)S(1)} %get-tuple-element.32.rest_0_), channel_id=1, source_target_pairs={{0,1},{1,0},{2,3},{3,2},{4,5},{5,4},{6,7},{7,6},{8,9},{9,8},{10,11... | collective-permute-start | bytes 98312 | tf_op jit(solution)/shard_map/ppermute | solution.py:372
  76.7 6.4 %collective-permute-start.8 = (f32[4,32,128]{2,1,0:T(8,128)S(1)}, f32[4,32,128]{2,1,0:T(8,128)S(1)}, u32[]{:S(2)}, u32[]{:S(2)}) collective-permute-start(f32[4,32,128]{2,1,0:T(8,128)S(1)} %constant_dynamic-update-slice_fusion.2), channel_id=1, source_target_pairs={{0,2},{1,7},{2,4},{3,1},{4,6},{5,3},{6,0},{7,5},{8,10},{9,15},{10,... | collective-permute-start | bytes 196616 | tf_op jit(solution)/shard_map/ppermute | solution.py:369
  78.4 9.1 %collective-permute-start.10 = (f32[4,32,128]{2,1,0:T(8,128)S(1)}, f32[4,32,128]{2,1,0:T(8,128)S(1)}, u32[]{:S(2)}, u32[]{:S(2)}) collective-permute-start(f32[4,32,128]{2,1,0:T(8,128)S(1)} %constant_dynamic-update-slice_fusion.2), channel_id=1, source_target_pairs={{0,4},{1,5},{2,6},{3,7},{4,0},{5,1},{6,2},{7,3},{8,12},{9,13},{10,... | collective-permute-start | bytes 196616 | tf_op jit(solution)/shard_map/ppermute | solution.py:397
  83.1 4.5 %collective-permute-start.9 = (f32[4,32,128]{2,1,0:T(8,128)S(1)}, f32[4,32,128]{2,1,0:T(8,128)S(1)}, u32[]{:S(2)}, u32[]{:S(2)}) collective-permute-start(f32[4,32,128]{2,1,0:T(8,128)S(1)} %collective-permute-done.8.rest_2_), channel_id=1, source_target_pairs={{0,1},{1,0},{2,3},{3,2},{4,5},{5,4},{6,7},{7,6},{8,9},{9,8},{10,11... | collective-permute-start | bytes 196616 | tf_op jit(solution)/shard_map/ppermute | solution.py:372

commit v2 on v1

--- a/solution.py
+++ b/solution.py
@@ -1,3 +1,4 @@
+import functools
 import math
 
 import jax
@@ -143,52 +144,48 @@
             sums[part, i, r] = x
 
 
-def other_kernel(*refs):
-    sources, (sums, kernels), held, sems = refs[:5], refs[5:7], refs[7:12], refs[12]
+def copies_in(sources, held, sems):
+    dates = held[0].shape[0]
+    for k in (1, 2, 3, 4, 0):
+        for t in range(dates):
+            pltpu.make_async_copy(sources[k].at[t], held[k].at[t], sems.at[k, t]).start()
+
+    def wait(k, t):
+        pltpu.make_async_copy(sources[k].at[t], held[k].at[t], sems.at[k, t]).wait()
+
+    return wait
+
+
+def far_kernel(*refs):
+    sources, sums, kernels, held, sems = refs[:5], refs[5:7], refs[7], refs[8:13], refs[13]
     refl, sun, view, azim, flags = held
-    dates, _, rows, _ = refl.shape
-    ring = sums.shape[0]
-    copies = [
-        [pltpu.make_async_copy(sources[k].at[t], held[k].at[t], sems.at[k, t]) for t in range(dates)]
-        for k in range(5)
-    ]
+    dates, _, rows, cols = refl.shape
+    ring = cols // LANES // 2
+    wait = copies_in(sources, held, sems)
+    blocks = [sums_part(3, flip, ring) for flip in (True, False)]
     for t in range(dates):
-        for k in range(1, 5):
-            copies[k][t].start()
-    for t in range(dates):
-        copies[0][t].start()
-    for t in range(dates):
-        for k in range(1, 4):
-            copies[k][t].wait()
-
-        def angles(i, carry):
-            block = sums_part(i, True, ring)
+        for k in (1, 2, 3):
+            wait(k, t)
+        for block in blocks:
             lanes = lanes_of(block)
             for g in range(rows // SUB):
                 r = slice(g * SUB, (g + 1) * SUB)
                 kvol, kgeo = ross_li(sun[t, r, lanes], view[t, r, lanes], azim[t, r, lanes])
                 kernels[block, t, 0, r] = kvol
                 kernels[block, t, 1, r] = kgeo
-            return carry
-
-        lax.fori_loop(0, ring, angles, 0)
-    for t in range(dates):
-        copies[4][t].wait()
-        copies[0][t].wait()
+    for k in (4, 0):
+        for t in range(dates):
+            wait(k, t)
+    for block, total in zip(blocks, sums):
+        kernel_of = lambda t, r: (kernels[block, t, 0, r], kernels[block, t, 1, r])
+        add_dates(total, 0, block, refl, flags, kernel_of)
+
+
+def rest_kernel(flip, refl, sun, view, azim, flags, _, sums, kernels):
+    ring = refl.shape[3] // LANES // 2
 
     def one(i, carry):
-        block = sums_part(i, True, ring)
-        add_dates(sums, i, block, refl, flags, lambda t, r: (kernels[block, t, 0, r], kernels[block, t, 1, r]))
-        return carry
-
-    lax.fori_loop(0, ring, one, 0)
-
-
-def own_kernel(refl, sun, view, azim, flags, _, sums, kernels):
-    ring = sums.shape[0]
-
-    def one(i, carry):
-        block = sums_part(i, False, ring)
+        block = sums_part(i, flip, ring)
         lanes = lanes_of(block)
 
         def kernel_of(t, r):
@@ -200,40 +197,43 @@
         add_dates(sums, i, block, refl, flags, kernel_of)
         return carry
 
-    lax.fori_loop(0, ring, one, 0)
-
-
-def sums_shapes(refl):
-    dates, bands, rows, cols = refl.shape
-    parts = cols // LANES
-    return [
-        jax.ShapeDtypeStruct((parts // 2, 6 + 3 * bands, rows, LANES), jnp.float32),
-        jax.ShapeDtypeStruct((parts, dates, 2, rows, LANES), jnp.float32),
-    ]
-
-
-def other_sums(*inputs):
+    lax.fori_loop(0, ring - 1, one, 0)
+
+
+def sums_shape(refl, parts):
+    _, bands, rows, _ = refl.shape
+    return jax.ShapeDtypeStruct((parts, 6 + 3 * bands, rows, LANES), jnp.float32)
+
+
+def kernels_shape(refl):
+    dates, _, rows, cols = refl.shape
+    return jax.ShapeDtypeStruct((cols // LANES, dates, 2, rows, LANES), jnp.float32)
+
+
+def far_sums(*inputs):
+    refl = inputs[0]
     held = [jax.ShapeDtypeStruct(x.shape, x.dtype) for x in inputs]
     return pl.pallas_call(
-        other_kernel,
+        far_kernel,
         in_specs=[pl.BlockSpec(memory_space=pltpu.HBM)] * 5,
-        out_specs=[VMEM] * 7,
-        out_shape=sums_shapes(inputs[0]) + held,
-        scratch_shapes=[pltpu.SemaphoreType.DMA((5, inputs[0].shape[0]))],
+        out_specs=[VMEM] * 8,
+        out_shape=[sums_shape(refl, 1), sums_shape(refl, 1), kernels_shape(refl)] + held,
+        scratch_shapes=[pltpu.SemaphoreType.DMA((5, refl.shape[0]))],
         compiler_params=pltpu.CompilerParams(vmem_limit_bytes=16 << 20),
-        name="other_sums",
+        name="far_sums",
     )(*(pltpu.with_memory_space_constraint(x, pltpu.HBM) for x in inputs))
 
 
-def own_sums(inputs, kernels):
+def rest_sums(flip, inputs, kernels):
+    refl = inputs[0]
+    ring = refl.shape[3] // LANES // 2
     return pl.pallas_call(
-        own_kernel,
+        functools.partial(rest_kernel, flip),
         in_specs=[VMEM] * 6,
         out_specs=[VMEM] * 2,
-        out_shape=sums_shapes(inputs[0]),
+        out_shape=[sums_shape(refl, ring - 1), kernels_shape(refl)],
         input_output_aliases={5: 1},
         compiler_params=pltpu.CompilerParams(vmem_limit_bytes=16 << 20),
-        name="own_sums",
     )(*inputs, kernels)
 
 
@@ -371,10 +371,13 @@
     def swap(x):
         return lax.ppermute(x, "dates", [(i, i ^ 1) for i in range(devices)])
 
-    other, kernels, *held = other_sums(reflectance, sun_zenith, view_zenith, rel_azimuth, flags)
+    inputs = (reflectance, sun_zenith, view_zenith, rel_azimuth, flags)
+    far_other, far_mine, kernels, *held = far_sums(*inputs)
+    far_other = swap(far_other)
+    other, kernels = rest_sums(True, held, kernels)
     other = swap(other)
-    mine, kernels = own_sums(held, kernels)
-    far = onward(mine[3] + other[3])
+    far = onward((far_mine + far_other)[0])
+    mine, kernels = rest_sums(False, held, kernels)
     near = onward(mine[2] + other[2])
     far = onward(mine[1] + other[1] + far)
     near = swap(near)

time: 92.9 us -> 93.8 us (level)
  the two profiles are of different devices: /device:TPU:6 before, /device:TPU:28 now
where the time goes in v2:
time: 93.8 us; the launch traced here: 92.2 us
  starting transfers between devices  46.9 us (50%)
  waiting for transfers between devices  33.8 us (36%)
  Pallas kernels  11.2 us (12%)
    ppermute x7, waiting for transfers between devices, onward(): return lax.ppermute(x, 'dates', pairs)  20.3 us
    ppermute x7, starting transfers between devices, onward(): return lax.ppermute(x, 'dates', pairs)  20.1 us
    ppermute x9, starting transfers between devices, swap(): return lax.ppermute(x, 'dates', [(i, i ^ 1) for i in range(devices)])  19.3 us
    ppermute x9, waiting for transfers between devices, swap(): return lax.ppermute(x, 'dates', [(i, i ^ 1) for i in range(devices)])  5.34 us
    pallas_call x1, Pallas kernels, correct(): pl.pallas_call(correct_kernel, grid=(parts,), in_specs=[VMEM] * (3 + len(...  5.16 us
    ppermute x1, waiting for transfers between devices, per_device(): lax.ppermute(halo_both, 'dates', [(i, (i + devices // 2) % devices) for i...  4.47 us
    ppermute x1, starting transfers between devices, per_device(): below = lax.ppermute(below, 'rows', [(i + 1, i) for i in range(blocks - 1)])  3.92 us
    ppermute x1, waiting for transfers between devices, per_device(): above = lax.ppermute(above, 'rows', [(i, i + 1) for i in range(blocks - 1)])  3.61 us
  transfers between devices with their start and end apart: 19, of which 10 were waited for; matrix products, arithmetic and copies ran while one was open for 0% of the time, Pallas kernels for 1%

profile of v2, /device:TPU:28, one launch (start us, length us, event | category | flops | bytes accessed | tf_op | source)
XLA Modules:
  0.0 92.2 jit_solution(12953269437563739303)
XLA Ops:
  0.0 3.2 %far_sums.1 = (f32[1,27,32,128]{3,2,1,0:T(8,128)S(1)}, f32[1,27,32,128]{3,2,1,0:T(8,128)S(1)}, f32[8,4,2,32,128]{4,3,2,1,0:T(8,128)S(1)}, f32[4,7,32,1024]{3,2,1...) custom-call(f32[4,7,32,1024]{3,2,1,0:T(8,128)} %refs_0_.1, ...), custom_call_target="tpu_custom_call" | custom-call | tf_op jit(solution)/shard_map/far_sums/pallas_call | solution.py:216
  3.2 1.3 %shard_map.64 = (f32[3,27,32,128]{3,2,1,0:T(8,128)S(1)}, f32[8,4,2,32,128]{4,3,2,1,0:T(8,128)S(1)}) custom-call(f32[4,7,32,1024]{3,2,1,0:T(8,128)S(1)} %get-tuple-element.20.refl, f32[4,32,1024]{2,1,0:T(8,128)S(1)} %get-tuple-element.21.sun, f32[4,32,1024]{2,1,0:T(8,128)S(1)} %get-tuple-element.22.view, ...), custom_call_target="tpu_custom_call", output_to_operand_aliasing={{1}: (5, {})} | custom-call | tf_op jit(solution)/shard_map/pallas_call | solution.py:230
  4.5 0.1 collective-permute-start
  4.6 0.5 collective-permute-start.3
  5.1 3.2 %collective-permute-done.3 = f32[1,27,32,128]{3,2,1,0:T(8,128)S(1)} collective-permute-done((f32[1,27,32,128]{3,2,1,0:T(8,128)S(1)}, f32[1,27,32,128]{3,2,1,0:T(8,128)S(1)}, u32[]{:S(2)}, u32[]{:S(2)}) %collective-permute-start.3) | collective-permute-done | bytes 442400 | tf_op jit(solution)/shard_map/ppermute | solution.py:372
  8.3 0.1 add_bitcast_fusion
  8.3 3.3 %collective-permute-start.4 = (f32[27,32,128]{2,1,0:T(8,128)S(1)}, f32[27,32,128]{2,1,0:T(8,128)S(1)}, u32[]{:S(2)}, u32[]{:S(2)}) collective-permute-start(f32[27,32,128]{2,1,0:T(8,128)S(1)} %add_bitcast_fusion), channel_id=1, source_target_pairs={{0,2},{1,7},{2,4},{3,1},{4,6},{5,3},{6,0},{7,5},{8,10},{9,15},{10,... | collective-permute-start | bytes 1327112 | tf_op jit(solution)/shard_map/ppermute | solution.py:369
  11.7 1.3 %shard_map.65 = (f32[3,27,32,128]{3,2,1,0:T(8,128)S(1)}, f32[8,4,2,32,128]{4,3,2,1,0:T(8,128)S(1)}) custom-call(f32[4,7,32,1024]{3,2,1,0:T(8,128)S(1)} %get-tuple-element.20.refl, f32[4,32,1024]{2,1,0:T(8,128)S(1)} %get-tuple-element.21.sun, f32[4,32,1024]{2,1,0:T(8,128)S(1)} %get-tuple-element.22.view, ...), custom_call_target="tpu_custom_call", output_to_operand_aliasing={{1}: (5, {})} | custom-call | tf_op jit(solution)/shard_map/pallas_call | solution.py:230
  13.0 0.0 collective-permute-done.own_b
  13.0 0.1 fusion.2
  13.0 4.6 %collective-permute-start.1 = (f32[27,32,128]{2,1,0:T(8,128)S(1)}, f32[27,32,128]{2,1,0:T(8,128)S(1)}, u32[]{:S(2)}, u32[]{:S(2)}) collective-permute-start(f32[27,32,128]{2,1,0:T(8,128)S(1)} %fusion.2), channel_id=1, source_target_pairs={{0,2},{1,7},{2,4},{3,1},{4,6},{5,3},{6,0},{7,5},{8,10},{9,15},{10,... | collective-permute-start | bytes 1327112 | tf_op jit(solution)/shard_map/ppermute | solution.py:369
  17.6 4.9 %collective-permute-done.4 = f32[27,32,128]{2,1,0:T(8,128)S(1)} collective-permute-done((f32[27,32,128]{2,1,0:T(8,128)S(1)}, f32[27,32,128]{2,1,0:T(8,128)S(1)}, u32[]{:S(2)}, u32[]{:S(2)}) %collective-permute-start.4) | collective-permute-done | bytes 442400 | tf_op jit(solution)/shard_map/ppermute | solution.py:369
  22.5 0.1 fusion.1
  22.6 0.0 copy-start
  22.7 1.7 %collective-permute-start.5 = (f32[27,32,128]{2,1,0:T(8,128)S(1)}, f32[27,32,128]{2,1,0:T(8,128)S(1)}, u32[]{:S(2)}, u32[]{:S(2)}) collective-permute-start(f32[27,32,128]{2,1,0:T(8,128)S(1)} %fusion.1), channel_id=1, source_target_pairs={{0,2},{1,7},{2,4},{3,1},{4,6},{5,3},{6,0},{7,5},{8,10},{9,15},{10,... | collective-permute-start | bytes 1327112 | tf_op jit(solution)/shard_map/ppermute | solution.py:369
  24.3 4.9 %collective-permute-done.1 = f32[27,32,128]{2,1,0:T(8,128)S(1)} collective-permute-done((f32[27,32,128]{2,1,0:T(8,128)S(1)}, f32[27,32,128]{2,1,0:T(8,128)S(1)}, u32[]{:S(2)}, u32[]{:S(2)}) %collective-permute-start.1) | collective-permute-done | bytes 442400 | tf_op jit(solution)/shard_map/ppermute | solution.py:369
  29.3 7.3 %collective-permute-start.2 = (f32[27,32,128]{2,1,0:T(8,128)S(1)}, f32[27,32,128]{2,1,0:T(8,128)S(1)}, u32[]{:S(2)}, u32[]{:S(2)}) collective-permute-start(f32[27,32,128]{2,1,0:T(8,128)S(1)} %collective-permute-done.1), channel_id=1, source_target_pairs={{0,1},{1,0},{2,3},{3,2},{4,5},{5,4},{6,7},{7,6},{8,9},{9,8},{10,11... | collective-permute-start | bytes 1327112 | tf_op jit(solution)/shard_map/ppermute | solution.py:372
  36.6 0.1 collective-permute-done.5.far
  36.7 1.3 %collective-permute-done.2.near = f32[27,32,128]{2,1,0:T(8,128)S(1)} collective-permute-done((f32[27,32,128]{2,1,0:T(8,128)S(1)}, f32[27,32,128]{2,1,0:T(8,128)S(1)}, u32[]{:S(2)}, u32[]{:S(2)}) %collective-permute-start.2) | collective-permute-done | bytes 442400 | tf_op jit(solution)/shard_map/ppermute | solution.py:372
  38.0 0.3 solve.1
  38.3 5.6 %collective-permute-start.13 = (f32[21,32,128]{2,1,0:T(8,128)S(1)}, f32[21,32,128]{2,1,0:T(8,128)S(1)}, u32[]{:S(2)}, u32[]{:S(2)}) collective-permute-start(f32[21,32,128]{2,1,0:T(8,128)S(1)} %get-tuple-element.34.rest_5_), channel_id=1, source_target_pairs={{0,1},{1,0},{2,3},{3,2},{4,5},{5,4},{6,7},{7,6},{8,9},{9,8},{10,11... | collective-permute-start | bytes 1032200 | tf_op jit(solution)/shard_map/ppermute | solution.py:372
  43.9 2.2 %collective-permute-start.12 = (f32[21,32,128]{2,1,0:T(8,128)S(1)}, f32[21,32,128]{2,1,0:T(8,128)S(1)}, u32[]{:S(2)}, u32[]{:S(2)}) collective-permute-start(f32[21,32,128]{2,1,0:T(8,128)S(1)} %get-tuple-element.34.rest_5_), channel_id=1, source_target_pairs={{0,2},{1,7},{2,4},{3,1},{4,6},{5,3},{6,0},{7,5},{8,10},{9,15},{10,... | collective-permute-start | bytes 1032200 | tf_op jit(solution)/shard_map/ppermute | solution.py:369
  46.1 0.0 collective-permute-done.13.rest_9_
  46.1 4.6 %collective-permute-start.14 = (f32[21,32,128]{2,1,0:T(8,128)S(1)}, f32[21,32,128]{2,1,0:T(8,128)S(1)}, u32[]{:S(2)}, u32[]{:S(2)}) collective-permute-start(f32[21,32,128]{2,1,0:T(8,128)S(1)} %collective-permute-done.13.rest_9_), channel_id=1, source_target_pairs={{0,2},{1,7},{2,4},{3,1},{4,6},{5,3},{6,0},{7,5},{8,10},{9,15},{10,... | collective-permute-start | bytes 1032200 | tf_op jit(solution)/shard_map/ppermute | solution.py:369
  50.6 7.2 %collective-permute-done.12.rest_6_ = f32[21,32,128]{2,1,0:T(8,128)S(1)} collective-permute-done((f32[21,32,128]{2,1,0:T(8,128)S(1)}, f32[21,32,128]{2,1,0:T(8,128)S(1)}, u32[]{:S(2)}, u32[]{:S(2)}) %collective-permute-start.12) | collective-permute-done | bytes 344096 | tf_op jit(solution)/shard_map/ppermute | solution.py:369
  57.9 2.1 %collective-permute-start.15 = (f32[21,32,128]{2,1,0:T(8,128)S(1)}, f32[21,32,128]{2,1,0:T(8,128)S(1)}, u32[]{:S(2)}, u32[]{:S(2)}) collective-permute-start(f32[21,32,128]{2,1,0:T(8,128)S(1)} %collective-permute-done.12.rest_6_), channel_id=1, source_target_pairs={{0,2},{1,7},{2,4},{3,1},{4,6},{5,3},{6,0},{7,5},{8,10},{9,15},{10,... | collective-permute-start | bytes 1032200 | tf_op jit(solution)/shard_map/ppermute | solution.py:369
  60.0 1.9 %collective-permute-start.6 = (f32[1,32,128]{2,1,0:T(8,128)S(1)}, f32[1,32,128]{2,1,0:T(8,128)S(1)}, u32[]{:S(2)}, u32[]{:S(2)}) collective-permute-start(f32[1,32,128]{2,1,0:T(8,128)S(1)} %get-tuple-element.32), channel_id=1, source_target_pairs={{0,8},{8,16},{16,24},{24,32},{32,40},{40,48},{48,56},{56,64},{64,7... | collective-permute-start | bytes 49160 | tf_op jit(solution)/shard_map/ppermute | solution.py:394
  61.9 3.9 %collective-permute-start.7 = (f32[1,32,128]{2,1,0:T(8,128)S(1)}, f32[1,32,128]{2,1,0:T(8,128)S(1)}, u32[]{:S(2)}, u32[]{:S(2)}) collective-permute-start(f32[1,32,128]{2,1,0:T(8,128)S(1)} %get-tuple-element.33), channel_id=1, source_target_pairs={{8,0},{16,8},{24,16},{32,24},{40,32},{48,40},{56,48},{64,56},{72,6... | collective-permute-start | bytes 49160 | tf_op jit(solution)/shard_map/ppermute | solution.py:395
  65.8 3.6 %collective-permute-done.6 = f32[1,32,128]{2,1,0:T(8,128)S(1)} collective-permute-done((f32[1,32,128]{2,1,0:T(8,128)S(1)}, f32[1,32,128]{2,1,0:T(8,128)S(1)}, u32[]{:S(2)}, u32[]{:S(2)}) %collective-permute-start.6) | collective-permute-done | bytes 16416 | tf_op jit(solution)/shard_map/ppermute | solution.py:394
  69.5 2.7 %collective-permute-start.16 = (f32[21,32,128]{2,1,0:T(8,128)S(1)}, f32[21,32,128]{2,1,0:T(8,128)S(1)}, u32[]{:S(2)}, u32[]{:S(2)}) collective-permute-start(f32[21,32,128]{2,1,0:T(8,128)S(1)} %collective-permute-done.12.rest_6_), channel_id=1, source_target_pairs={{0,1},{1,0},{2,3},{3,2},{4,5},{5,4},{6,7},{7,6},{8,9},{9,8},{10,11... | collective-permute-start | bytes 1032200 | tf_op jit(solution)/shard_map/ppermute | solution.py:372
  72.1 0.0 collective-permute-done.14.rest_7_
  72.1 0.1 collective-permute-start.17
  72.2 0.0 collective-permute-done.15.rest_8_
  72.3 0.4 collective-permute-start.18
  72.7 0.0 collective-permute-done.7
  72.7 2.6 %collective-permute-start.8 = (f32[2,32,128]{2,1,0:T(8,128)S(1)}, f32[2,32,128]{2,1,0:T(8,128)S(1)}, u32[]{:S(2)}, u32[]{:S(2)}) collective-permute-start(f32[2,32,128]{2,1,0:T(8,128)S(1)} %get-tuple-element.36.rest_0_), channel_id=1, source_target_pairs={{0,1},{1,0},{2,3},{3,2},{4,5},{5,4},{6,7},{7,6},{8,9},{9,8},{10,11... | collective-permute-start | bytes 98312 | tf_op jit(solution)/shard_map/ppermute | solution.py:372
  75.3 0.9 collective-permute-done.8.rest_1_
  76.1 1.6 %collective-permute-start.9 = (f32[4,32,128]{2,1,0:T(8,128)S(1)}, f32[4,32,128]{2,1,0:T(8,128)S(1)}, u32[]{:S(2)}, u32[]{:S(2)}) collective-permute-start(f32[4,32,128]{2,1,0:T(8,128)S(1)} %constant_dynamic-update-slice_fusion.2), channel_id=1, source_target_pairs={{0,2},{1,7},{2,4},{3,1},{4,6},{5,3},{6,0},{7,5},{8,10},{9,15},{10,... | collective-permute-start | bytes 196616 | tf_op jit(solution)/shard_map/ppermute | solution.py:369
  77.8 1.7 %collective-permute-start.11 = (f32[4,32,128]{2,1,0:T(8,128)S(1)}, f32[4,32,128]{2,1,0:T(8,128)S(1)}, u32[]{:S(2)}, u32[]{:S(2)}) collective-permute-start(f32[4,32,128]{2,1,0:T(8,128)S(1)} %constant_dynamic-update-slice_fusion.2), channel_id=1, source_target_pairs={{0,4},{1,5},{2,6},{3,7},{4,0},{5,1},{6,2},{7,3},{8,12},{9,13},{10,... | collective-permute-start | bytes 196616 | tf_op jit(solution)/shard_map/ppermute | solution.py:400
  79.4 3.1 %collective-permute-done.9.rest_2_ = f32[4,32,128]{2,1,0:T(8,128)S(1)} collective-permute-done((f32[4,32,128]{2,1,0:T(8,128)S(1)}, f32[4,32,128]{2,1,0:T(8,128)S(1)}, u32[]{:S(2)}, u32[]{:S(2)}) %collective-permute-start.9) | collective-permute-done | bytes 65568 | tf_op jit(solution)/shard_map/ppermute | solution.py:369
  82.5 0.0 collective-permute-start.10
  82.5 4.5 %collective-permute-done.11.rest_4_ = f32[4,32,128]{2,1,0:T(8,128)S(1)} collective-permute-done((f32[4,32,128]{2,1,0:T(8,128)S(1)}, f32[4,32,128]{2,1,0:T(8,128)S(1)}, u32[]{:S(2)}, u32[]{:S(2)}) %collective-permute-start.11) | collective-permute-done | bytes 65568 | tf_op jit(solution)/shard_map/ppermute | solution.py:400
  87.0 0.0 collective-permute-done.10.rest_3_
  87.0 0.0 collective-permute-done.16.rest_10_
  87.0 0.0 collective-permute-done.17.rest_11_
  87.0 0.0 collective-permute-done.18.rest_12_
  87.0 0.0 copy-done
  87.0 5.2 %correct.1 = f32[4,7,32,1024]{3,2,1,0:T(8,128)} custom-call(f32[4,7,32,1024]{3,2,1,0:T(8,128)S(1)} %get-tuple-element.20.refl, f32[8,4,2,32,128]{4,3,2,1,0:T(8,128)S(1)} %get-tuple-element.27.kernels, f32[32,1024]{1,0:T(8,128)S(1)} %copy-done, f32[2,32,128]{2,1,0:T(8,128)S(1)} %get-tuple-element.36.rest_0_, ...), custom_call_target="tpu_custom_call" | custom-call | tf_op jit(solution)/shard_map/correct/pallas_call | solution.py:351
  (3 shorter events, 0.0 us)
Async XLA Ops:
  4.5 8.5 %collective-permute-start = (f32[3,27,32,128]{3,2,1,0:T(8,128)S(1)}, f32[3,27,32,128]{3,2,1,0:T(8,128)S(1)}, u32[]{:S(2)}, u32[]{:S(2)}) collective-permute-start(f32[3,27,32,128]{3,2,1,0:T(8,128)S(1)} %get-tuple-element.29), channel_id=1, source_target_pairs={{0,1},{1,0},{2,3},{3,2},{4,5},{5,4},{6,7},{7,6},{8,9},{9,8},{10,11... | collective-permute-start | bytes 3981320 | tf_op jit(solution)/shard_map/ppermute | solution.py:372
  4.6 3.7 %collective-permute-start.3 = (f32[1,27,32,128]{3,2,1,0:T(8,128)S(1)}, f32[1,27,32,128]{3,2,1,0:T(8,128)S(1)}, u32[]{:S(2)}, u32[]{:S(2)}) collective-permute-start(f32[1,27,32,128]{3,2,1,0:T(8,128)S(1)} %get-tuple-element.31), channel_id=1, source_target_pairs={{0,1},{1,0},{2,3},{3,2},{4,5},{5,4},{6,7},{7,6},{8,9},{9,8},{10,11... | collective-permute-start | bytes 1327112 | tf_op jit(solution)/shard_map/ppermute | solution.py:372
  8.3 14.2 %collective-permute-start.4 = (f32[27,32,128]{2,1,0:T(8,128)S(1)}, f32[27,32,128]{2,1,0:T(8,128)S(1)}, u32[]{:S(2)}, u32[]{:S(2)}) collective-permute-start(f32[27,32,128]{2,1,0:T(8,128)S(1)} %add_bitcast_fusion), channel_id=1, source_target_pairs={{0,2},{1,7},{2,4},{3,1},{4,6},{5,3},{6,0},{7,5},{8,10},{9,15},{10,... | collective-permute-start | bytes 1327112 | tf_op jit(solution)/shard_map/ppermute | solution.py:369
  13.0 16.2 %collective-permute-start.1 = (f32[27,32,128]{2,1,0:T(8,128)S(1)}, f32[27,32,128]{2,1,0:T(8,128)S(1)}, u32[]{:S(2)}, u32[]{:S(2)}) collective-permute-start(f32[27,32,128]{2,1,0:T(8,128)S(1)} %fusion.2), channel_id=1, source_target_pairs={{0,2},{1,7},{2,4},{3,1},{4,6},{5,3},{6,0},{7,5},{8,10},{9,15},{10,... | collective-permute-start | bytes 1327112 | tf_op jit(solution)/shard_map/ppermute | solution.py:369
  22.6 64.4 %copy-start = (f32[32,1024]{1,0:T(8,128)S(1)}, f32[32,1024]{1,0:T(8,128)}, u32[]{:S(2)}) copy-start(f32[32,1024]{1,0:T(8,128)} %nadir.1) | copy-start | bytes 393220
  22.7 14.0 %collective-permute-start.5 = (f32[27,32,128]{2,1,0:T(8,128)S(1)}, f32[27,32,128]{2,1,0:T(8,128)S(1)}, u32[]{:S(2)}, u32[]{:S(2)}) collective-permute-start(f32[27,32,128]{2,1,0:T(8,128)S(1)} %fusion.1), channel_id=1, source_target_pairs={{0,2},{1,7},{2,4},{3,1},{4,6},{5,3},{6,0},{7,5},{8,10},{9,15},{10,... | collective-permute-start | bytes 1327112 | tf_op jit(solution)/shard_map/ppermute | solution.py:369
  29.3 8.7 %collective-permute-start.2 = (f32[27,32,128]{2,1,0:T(8,128)S(1)}, f32[27,32,128]{2,1,0:T(8,128)S(1)}, u32[]{:S(2)}, u32[]{:S(2)}) collective-permute-start(f32[27,32,128]{2,1,0:T(8,128)S(1)} %collective-permute-done.1), channel_id=1, source_target_pairs={{0,1},{1,0},{2,3},{3,2},{4,5},{5,4},{6,7},{7,6},{8,9},{9,8},{10,11... | collective-permute-start | bytes 1327112 | tf_op jit(solution)/shard_map/ppermute | solution.py:372
  38.3 7.8 %collective-permute-start.13 = (f32[21,32,128]{2,1,0:T(8,128)S(1)}, f32[21,32,128]{2,1,0:T(8,128)S(1)}, u32[]{:S(2)}, u32[]{:S(2)}) collective-permute-start(f32[21,32,128]{2,1,0:T(8,128)S(1)} %get-tuple-element.34.rest_5_), channel_id=1, source_target_pairs={{0,1},{1,0},{2,3},{3,2},{4,5},{5,4},{6,7},{7,6},{8,9},{9,8},{10,11... | collective-permute-start | bytes 1032200 | tf_op jit(solution)/shard_map/ppermute | solution.py:372
  43.9 14.0 %collective-permute-start.12 = (f32[21,32,128]{2,1,0:T(8,128)S(1)}, f32[21,32,128]{2,1,0:T(8,128)S(1)}, u32[]{:S(2)}, u32[]{:S(2)}) collective-permute-start(f32[21,32,128]{2,1,0:T(8,128)S(1)} %get-tuple-element.34.rest_5_), channel_id=1, source_target_pairs={{0,2},{1,7},{2,4},{3,1},{4,6},{5,3},{6,0},{7,5},{8,10},{9,15},{10,... | collective-permute-start | bytes 1032200 | tf_op jit(solution)/shard_map/ppermute | solution.py:369
  46.1 26.1 %collective-permute-start.14 = (f32[21,32,128]{2,1,0:T(8,128)S(1)}, f32[21,32,128]{2,1,0:T(8,128)S(1)}, u32[]{:S(2)}, u32[]{:S(2)}) collective-permute-start(f32[21,32,128]{2,1,0:T(8,128)S(1)} %collective-permute-done.13.rest_9_), channel_id=1, source_target_pairs={{0,2},{1,7},{2,4},{3,1},{4,6},{5,3},{6,0},{7,5},{8,10},{9,15},{10,... | collective-permute-start | bytes 1032200 | tf_op jit(solution)/shard_map/ppermute | solution.py:369
  57.9 14.4 %collective-permute-start.15 = (f32[21,32,128]{2,1,0:T(8,128)S(1)}, f32[21,32,128]{2,1,0:T(8,128)S(1)}, u32[]{:S(2)}, u32[]{:S(2)}) collective-permute-start(f32[21,32,128]{2,1,0:T(8,128)S(1)} %collective-permute-done.12.rest_6_), channel_id=1, source_target_pairs={{0,2},{1,7},{2,4},{3,1},{4,6},{5,3},{6,0},{7,5},{8,10},{9,15},{10,... | collective-permute-start | bytes 1032200 | tf_op jit(solution)/shard_map/ppermute | solution.py:369
  60.0 9.5 %collective-permute-start.6 = (f32[1,32,128]{2,1,0:T(8,128)S(1)}, f32[1,32,128]{2,1,0:T(8,128)S(1)}, u32[]{:S(2)}, u32[]{:S(2)}) collective-permute-start(f32[1,32,128]{2,1,0:T(8,128)S(1)} %get-tuple-element.32), channel_id=1, source_target_pairs={{0,8},{8,16},{16,24},{24,32},{32,40},{40,48},{48,56},{56,64},{64,7... | collective-permute-start | bytes 49160 | tf_op jit(solution)/shard_map/ppermute | solution.py:394
  61.9 10.7 %collective-permute-start.7 = (f32[1,32,128]{2,1,0:T(8,128)S(1)}, f32[1,32,128]{2,1,0:T(8,128)S(1)}, u32[]{:S(2)}, u32[]{:S(2)}) collective-permute-start(f32[1,32,128]{2,1,0:T(8,128)S(1)} %get-tuple-element.33), channel_id=1, source_target_pairs={{8,0},{16,8},{24,16},{32,24},{40,32},{48,40},{56,48},{64,56},{72,6... | collective-permute-start | bytes 49160 | tf_op jit(solution)/shard_map/ppermute | solution.py:395
  69.5 17.5 %collective-permute-start.16 = (f32[21,32,128]{2,1,0:T(8,128)S(1)}, f32[21,32,128]{2,1,0:T(8,128)S(1)}, u32[]{:S(2)}, u32[]{:S(2)}) collective-permute-start(f32[21,32,128]{2,1,0:T(8,128)S(1)} %collective-permute-done.12.rest_6_), channel_id=1, source_target_pairs={{0,1},{1,0},{2,3},{3,2},{4,5},{5,4},{6,7},{7,6},{8,9},{9,8},{10,11... | collective-permute-start | bytes 1032200 | tf_op jit(solution)/shard_map/ppermute | solution.py:372
  72.1 14.9 %collective-permute-start.17 = (f32[21,32,128]{2,1,0:T(8,128)S(1)}, f32[21,32,128]{2,1,0:T(8,128)S(1)}, u32[]{:S(2)}, u32[]{:S(2)}) collective-permute-start(f32[21,32,128]{2,1,0:T(8,128)S(1)} %collective-permute-done.14.rest_7_), channel_id=1, source_target_pairs={{0,1},{1,0},{2,3},{3,2},{4,5},{5,4},{6,7},{7,6},{8,9},{9,8},{10,11... | collective-permute-start | bytes 1032200 | tf_op jit(solution)/shard_map/ppermute | solution.py:372
  72.3 14.7 %collective-permute-start.18 = (f32[21,32,128]{2,1,0:T(8,128)S(1)}, f32[21,32,128]{2,1,0:T(8,128)S(1)}, u32[]{:S(2)}, u32[]{:S(2)}) collective-permute-start(f32[21,32,128]{2,1,0:T(8,128)S(1)} %collective-permute-done.15.rest_8_), channel_id=1, source_target_pairs={{0,1},{1,0},{2,3},{3,2},{4,5},{5,4},{6,7},{7,6},{8,9},{9,8},{10,11... | collective-permute-start | bytes 1032200 | tf_op jit(solution)/shard_map/ppermute | solution.py:372
  72.7 3.5 %collective-permute-start.8 = (f32[2,32,128]{2,1,0:T(8,128)S(1)}, f32[2,32,128]{2,1,0:T(8,128)S(1)}, u32[]{:S(2)}, u32[]{:S(2)}) collective-permute-start(f32[2,32,128]{2,1,0:T(8,128)S(1)} %get-tuple-element.36.rest_0_), channel_id=1, source_target_pairs={{0,1},{1,0},{2,3},{3,2},{4,5},{5,4},{6,7},{7,6},{8,9},{9,8},{10,11... | collective-permute-start | bytes 98312 | tf_op jit(solution)/shard_map/ppermute | solution.py:372
  76.1 6.4 %collective-permute-start.9 = (f32[4,32,128]{2,1,0:T(8,128)S(1)}, f32[4,32,128]{2,1,0:T(8,128)S(1)}, u32[]{:S(2)}, u32[]{:S(2)}) collective-permute-start(f32[4,32,128]{2,1,0:T(8,128)S(1)} %constant_dynamic-update-slice_fusion.2), channel_id=1, source_target_pairs={{0,2},{1,7},{2,4},{3,1},{4,6},{5,3},{6,0},{7,5},{8,10},{9,15},{10,... | collective-permute-start | bytes 196616 | tf_op jit(solution)/shard_map/ppermute | solution.py:369
  77.8 9.2 %collective-permute-start.11 = (f32[4,32,128]{2,1,0:T(8,128)S(1)}, f32[4,32,128]{2,1,0:T(8,128)S(1)}, u32[]{:S(2)}, u32[]{:S(2)}) collective-permute-start(f32[4,32,128]{2,1,0:T(8,128)S(1)} %constant_dynamic-update-slice_fusion.2), channel_id=1, source_target_pairs={{0,4},{1,5},{2,6},{3,7},{4,0},{5,1},{6,2},{7,3},{8,12},{9,13},{10,... | collective-permute-start | bytes 196616 | tf_op jit(solution)/shard_map/ppermute | solution.py:400
  82.5 4.5 %collective-permute-start.10 = (f32[4,32,128]{2,1,0:T(8,128)S(1)}, f32[4,32,128]{2,1,0:T(8,128)S(1)}, u32[]{:S(2)}, u32[]{:S(2)}) collective-permute-start(f32[4,32,128]{2,1,0:T(8,128)S(1)} %collective-permute-done.9.rest_2_), channel_id=1, source_target_pairs={{0,1},{1,0},{2,3},{3,2},{4,5},{5,4},{6,7},{7,6},{8,9},{9,8},{10,11... | collective-permute-start | bytes 196616 | tf_op jit(solution)/shard_map/ppermute | solution.py:372

commit v3 on v2

--- a/solution.py
+++ b/solution.py
@@ -272,12 +272,12 @@
     below[...] = jnp.zeros(below.shape, jnp.float32)
     for p in range(planes):
         x = [smooth[p, g * SUB : (g + 1) * SUB] for g in range(groups)]
-        below[0, p : p + 1] = x[0][:1] * 0.25
-        above[0, p : p + 1] = x[-1][SUB - 1 :] * 0.25
+        below[0, p : p + 1] = x[0][:1] * 0.0625
+        above[0, p : p + 1] = x[-1][SUB - 1 :] * 0.0625
         for g in range(groups):
             prior = jnp.where(last, x[g - 1] if g else zero, x[g])
             later = jnp.where(first, x[g + 1] if g < groups - 1 else zero, x[g])
-            y = (pltpu.roll(prior, 1, 0) + 2.0 * x[g] + pltpu.roll(later, SUB - 1, 0)) * 0.25
+            y = (pltpu.roll(prior, 1, 0) + 2.0 * x[g] + pltpu.roll(later, SUB - 1, 0)) * 0.0625
             smooth[p, g * SUB : (g + 1) * SUB] = y
 
 
@@ -335,7 +335,7 @@
             x = strip[step + 1, p, r]
             prior = pltpu.roll(jnp.where(last, strip[step, p, r], x), 1, 1)
             later = pltpu.roll(jnp.where(first, strip[step + 2, p, r], x), LANES - 1, 1)
-            return (prior + 2.0 * x + later) * 0.25
+            return prior + 2.0 * x + later
 
         for b in range(bands):
             iso, vol, geo = smooth(b), smooth(bands + b), smooth(2 * bands + b)

time: 93.8 us -> 93.7 us (level)
  no operation moved by 1% of the time
where the time goes in v3:
time: 93.7 us; the launch traced here: 92.1 us
  starting transfers between devices  46.9 us (50%)
  waiting for transfers between devices  33.8 us (36%)
  Pallas kernels  11.2 us (12%)
    ppermute x7, waiting for transfers between devices, onward(): return lax.ppermute(x, 'dates', pairs)  20.3 us
    ppermute x7, starting transfers between devices, onward(): return lax.ppermute(x, 'dates', pairs)  20.1 us
    ppermute x9, starting transfers between devices, swap(): return lax.ppermute(x, 'dates', [(i, i ^ 1) for i in range(devices)])  19.3 us
    ppermute x9, waiting for transfers between devices, swap(): return lax.ppermute(x, 'dates', [(i, i ^ 1) for i in range(devices)])  5.34 us
    pallas_call x1, Pallas kernels, correct(): pl.pallas_call(correct_kernel, grid=(parts,), in_specs=[VMEM] * (3 + len(...  5.12 us
    ppermute x1, waiting for transfers between devices, per_device(): lax.ppermute(halo_both, 'dates', [(i, (i + devices // 2) % devices) for i...  4.47 us
    ppermute x1, starting transfers between devices, per_device(): below = lax.ppermute(below, 'rows', [(i + 1, i) for i in range(blocks - 1)])  3.92 us
    ppermute x1, waiting for transfers between devices, per_device(): above = lax.ppermute(above, 'rows', [(i, i + 1) for i in range(blocks - 1)])  3.61 us
  transfers between devices with their start and end apart: 19, of which 10 were waited for; matrix products, arithmetic and copies ran while one was open for 0% of the time, Pallas kernels for 1%

profile of v3, /device:TPU:28, one launch (start us, length us, event | category | flops | bytes accessed | tf_op | source)
XLA Modules:
  0.0 92.1 jit_solution(16057066491515127508)
XLA Ops:
  0.0 3.2 %far_sums.1 = (f32[1,27,32,128]{3,2,1,0:T(8,128)S(1)}, f32[1,27,32,128]{3,2,1,0:T(8,128)S(1)}, f32[8,4,2,32,128]{4,3,2,1,0:T(8,128)S(1)}, f32[4,7,32,1024]{3,2,1...) custom-call(f32[4,7,32,1024]{3,2,1,0:T(8,128)} %refs_0_.1, ...), custom_call_target="tpu_custom_call" | custom-call | tf_op jit(solution)/shard_map/far_sums/pallas_call | solution.py:216
  3.2 1.3 %shard_map.64 = (f32[3,27,32,128]{3,2,1,0:T(8,128)S(1)}, f32[8,4,2,32,128]{4,3,2,1,0:T(8,128)S(1)}) custom-call(f32[4,7,32,1024]{3,2,1,0:T(8,128)S(1)} %get-tuple-element.20.refl, f32[4,32,1024]{2,1,0:T(8,128)S(1)} %get-tuple-element.21.sun, f32[4,32,1024]{2,1,0:T(8,128)S(1)} %get-tuple-element.22.view, ...), custom_call_target="tpu_custom_call", output_to_operand_aliasing={{1}: (5, {})} | custom-call | tf_op jit(solution)/shard_map/pallas_call | solution.py:230
  4.5 0.1 collective-permute-start
  4.6 0.5 collective-permute-start.3
  5.1 3.2 %collective-permute-done.3 = f32[1,27,32,128]{3,2,1,0:T(8,128)S(1)} collective-permute-done((f32[1,27,32,128]{3,2,1,0:T(8,128)S(1)}, f32[1,27,32,128]{3,2,1,0:T(8,128)S(1)}, u32[]{:S(2)}, u32[]{:S(2)}) %collective-permute-start.3) | collective-permute-done | bytes 442400 | tf_op jit(solution)/shard_map/ppermute | solution.py:372
  8.3 0.1 add_bitcast_fusion
  8.3 3.3 %collective-permute-start.4 = (f32[27,32,128]{2,1,0:T(8,128)S(1)}, f32[27,32,128]{2,1,0:T(8,128)S(1)}, u32[]{:S(2)}, u32[]{:S(2)}) collective-permute-start(f32[27,32,128]{2,1,0:T(8,128)S(1)} %add_bitcast_fusion), channel_id=1, source_target_pairs={{0,2},{1,7},{2,4},{3,1},{4,6},{5,3},{6,0},{7,5},{8,10},{9,15},{10,... | collective-permute-start | bytes 1327112 | tf_op jit(solution)/shard_map/ppermute | solution.py:369
  11.7 1.3 %shard_map.65 = (f32[3,27,32,128]{3,2,1,0:T(8,128)S(1)}, f32[8,4,2,32,128]{4,3,2,1,0:T(8,128)S(1)}) custom-call(f32[4,7,32,1024]{3,2,1,0:T(8,128)S(1)} %get-tuple-element.20.refl, f32[4,32,1024]{2,1,0:T(8,128)S(1)} %get-tuple-element.21.sun, f32[4,32,1024]{2,1,0:T(8,128)S(1)} %get-tuple-element.22.view, ...), custom_call_target="tpu_custom_call", output_to_operand_aliasing={{1}: (5, {})} | custom-call | tf_op jit(solution)/shard_map/pallas_call | solution.py:230
  13.0 0.0 collective-permute-done.own_b
  13.0 0.1 fusion.2
  13.0 4.6 %collective-permute-start.1 = (f32[27,32,128]{2,1,0:T(8,128)S(1)}, f32[27,32,128]{2,1,0:T(8,128)S(1)}, u32[]{:S(2)}, u32[]{:S(2)}) collective-permute-start(f32[27,32,128]{2,1,0:T(8,128)S(1)} %fusion.2), channel_id=1, source_target_pairs={{0,2},{1,7},{2,4},{3,1},{4,6},{5,3},{6,0},{7,5},{8,10},{9,15},{10,... | collective-permute-start | bytes 1327112 | tf_op jit(solution)/shard_map/ppermute | solution.py:369
  17.6 4.9 %collective-permute-done.4 = f32[27,32,128]{2,1,0:T(8,128)S(1)} collective-permute-done((f32[27,32,128]{2,1,0:T(8,128)S(1)}, f32[27,32,128]{2,1,0:T(8,128)S(1)}, u32[]{:S(2)}, u32[]{:S(2)}) %collective-permute-start.4) | collective-permute-done | bytes 442400 | tf_op jit(solution)/shard_map/ppermute | solution.py:369
  22.5 0.1 fusion.1
  22.6 0.0 copy-start
  22.7 1.7 %collective-permute-start.5 = (f32[27,32,128]{2,1,0:T(8,128)S(1)}, f32[27,32,128]{2,1,0:T(8,128)S(1)}, u32[]{:S(2)}, u32[]{:S(2)}) collective-permute-start(f32[27,32,128]{2,1,0:T(8,128)S(1)} %fusion.1), channel_id=1, source_target_pairs={{0,2},{1,7},{2,4},{3,1},{4,6},{5,3},{6,0},{7,5},{8,10},{9,15},{10,... | collective-permute-start | bytes 1327112 | tf_op jit(solution)/shard_map/ppermute | solution.py:369
  24.3 4.9 %collective-permute-done.1 = f32[27,32,128]{2,1,0:T(8,128)S(1)} collective-permute-done((f32[27,32,128]{2,1,0:T(8,128)S(1)}, f32[27,32,128]{2,1,0:T(8,128)S(1)}, u32[]{:S(2)}, u32[]{:S(2)}) %collective-permute-start.1) | collective-permute-done | bytes 442400 | tf_op jit(solution)/shard_map/ppermute | solution.py:369
  29.3 7.3 %collective-permute-start.2 = (f32[27,32,128]{2,1,0:T(8,128)S(1)}, f32[27,32,128]{2,1,0:T(8,128)S(1)}, u32[]{:S(2)}, u32[]{:S(2)}) collective-permute-start(f32[27,32,128]{2,1,0:T(8,128)S(1)} %collective-permute-done.1), channel_id=1, source_target_pairs={{0,1},{1,0},{2,3},{3,2},{4,5},{5,4},{6,7},{7,6},{8,9},{9,8},{10,11... | collective-permute-start | bytes 1327112 | tf_op jit(solution)/shard_map/ppermute | solution.py:372
  36.6 0.1 collective-permute-done.5.far
  36.7 1.3 %collective-permute-done.2.near = f32[27,32,128]{2,1,0:T(8,128)S(1)} collective-permute-done((f32[27,32,128]{2,1,0:T(8,128)S(1)}, f32[27,32,128]{2,1,0:T(8,128)S(1)}, u32[]{:S(2)}, u32[]{:S(2)}) %collective-permute-start.2) | collective-permute-done | bytes 442400 | tf_op jit(solution)/shard_map/ppermute | solution.py:372
  38.0 0.3 solve.1
  38.3 5.6 %collective-permute-start.13 = (f32[21,32,128]{2,1,0:T(8,128)S(1)}, f32[21,32,128]{2,1,0:T(8,128)S(1)}, u32[]{:S(2)}, u32[]{:S(2)}) collective-permute-start(f32[21,32,128]{2,1,0:T(8,128)S(1)} %get-tuple-element.34.rest_5_), channel_id=1, source_target_pairs={{0,1},{1,0},{2,3},{3,2},{4,5},{5,4},{6,7},{7,6},{8,9},{9,8},{10,11... | collective-permute-start | bytes 1032200 | tf_op jit(solution)/shard_map/ppermute | solution.py:372
  43.9 2.2 %collective-permute-start.12 = (f32[21,32,128]{2,1,0:T(8,128)S(1)}, f32[21,32,128]{2,1,0:T(8,128)S(1)}, u32[]{:S(2)}, u32[]{:S(2)}) collective-permute-start(f32[21,32,128]{2,1,0:T(8,128)S(1)} %get-tuple-element.34.rest_5_), channel_id=1, source_target_pairs={{0,2},{1,7},{2,4},{3,1},{4,6},{5,3},{6,0},{7,5},{8,10},{9,15},{10,... | collective-permute-start | bytes 1032200 | tf_op jit(solution)/shard_map/ppermute | solution.py:369
  46.1 0.0 collective-permute-done.13.rest_9_
  46.1 4.6 %collective-permute-start.14 = (f32[21,32,128]{2,1,0:T(8,128)S(1)}, f32[21,32,128]{2,1,0:T(8,128)S(1)}, u32[]{:S(2)}, u32[]{:S(2)}) collective-permute-start(f32[21,32,128]{2,1,0:T(8,128)S(1)} %collective-permute-done.13.rest_9_), channel_id=1, source_target_pairs={{0,2},{1,7},{2,4},{3,1},{4,6},{5,3},{6,0},{7,5},{8,10},{9,15},{10,... | collective-permute-start | bytes 1032200 | tf_op jit(solution)/shard_map/ppermute | solution.py:369
  50.6 7.2 %collective-permute-done.12.rest_6_ = f32[21,32,128]{2,1,0:T(8,128)S(1)} collective-permute-done((f32[21,32,128]{2,1,0:T(8,128)S(1)}, f32[21,32,128]{2,1,0:T(8,128)S(1)}, u32[]{:S(2)}, u32[]{:S(2)}) %collective-permute-start.12) | collective-permute-done | bytes 344096 | tf_op jit(solution)/shard_map/ppermute | solution.py:369
  57.9 2.1 %collective-permute-start.15 = (f32[21,32,128]{2,1,0:T(8,128)S(1)}, f32[21,32,128]{2,1,0:T(8,128)S(1)}, u32[]{:S(2)}, u32[]{:S(2)}) collective-permute-start(f32[21,32,128]{2,1,0:T(8,128)S(1)} %collective-permute-done.12.rest_6_), channel_id=1, source_target_pairs={{0,2},{1,7},{2,4},{3,1},{4,6},{5,3},{6,0},{7,5},{8,10},{9,15},{10,... | collective-permute-start | bytes 1032200 | tf_op jit(solution)/shard_map/ppermute | solution.py:369
  60.0 1.9 %collective-permute-start.6 = (f32[1,32,128]{2,1,0:T(8,128)S(1)}, f32[1,32,128]{2,1,0:T(8,128)S(1)}, u32[]{:S(2)}, u32[]{:S(2)}) collective-permute-start(f32[1,32,128]{2,1,0:T(8,128)S(1)} %get-tuple-element.32), channel_id=1, source_target_pairs={{0,8},{8,16},{16,24},{24,32},{32,40},{40,48},{48,56},{56,64},{64,7... | collective-permute-start | bytes 49160 | tf_op jit(solution)/shard_map/ppermute | solution.py:394
  61.9 3.9 %collective-permute-start.7 = (f32[1,32,128]{2,1,0:T(8,128)S(1)}, f32[1,32,128]{2,1,0:T(8,128)S(1)}, u32[]{:S(2)}, u32[]{:S(2)}) collective-permute-start(f32[1,32,128]{2,1,0:T(8,128)S(1)} %get-tuple-element.33), channel_id=1, source_target_pairs={{8,0},{16,8},{24,16},{32,24},{40,32},{48,40},{56,48},{64,56},{72,6... | collective-permute-start | bytes 49160 | tf_op jit(solution)/shard_map/ppermute | solution.py:395
  65.8 3.6 %collective-permute-done.6 = f32[1,32,128]{2,1,0:T(8,128)S(1)} collective-permute-done((f32[1,32,128]{2,1,0:T(8,128)S(1)}, f32[1,32,128]{2,1,0:T(8,128)S(1)}, u32[]{:S(2)}, u32[]{:S(2)}) %collective-permute-start.6) | collective-permute-done | bytes 16416 | tf_op jit(solution)/shard_map/ppermute | solution.py:394
  69.5 2.7 %collective-permute-start.16 = (f32[21,32,128]{2,1,0:T(8,128)S(1)}, f32[21,32,128]{2,1,0:T(8,128)S(1)}, u32[]{:S(2)}, u32[]{:S(2)}) collective-permute-start(f32[21,32,128]{2,1,0:T(8,128)S(1)} %collective-permute-done.12.rest_6_), channel_id=1, source_target_pairs={{0,1},{1,0},{2,3},{3,2},{4,5},{5,4},{6,7},{7,6},{8,9},{9,8},{10,11... | collective-permute-start | bytes 1032200 | tf_op jit(solution)/shard_map/ppermute | solution.py:372
  72.1 0.0 collective-permute-done.14.rest_7_
  72.1 0.1 collective-permute-start.17
  72.2 0.0 collective-permute-done.15.rest_8_
  72.3 0.4 collective-permute-start.18
  72.7 0.0 collective-permute-done.7
  72.7 2.6 %collective-permute-start.8 = (f32[2,32,128]{2,1,0:T(8,128)S(1)}, f32[2,32,128]{2,1,0:T(8,128)S(1)}, u32[]{:S(2)}, u32[]{:S(2)}) collective-permute-start(f32[2,32,128]{2,1,0:T(8,128)S(1)} %get-tuple-element.36.rest_0_), channel_id=1, source_target_pairs={{0,1},{1,0},{2,3},{3,2},{4,5},{5,4},{6,7},{7,6},{8,9},{9,8},{10,11... | collective-permute-start | bytes 98312 | tf_op jit(solution)/shard_map/ppermute | solution.py:372
  75.3 0.9 collective-permute-done.8.rest_1_
  76.1 1.6 %collective-permute-start.9 = (f32[4,32,128]{2,1,0:T(8,128)S(1)}, f32[4,32,128]{2,1,0:T(8,128)S(1)}, u32[]{:S(2)}, u32[]{:S(2)}) collective-permute-start(f32[4,32,128]{2,1,0:T(8,128)S(1)} %constant_dynamic-update-slice_fusion.2), channel_id=1, source_target_pairs={{0,2},{1,7},{2,4},{3,1},{4,6},{5,3},{6,0},{7,5},{8,10},{9,15},{10,... | collective-permute-start | bytes 196616 | tf_op jit(solution)/shard_map/ppermute | solution.py:369
  77.8 1.7 %collective-permute-start.11 = (f32[4,32,128]{2,1,0:T(8,128)S(1)}, f32[4,32,128]{2,1,0:T(8,128)S(1)}, u32[]{:S(2)}, u32[]{:S(2)}) collective-permute-start(f32[4,32,128]{2,1,0:T(8,128)S(1)} %constant_dynamic-update-slice_fusion.2), channel_id=1, source_target_pairs={{0,4},{1,5},{2,6},{3,7},{4,0},{5,1},{6,2},{7,3},{8,12},{9,13},{10,... | collective-permute-start | bytes 196616 | tf_op jit(solution)/shard_map/ppermute | solution.py:400
  79.4 3.1 %collective-permute-done.9.rest_2_ = f32[4,32,128]{2,1,0:T(8,128)S(1)} collective-permute-done((f32[4,32,128]{2,1,0:T(8,128)S(1)}, f32[4,32,128]{2,1,0:T(8,128)S(1)}, u32[]{:S(2)}, u32[]{:S(2)}) %collective-permute-start.9) | collective-permute-done | bytes 65568 | tf_op jit(solution)/shard_map/ppermute | solution.py:369
  82.5 0.0 collective-permute-start.10
  82.5 4.5 %collective-permute-done.11.rest_4_ = f32[4,32,128]{2,1,0:T(8,128)S(1)} collective-permute-done((f32[4,32,128]{2,1,0:T(8,128)S(1)}, f32[4,32,128]{2,1,0:T(8,128)S(1)}, u32[]{:S(2)}, u32[]{:S(2)}) %collective-permute-start.11) | collective-permute-done | bytes 65568 | tf_op jit(solution)/shard_map/ppermute | solution.py:400
  87.0 0.0 collective-permute-done.10.rest_3_
  87.0 0.0 collective-permute-done.16.rest_10_
  87.0 0.0 collective-permute-done.17.rest_11_
  87.0 0.0 collective-permute-done.18.rest_12_
  87.0 0.0 copy-done
  87.0 5.1 %correct.1 = f32[4,7,32,1024]{3,2,1,0:T(8,128)} custom-call(f32[4,7,32,1024]{3,2,1,0:T(8,128)S(1)} %get-tuple-element.20.refl, f32[8,4,2,32,128]{4,3,2,1,0:T(8,128)S(1)} %get-tuple-element.27.kernels, f32[32,1024]{1,0:T(8,128)S(1)} %copy-done, f32[2,32,128]{2,1,0:T(8,128)S(1)} %get-tuple-element.36.rest_0_, ...), custom_call_target="tpu_custom_call" | custom-call | tf_op jit(solution)/shard_map/correct/pallas_call | solution.py:351
  (3 shorter events, 0.0 us)
Async XLA Ops:
  4.5 8.5 %collective-permute-start = (f32[3,27,32,128]{3,2,1,0:T(8,128)S(1)}, f32[3,27,32,128]{3,2,1,0:T(8,128)S(1)}, u32[]{:S(2)}, u32[]{:S(2)}) collective-permute-start(f32[3,27,32,128]{3,2,1,0:T(8,128)S(1)} %get-tuple-element.29), channel_id=1, source_target_pairs={{0,1},{1,0},{2,3},{3,2},{4,5},{5,4},{6,7},{7,6},{8,9},{9,8},{10,11... | collective-permute-start | bytes 3981320 | tf_op jit(solution)/shard_map/ppermute | solution.py:372
  4.6 3.7 %collective-permute-start.3 = (f32[1,27,32,128]{3,2,1,0:T(8,128)S(1)}, f32[1,27,32,128]{3,2,1,0:T(8,128)S(1)}, u32[]{:S(2)}, u32[]{:S(2)}) collective-permute-start(f32[1,27,32,128]{3,2,1,0:T(8,128)S(1)} %get-tuple-element.31), channel_id=1, source_target_pairs={{0,1},{1,0},{2,3},{3,2},{4,5},{5,4},{6,7},{7,6},{8,9},{9,8},{10,11... | collective-permute-start | bytes 1327112 | tf_op jit(solution)/shard_map/ppermute | solution.py:372
  8.3 14.2 %collective-permute-start.4 = (f32[27,32,128]{2,1,0:T(8,128)S(1)}, f32[27,32,128]{2,1,0:T(8,128)S(1)}, u32[]{:S(2)}, u32[]{:S(2)}) collective-permute-start(f32[27,32,128]{2,1,0:T(8,128)S(1)} %add_bitcast_fusion), channel_id=1, source_target_pairs={{0,2},{1,7},{2,4},{3,1},{4,6},{5,3},{6,0},{7,5},{8,10},{9,15},{10,... | collective-permute-start | bytes 1327112 | tf_op jit(solution)/shard_map/ppermute | solution.py:369
  13.0 16.2 %collective-permute-start.1 = (f32[27,32,128]{2,1,0:T(8,128)S(1)}, f32[27,32,128]{2,1,0:T(8,128)S(1)}, u32[]{:S(2)}, u32[]{:S(2)}) collective-permute-start(f32[27,32,128]{2,1,0:T(8,128)S(1)} %fusion.2), channel_id=1, source_target_pairs={{0,2},{1,7},{2,4},{3,1},{4,6},{5,3},{6,0},{7,5},{8,10},{9,15},{10,... | collective-permute-start | bytes 1327112 | tf_op jit(solution)/shard_map/ppermute | solution.py:369
  22.6 64.4 %copy-start = (f32[32,1024]{1,0:T(8,128)S(1)}, f32[32,1024]{1,0:T(8,128)}, u32[]{:S(2)}) copy-start(f32[32,1024]{1,0:T(8,128)} %nadir.1) | copy-start | bytes 393220
  22.7 14.0 %collective-permute-start.5 = (f32[27,32,128]{2,1,0:T(8,128)S(1)}, f32[27,32,128]{2,1,0:T(8,128)S(1)}, u32[]{:S(2)}, u32[]{:S(2)}) collective-permute-start(f32[27,32,128]{2,1,0:T(8,128)S(1)} %fusion.1), channel_id=1, source_target_pairs={{0,2},{1,7},{2,4},{3,1},{4,6},{5,3},{6,0},{7,5},{8,10},{9,15},{10,... | collective-permute-start | bytes 1327112 | tf_op jit(solution)/shard_map/ppermute | solution.py:369
  29.3 8.7 %collective-permute-start.2 = (f32[27,32,128]{2,1,0:T(8,128)S(1)}, f32[27,32,128]{2,1,0:T(8,128)S(1)}, u32[]{:S(2)}, u32[]{:S(2)}) collective-permute-start(f32[27,32,128]{2,1,0:T(8,128)S(1)} %collective-permute-done.1), channel_id=1, source_target_pairs={{0,1},{1,0},{2,3},{3,2},{4,5},{5,4},{6,7},{7,6},{8,9},{9,8},{10,11... | collective-permute-start | bytes 1327112 | tf_op jit(solution)/shard_map/ppermute | solution.py:372
  38.3 7.8 %collective-permute-start.13 = (f32[21,32,128]{2,1,0:T(8,128)S(1)}, f32[21,32,128]{2,1,0:T(8,128)S(1)}, u32[]{:S(2)}, u32[]{:S(2)}) collective-permute-start(f32[21,32,128]{2,1,0:T(8,128)S(1)} %get-tuple-element.34.rest_5_), channel_id=1, source_target_pairs={{0,1},{1,0},{2,3},{3,2},{4,5},{5,4},{6,7},{7,6},{8,9},{9,8},{10,11... | collective-permute-start | bytes 1032200 | tf_op jit(solution)/shard_map/ppermute | solution.py:372
  43.9 14.0 %collective-permute-start.12 = (f32[21,32,128]{2,1,0:T(8,128)S(1)}, f32[21,32,128]{2,1,0:T(8,128)S(1)}, u32[]{:S(2)}, u32[]{:S(2)}) collective-permute-start(f32[21,32,128]{2,1,0:T(8,128)S(1)} %get-tuple-element.34.rest_5_), channel_id=1, source_target_pairs={{0,2},{1,7},{2,4},{3,1},{4,6},{5,3},{6,0},{7,5},{8,10},{9,15},{10,... | collective-permute-start | bytes 1032200 | tf_op jit(solution)/shard_map/ppermute | solution.py:369
  46.1 26.1 %collective-permute-start.14 = (f32[21,32,128]{2,1,0:T(8,128)S(1)}, f32[21,32,128]{2,1,0:T(8,128)S(1)}, u32[]{:S(2)}, u32[]{:S(2)}) collective-permute-start(f32[21,32,128]{2,1,0:T(8,128)S(1)} %collective-permute-done.13.rest_9_), channel_id=1, source_target_pairs={{0,2},{1,7},{2,4},{3,1},{4,6},{5,3},{6,0},{7,5},{8,10},{9,15},{10,... | collective-permute-start | bytes 1032200 | tf_op jit(solution)/shard_map/ppermute | solution.py:369
  57.9 14.4 %collective-permute-start.15 = (f32[21,32,128]{2,1,0:T(8,128)S(1)}, f32[21,32,128]{2,1,0:T(8,128)S(1)}, u32[]{:S(2)}, u32[]{:S(2)}) collective-permute-start(f32[21,32,128]{2,1,0:T(8,128)S(1)} %collective-permute-done.12.rest_6_), channel_id=1, source_target_pairs={{0,2},{1,7},{2,4},{3,1},{4,6},{5,3},{6,0},{7,5},{8,10},{9,15},{10,... | collective-permute-start | bytes 1032200 | tf_op jit(solution)/shard_map/ppermute | solution.py:369
  60.0 9.5 %collective-permute-start.6 = (f32[1,32,128]{2,1,0:T(8,128)S(1)}, f32[1,32,128]{2,1,0:T(8,128)S(1)}, u32[]{:S(2)}, u32[]{:S(2)}) collective-permute-start(f32[1,32,128]{2,1,0:T(8,128)S(1)} %get-tuple-element.32), channel_id=1, source_target_pairs={{0,8},{8,16},{16,24},{24,32},{32,40},{40,48},{48,56},{56,64},{64,7... | collective-permute-start | bytes 49160 | tf_op jit(solution)/shard_map/ppermute | solution.py:394
  61.9 10.7 %collective-permute-start.7 = (f32[1,32,128]{2,1,0:T(8,128)S(1)}, f32[1,32,128]{2,1,0:T(8,128)S(1)}, u32[]{:S(2)}, u32[]{:S(2)}) collective-permute-start(f32[1,32,128]{2,1,0:T(8,128)S(1)} %get-tuple-element.33), channel_id=1, source_target_pairs={{8,0},{16,8},{24,16},{32,24},{40,32},{48,40},{56,48},{64,56},{72,6... | collective-permute-start | bytes 49160 | tf_op jit(solution)/shard_map/ppermute | solution.py:395
  69.5 17.5 %collective-permute-start.16 = (f32[21,32,128]{2,1,0:T(8,128)S(1)}, f32[21,32,128]{2,1,0:T(8,128)S(1)}, u32[]{:S(2)}, u32[]{:S(2)}) collective-permute-start(f32[21,32,128]{2,1,0:T(8,128)S(1)} %collective-permute-done.12.rest_6_), channel_id=1, source_target_pairs={{0,1},{1,0},{2,3},{3,2},{4,5},{5,4},{6,7},{7,6},{8,9},{9,8},{10,11... | collective-permute-start | bytes 1032200 | tf_op jit(solution)/shard_map/ppermute | solution.py:372
  72.1 14.9 %collective-permute-start.17 = (f32[21,32,128]{2,1,0:T(8,128)S(1)}, f32[21,32,128]{2,1,0:T(8,128)S(1)}, u32[]{:S(2)}, u32[]{:S(2)}) collective-permute-start(f32[21,32,128]{2,1,0:T(8,128)S(1)} %collective-permute-done.14.rest_7_), channel_id=1, source_target_pairs={{0,1},{1,0},{2,3},{3,2},{4,5},{5,4},{6,7},{7,6},{8,9},{9,8},{10,11... | collective-permute-start | bytes 1032200 | tf_op jit(solution)/shard_map/ppermute | solution.py:372
  72.3 14.7 %collective-permute-start.18 = (f32[21,32,128]{2,1,0:T(8,128)S(1)}, f32[21,32,128]{2,1,0:T(8,128)S(1)}, u32[]{:S(2)}, u32[]{:S(2)}) collective-permute-start(f32[21,32,128]{2,1,0:T(8,128)S(1)} %collective-permute-done.15.rest_8_), channel_id=1, source_target_pairs={{0,1},{1,0},{2,3},{3,2},{4,5},{5,4},{6,7},{7,6},{8,9},{9,8},{10,11... | collective-permute-start | bytes 1032200 | tf_op jit(solution)/shard_map/ppermute | solution.py:372
  72.7 3.5 %collective-permute-start.8 = (f32[2,32,128]{2,1,0:T(8,128)S(1)}, f32[2,32,128]{2,1,0:T(8,128)S(1)}, u32[]{:S(2)}, u32[]{:S(2)}) collective-permute-start(f32[2,32,128]{2,1,0:T(8,128)S(1)} %get-tuple-element.36.rest_0_), channel_id=1, source_target_pairs={{0,1},{1,0},{2,3},{3,2},{4,5},{5,4},{6,7},{7,6},{8,9},{9,8},{10,11... | collective-permute-start | bytes 98312 | tf_op jit(solution)/shard_map/ppermute | solution.py:372
  76.1 6.4 %collective-permute-start.9 = (f32[4,32,128]{2,1,0:T(8,128)S(1)}, f32[4,32,128]{2,1,0:T(8,128)S(1)}, u32[]{:S(2)}, u32[]{:S(2)}) collective-permute-start(f32[4,32,128]{2,1,0:T(8,128)S(1)} %constant_dynamic-update-slice_fusion.2), channel_id=1, source_target_pairs={{0,2},{1,7},{2,4},{3,1},{4,6},{5,3},{6,0},{7,5},{8,10},{9,15},{10,... | collective-permute-start | bytes 196616 | tf_op jit(solution)/shard_map/ppermute | solution.py:369
  77.8 9.2 %collective-permute-start.11 = (f32[4,32,128]{2,1,0:T(8,128)S(1)}, f32[4,32,128]{2,1,0:T(8,128)S(1)}, u32[]{:S(2)}, u32[]{:S(2)}) collective-permute-start(f32[4,32,128]{2,1,0:T(8,128)S(1)} %constant_dynamic-update-slice_fusion.2), channel_id=1, source_target_pairs={{0,4},{1,5},{2,6},{3,7},{4,0},{5,1},{6,2},{7,3},{8,12},{9,13},{10,... | collective-permute-start | bytes 196616 | tf_op jit(solution)/shard_map/ppermute | solution.py:400
  82.5 4.5 %collective-permute-start.10 = (f32[4,32,128]{2,1,0:T(8,128)S(1)}, f32[4,32,128]{2,1,0:T(8,128)S(1)}, u32[]{:S(2)}, u32[]{:S(2)}) collective-permute-start(f32[4,32,128]{2,1,0:T(8,128)S(1)} %collective-permute-done.9.rest_2_), channel_id=1, source_target_pairs={{0,1},{1,0},{2,3},{3,2},{4,5},{5,4},{6,7},{7,6},{8,9},{9,8},{10,11... | collective-permute-start | bytes 196616 | tf_op jit(solution)/shard_map/ppermute | solution.py:372

commit v4 on v3

--- a/solution.py
+++ b/solution.py
@@ -237,8 +237,8 @@
     )(*inputs, kernels)
 
 
-def solve_kernel(own_a, own_b, near, far, smooth, above, below):
-    planes, rows, _ = smooth.shape
+def solve_kernel(own_a, own_b, near, far, smooth):
+    planes, rows = smooth.shape[0] - 2, smooth.shape[1]
     bands = planes // 3
     groups = rows // SUB
     for g in range(groups):
@@ -268,12 +268,13 @@
     row = lax.broadcasted_iota(jnp.int32, (SUB, LANES), 0)
     first, last = row == 0, row == SUB - 1
     zero = jnp.zeros((SUB, LANES), jnp.float32)
-    above[...] = jnp.zeros(above.shape, jnp.float32)
-    below[...] = jnp.zeros(below.shape, jnp.float32)
+    smooth[planes:] = jnp.zeros((2,) + smooth.shape[1:], jnp.float32)
+    up = ring_place()[1] == 0
     for p in range(planes):
         x = [smooth[p, g * SUB : (g + 1) * SUB] for g in range(groups)]
-        below[0, p : p + 1] = x[0][:1] * 0.0625
-        above[0, p : p + 1] = x[-1][SUB - 1 :] * 0.0625
+        low, high = x[0][:1] * 0.0625, x[-1][SUB - 1 :] * 0.0625
+        smooth[planes, p : p + 1] = jnp.where(up, high, low)
+        smooth[planes + 1, p : p + 1] = jnp.where(up, low, high)
         for g in range(groups):
             prior = jnp.where(last, x[g - 1] if g else zero, x[g])
             later = jnp.where(first, x[g + 1] if g < groups - 1 else zero, x[g])
@@ -283,19 +284,18 @@
 
 def solve(own_a, own_b, near, far, bands):
     rows = own_a.shape[2]
-    shape = lambda *dims: jax.ShapeDtypeStruct(dims, jnp.float32)
     return pl.pallas_call(
         solve_kernel,
         in_specs=[VMEM] * 4,
-        out_specs=[VMEM] * 3,
-        out_shape=[shape(3 * bands, rows, LANES)] + [shape(1, rows, LANES)] * 2,
+        out_specs=VMEM,
+        out_shape=jax.ShapeDtypeStruct((3 * bands + 2, rows, LANES), jnp.float32),
         compiler_params=pltpu.CompilerParams(vmem_limit_bytes=16 << 20),
         name="solve",
     )(own_a, own_b, near, far)
 
 
 def correct_kernel(refl, kernels, nadir, *rest):
-    (halos, pieces), (out, strip) = (rest[:5], rest[5:-2]), rest[-2:]
+    (halo, *ends, beyond), pieces, (out, strip) = rest[:4], rest[4:-2], rest[-2:]
     step = pl.program_id(0)
     parts = pl.num_programs(0)
     dates, bands, rows, _ = out.shape
@@ -306,23 +306,26 @@
         strip[0] = jnp.zeros(strip.shape[1:], jnp.float32)
         strip[parts + 1] = jnp.zeros(strip.shape[1:], jnp.float32)
         place, core, way = ring_place()
-        own, partner, behind, ahead, beyond = halos
-        for (by, flip), piece, (halo, at) in zip(
+        for (by, flip), piece, (source, at, sent_by) in zip(
             (
                 (0, 0), (-way, 0), (-way, 1), (-2 * way, 0),
                 (0, 1), (way, 1), (way, 0), (2 * way, 1),
             ),
             pieces,
             (
-                (own, 0), (behind, 0), (behind, 2), (beyond, 0),
-                (partner, 0), (ahead, 0), (ahead, 2), (beyond, 2),
+                (halo, (0, 3), core), (ends[0], (0, 3), core),
+                (ends[0], (1, 2), core), (beyond, (0, 3), core),
+                (halo, (1, 2), core), (ends[1], (0, 3), 1 - core),
+                (ends[1], (1, 2), 1 - core), (beyond, (1, 2), core),
             ),
         ):
             spot = part_at(place + by, 1 - core if flip else core, ring) + 1
+            top = jnp.where(sent_by == 0, at[0], at[1])
+            bottom = jnp.where(sent_by == 0, at[1], at[0])
             for p in range(planes):
                 strip[spot, p] = piece[p]
-                strip[spot, p, :1] += halo[at, p : p + 1]
-                strip[spot, p, rows - 1 :] += halo[at + 1, p : p + 1]
+                strip[spot, p, :1] += source[top, p : p + 1]
+                strip[spot, p, rows - 1 :] += source[bottom, p : p + 1]
 
     lanes = lanes_of(step)
     lane = lax.broadcasted_iota(jnp.int32, (SUB, LANES), 1)
@@ -381,26 +384,30 @@
     near = onward(mine[2] + other[2])
     far = onward(mine[1] + other[1] + far)
     near = swap(near)
-    own, above, below = solve(mine, other, near, far, bands)
-
-    behind = onward(own)
+    planes = 3 * bands
+    own = solve(mine, other, near, far, bands)
+
+    behind = onward(own[:planes])
     partner = swap(own)
-    behind_partner = onward(partner)
+    behind_partner = onward(partner[:planes])
+    blocks = lax.axis_size("rows")
+    pairs = []
+    for r in range(blocks):
+        for d in range(devices):
+            to = r + 1 - 2 * (d % 2)
+            if 0 <= to < blocks:
+                pairs.append((r * devices + d, to * devices + d))
+    edges = jnp.concatenate([own[planes : planes + 1], partner[planes + 1 :]], 0)
+    edges = lax.ppermute(edges, ("rows", "dates"), pairs)
+    halo = jnp.concatenate([edges, swap(edges)], 0)
     relayed = onward(behind)
+    halo_behind = onward(halo)
+    halo_far = lax.ppermute(
+        halo, "dates", [(i, (i + devices // 2) % devices) for i in range(devices)]
+    )
     pieces = (own, behind, behind_partner, relayed, partner)
     pieces += (swap(behind), swap(behind_partner), swap(relayed))
-
-    blocks = lax.axis_size("rows")
-    above = lax.ppermute(above, "rows", [(i, i + 1) for i in range(blocks - 1)])
-    below = lax.ppermute(below, "rows", [(i + 1, i) for i in range(blocks - 1)])
-    halo = jnp.concatenate([above, below], 0)
-    halo_partner = swap(halo)
-    halo_both = jnp.concatenate([halo, halo_partner], 0)
-    halo_behind = onward(halo_both)
-    halo_far = lax.ppermute(
-        halo_both, "dates", [(i, (i + devices // 2) % devices) for i in range(devices)]
-    )
-    halos = (halo, halo_partner, halo_behind, swap(halo_behind), halo_far)
+    halos = (halo, halo_behind, swap(halo_behind), halo_far)
     return correct(held[0], kernels, nadir_sun, halos, pieces)
 
 

time: 93.7 us -> 95.4 us (1.018)
  the two profiles are of different devices: /device:TPU:28 before, /device:TPU:36 now
where the time goes in v4:
time: 95.4 us; the launch traced here: 95.3 us
  waiting for transfers between devices  58.9 us (62%)
  starting transfers between devices  24.7 us (26%)
  Pallas kernels  11.2 us (12%)
    ppermute x7, waiting for transfers between devices, onward(): return lax.ppermute(x, 'dates', pairs)  39 us
    ppermute x7, starting transfers between devices, onward(): return lax.ppermute(x, 'dates', pairs)  16.8 us
    ppermute x1, waiting for transfers between devices, per_device(): edges = lax.ppermute(edges, ('rows', 'dates'), pairs)  11.4 us
    pallas_call x1, Pallas kernels, correct(): pl.pallas_call(correct_kernel, grid=(parts,), in_specs=[VMEM] * (3 + len(...  5.12 us
    ppermute x1, waiting for transfers between devices, per_device(): lax.ppermute(halo, 'dates', [(i, (i + devices // 2) % devices) for i in r...  4.75 us
    ppermute x9, waiting for transfers between devices, swap(): return lax.ppermute(x, 'dates', [(i, i ^ 1) for i in range(devices)])  3.79 us
    ppermute x9, starting transfers between devices, swap(): return lax.ppermute(x, 'dates', [(i, i ^ 1) for i in range(devices)])  3.5 us
    ppermute x1, starting transfers between devices, per_device(): edges = lax.ppermute(edges, ('rows', 'dates'), pairs)  3.48 us
  transfers between devices with their start and end apart: 18, of which 10 were waited for; matrix products, arithmetic and copies ran while one was open for 0% of the time, Pallas kernels for 1%

profile of v4, /device:TPU:36, one launch (start us, length us, event | category | flops | bytes accessed | tf_op | source)
XLA Modules:
  0.0 95.3 jit_solution(4917524952808013501)
XLA Ops:
  0.0 3.2 %far_sums.1 = (f32[1,27,32,128]{3,2,1,0:T(8,128)S(1)}, f32[1,27,32,128]{3,2,1,0:T(8,128)S(1)}, f32[8,4,2,32,128]{4,3,2,1,0:T(8,128)S(1)}, f32[4,7,32,1024]{3,2,1...) custom-call(f32[4,7,32,1024]{3,2,1,0:T(8,128)} %refs_0_.1, ...), custom_call_target="tpu_custom_call" | custom-call | tf_op jit(solution)/shard_map/far_sums/pallas_call | solution.py:216
  3.2 1.3 %shard_map.64 = (f32[3,27,32,128]{3,2,1,0:T(8,128)S(1)}, f32[8,4,2,32,128]{4,3,2,1,0:T(8,128)S(1)}) custom-call(f32[4,7,32,1024]{3,2,1,0:T(8,128)S(1)} %get-tuple-element.17.refl, f32[4,32,1024]{2,1,0:T(8,128)S(1)} %get-tuple-element.18.sun, f32[4,32,1024]{2,1,0:T(8,128)S(1)} %get-tuple-element.19.view, ...), custom_call_target="tpu_custom_call", output_to_operand_aliasing={{1}: (5, {})} | custom-call | tf_op jit(solution)/shard_map/pallas_call | solution.py:230
  4.5 0.1 collective-permute-start
  4.6 0.5 collective-permute-start.3
  5.1 3.2 %collective-permute-done.3 = f32[1,27,32,128]{3,2,1,0:T(8,128)S(1)} collective-permute-done((f32[1,27,32,128]{3,2,1,0:T(8,128)S(1)}, f32[1,27,32,128]{3,2,1,0:T(8,128)S(1)}, u32[]{:S(2)}, u32[]{:S(2)}) %collective-permute-start.3) | collective-permute-done | bytes 442400 | tf_op jit(solution)/shard_map/ppermute | solution.py:375
  8.3 0.1 add_bitcast_fusion
  8.3 3.3 %collective-permute-start.4 = (f32[27,32,128]{2,1,0:T(8,128)S(1)}, f32[27,32,128]{2,1,0:T(8,128)S(1)}, u32[]{:S(2)}, u32[]{:S(2)}) collective-permute-start(f32[27,32,128]{2,1,0:T(8,128)S(1)} %add_bitcast_fusion), channel_id=1, source_target_pairs={{0,2},{1,7},{2,4},{3,1},{4,6},{5,3},{6,0},{7,5},{8,10},{9,15},{10,... | collective-permute-start | bytes 1327112 | tf_op jit(solution)/shard_map/ppermute | solution.py:372
  11.7 1.3 %shard_map.65 = (f32[3,27,32,128]{3,2,1,0:T(8,128)S(1)}, f32[8,4,2,32,128]{4,3,2,1,0:T(8,128)S(1)}) custom-call(f32[4,7,32,1024]{3,2,1,0:T(8,128)S(1)} %get-tuple-element.17.refl, f32[4,32,1024]{2,1,0:T(8,128)S(1)} %get-tuple-element.18.sun, f32[4,32,1024]{2,1,0:T(8,128)S(1)} %get-tuple-element.19.view, ...), custom_call_target="tpu_custom_call", output_to_operand_aliasing={{1}: (5, {})} | custom-call | tf_op jit(solution)/shard_map/pallas_call | solution.py:230
  13.0 0.0 collective-permute-done.own_b
  13.0 0.1 fusion.2
  13.0 3.7 %collective-permute-start.1 = (f32[27,32,128]{2,1,0:T(8,128)S(1)}, f32[27,32,128]{2,1,0:T(8,128)S(1)}, u32[]{:S(2)}, u32[]{:S(2)}) collective-permute-start(f32[27,32,128]{2,1,0:T(8,128)S(1)} %fusion.2), channel_id=1, source_target_pairs={{0,2},{1,7},{2,4},{3,1},{4,6},{5,3},{6,0},{7,5},{8,10},{9,15},{10,... | collective-permute-start | bytes 1327112 | tf_op jit(solution)/shard_map/ppermute | solution.py:372
  16.7 13.7 %collective-permute-done.4 = f32[27,32,128]{2,1,0:T(8,128)S(1)} collective-permute-done((f32[27,32,128]{2,1,0:T(8,128)S(1)}, f32[27,32,128]{2,1,0:T(8,128)S(1)}, u32[]{:S(2)}, u32[]{:S(2)}) %collective-permute-start.4) | collective-permute-done | bytes 442400 | tf_op jit(solution)/shard_map/ppermute | solution.py:372
  30.4 0.1 fusion.1
  30.5 2.2 %collective-permute-start.5 = (f32[27,32,128]{2,1,0:T(8,128)S(1)}, f32[27,32,128]{2,1,0:T(8,128)S(1)}, u32[]{:S(2)}, u32[]{:S(2)}) collective-permute-start(f32[27,32,128]{2,1,0:T(8,128)S(1)} %fusion.1), channel_id=1, source_target_pairs={{0,2},{1,7},{2,4},{3,1},{4,6},{5,3},{6,0},{7,5},{8,10},{9,15},{10,... | collective-permute-start | bytes 1327112 | tf_op jit(solution)/shard_map/ppermute | solution.py:372
  32.7 6.3 %collective-permute-done.1 = f32[27,32,128]{2,1,0:T(8,128)S(1)} collective-permute-done((f32[27,32,128]{2,1,0:T(8,128)S(1)}, f32[27,32,128]{2,1,0:T(8,128)S(1)}, u32[]{:S(2)}, u32[]{:S(2)}) %collective-permute-start.1) | collective-permute-done | bytes 442400 | tf_op jit(solution)/shard_map/ppermute | solution.py:372
  39.0 0.0 collective-permute-start.2
  39.0 4.7 %collective-permute-done.5.far = f32[27,32,128]{2,1,0:T(8,128)S(1)} collective-permute-done((f32[27,32,128]{2,1,0:T(8,128)S(1)}, f32[27,32,128]{2,1,0:T(8,128)S(1)}, u32[]{:S(2)}, u32[]{:S(2)}) %collective-permute-start.5) | collective-permute-done | bytes 442400 | tf_op jit(solution)/shard_map/ppermute | solution.py:372
  43.8 0.0 collective-permute-done.2.near
  43.8 0.3 solve.1.rest_4_
  44.1 0.0 copy-start
  44.1 0.1 collective-permute-start.6
  44.2 0.4 collective-permute-start.12
  44.6 11.7 %collective-permute-done.12.rest_5_ = f32[21,32,128]{2,1,0:T(8,128)S(1)} collective-permute-done((f32[21,32,128]{2,1,0:T(8,128)S(1)}, f32[21,32,128]{2,1,0:T(8,128)S(1)}, u32[]{:S(2)}, u32[]{:S(2)}) %collective-permute-start.12) | collective-permute-done | bytes 344096 | tf_op jit(solution)/shard_map/ppermute | solution.py:372
  56.4 0.2 collective-permute-start.14
  56.6 0.0 collective-permute-done.6.rest_8_
  56.6 2.4 %collective-permute-start.13 = (f32[21,32,128]{2,1,0:T(8,128)S(1)}, f32[21,32,128]{2,1,0:T(8,128)S(1)}, u32[]{:S(2)}, u32[]{:S(2)}) collective-permute-start(f32[21,32,128]{2,1,0:T(8,128)S(1)} %slice.37), channel_id=1, source_target_pairs={{0,2},{1,7},{2,4},{3,1},{4,6},{5,3},{6,0},{7,5},{8,10},{9,15},{10,... | collective-permute-start | bytes 1032200 | tf_op jit(solution)/shard_map/ppermute | solution.py:372
  59.1 3.5 %collective-permute-start.7 = (f32[2,32,128]{2,1,0:T(8,128)S(1)}, f32[2,32,128]{2,1,0:T(8,128)S(1)}, u32[]{:S(2)}, u32[]{:S(2)}) collective-permute-start(f32[2,32,128]{2,1,0:T(8,128)S(1)} %pad_maximum_fusion), channel_id=1, source_target_pairs={{0,8},{2,10},{4,12},{6,14},{8,16},{9,1},{10,18},{11,3},{12,20},{13... | collective-permute-start | bytes 98312 | tf_op jit(solution)/shard_map/ppermute | solution.py:401
  62.5 2.3 %collective-permute-start.15 = (f32[21,32,128]{2,1,0:T(8,128)S(1)}, f32[21,32,128]{2,1,0:T(8,128)S(1)}, u32[]{:S(2)}, u32[]{:S(2)}) collective-permute-start(f32[21,32,128]{2,1,0:T(8,128)S(1)} %collective-permute-done.12.rest_5_), channel_id=1, source_target_pairs={{0,1},{1,0},{2,3},{3,2},{4,5},{5,4},{6,7},{7,6},{8,9},{9,8},{10,11... | collective-permute-start | bytes 1032200 | tf_op jit(solution)/shard_map/ppermute | solution.py:375
  64.8 11.4 %collective-permute-done.7 = f32[2,32,128]{2,1,0:T(8,128)S(1)} collective-permute-done((f32[2,32,128]{2,1,0:T(8,128)S(1)}, f32[2,32,128]{2,1,0:T(8,128)S(1)}, u32[]{:S(2)}, u32[]{:S(2)}) %collective-permute-start.7) | collective-permute-done | bytes 32800 | tf_op jit(solution)/shard_map/ppermute | solution.py:401
  76.2 0.0 collective-permute-start.8
  76.2 0.0 collective-permute-done.14.rest_7_
  76.2 0.5 collective-permute-start.17
  76.7 0.1 collective-permute-done.13.rest_6_
  76.8 0.0 collective-permute-start.16
  76.8 0.6 collective-permute-done.8
  77.4 4.5 %collective-permute-start.9 = (f32[4,32,128]{2,1,0:T(8,128)S(1)}, f32[4,32,128]{2,1,0:T(8,128)S(1)}, u32[]{:S(2)}, u32[]{:S(2)}) collective-permute-start(f32[4,32,128]{2,1,0:T(8,128)S(1)} %constant_dynamic-update-slice_fusion.rest_0_), channel_id=1, source_target_pairs={{0,2},{1,7},{2,4},{3,1},{4,6},{5,3},{6,0},{7,5},{8,10},{9,15},{10,... | collective-permute-start | bytes 196616 | tf_op jit(solution)/shard_map/ppermute | solution.py:372
  81.9 1.0 %collective-permute-start.11 = (f32[4,32,128]{2,1,0:T(8,128)S(1)}, f32[4,32,128]{2,1,0:T(8,128)S(1)}, u32[]{:S(2)}, u32[]{:S(2)}) collective-permute-start(f32[4,32,128]{2,1,0:T(8,128)S(1)} %constant_dynamic-update-slice_fusion.rest_0_), channel_id=1, source_target_pairs={{0,4},{1,5},{2,6},{3,7},{4,0},{5,1},{6,2},{7,3},{8,12},{9,13},{10,... | collective-permute-start | bytes 196616 | tf_op jit(solution)/shard_map/ppermute | solution.py:405
  82.9 2.5 %collective-permute-done.9.rest_1_ = f32[4,32,128]{2,1,0:T(8,128)S(1)} collective-permute-done((f32[4,32,128]{2,1,0:T(8,128)S(1)}, f32[4,32,128]{2,1,0:T(8,128)S(1)}, u32[]{:S(2)}, u32[]{:S(2)}) %collective-permute-start.9) | collective-permute-done | bytes 65568 | tf_op jit(solution)/shard_map/ppermute | solution.py:372
  85.4 0.0 collective-permute-start.10
  85.4 4.8 %collective-permute-done.11.rest_3_ = f32[4,32,128]{2,1,0:T(8,128)S(1)} collective-permute-done((f32[4,32,128]{2,1,0:T(8,128)S(1)}, f32[4,32,128]{2,1,0:T(8,128)S(1)}, u32[]{:S(2)}, u32[]{:S(2)}) %collective-permute-start.11) | collective-permute-done | bytes 65568 | tf_op jit(solution)/shard_map/ppermute | solution.py:405
  90.1 0.0 collective-permute-done.10.rest_2_
  90.1 0.0 collective-permute-done.15.rest_9_
  90.1 0.0 collective-permute-done.17.rest_11_
  90.1 0.0 collective-permute-done.16.rest_10_
  90.1 0.0 copy-done
  90.1 5.1 %correct.1 = f32[4,7,32,1024]{3,2,1,0:T(8,128)} custom-call(f32[4,7,32,1024]{3,2,1,0:T(8,128)S(1)} %get-tuple-element.17.refl, f32[8,4,2,32,128]{4,3,2,1,0:T(8,128)S(1)} %get-tuple-element.24.kernels, f32[32,1024]{1,0:T(8,128)S(1)} %copy-done, f32[4,32,128]{2,1,0:T(8,128)S(1)} %constant_dynamic-update-slice_fusion.rest_0_, ...), custom_call_target="tpu_custom_call" | custom-call | tf_op jit(solution)/shard_map/correct/pallas_call | solution.py:354
  (7 shorter events, 0.1 us)
Async XLA Ops:
  4.5 8.5 %collective-permute-start = (f32[3,27,32,128]{3,2,1,0:T(8,128)S(1)}, f32[3,27,32,128]{3,2,1,0:T(8,128)S(1)}, u32[]{:S(2)}, u32[]{:S(2)}) collective-permute-start(f32[3,27,32,128]{3,2,1,0:T(8,128)S(1)} %get-tuple-element.26), channel_id=1, source_target_pairs={{0,1},{1,0},{2,3},{3,2},{4,5},{5,4},{6,7},{7,6},{8,9},{9,8},{10,11... | collective-permute-start | bytes 3981320 | tf_op jit(solution)/shard_map/ppermute | solution.py:375
  4.6 3.7 %collective-permute-start.3 = (f32[1,27,32,128]{3,2,1,0:T(8,128)S(1)}, f32[1,27,32,128]{3,2,1,0:T(8,128)S(1)}, u32[]{:S(2)}, u32[]{:S(2)}) collective-permute-start(f32[1,27,32,128]{3,2,1,0:T(8,128)S(1)} %get-tuple-element.28), channel_id=1, source_target_pairs={{0,1},{1,0},{2,3},{3,2},{4,5},{5,4},{6,7},{7,6},{8,9},{9,8},{10,11... | collective-permute-start | bytes 1327112 | tf_op jit(solution)/shard_map/ppermute | solution.py:375
  8.3 22.0 %collective-permute-start.4 = (f32[27,32,128]{2,1,0:T(8,128)S(1)}, f32[27,32,128]{2,1,0:T(8,128)S(1)}, u32[]{:S(2)}, u32[]{:S(2)}) collective-permute-start(f32[27,32,128]{2,1,0:T(8,128)S(1)} %add_bitcast_fusion), channel_id=1, source_target_pairs={{0,2},{1,7},{2,4},{3,1},{4,6},{5,3},{6,0},{7,5},{8,10},{9,15},{10,... | collective-permute-start | bytes 1327112 | tf_op jit(solution)/shard_map/ppermute | solution.py:372
  13.0 26.0 %collective-permute-start.1 = (f32[27,32,128]{2,1,0:T(8,128)S(1)}, f32[27,32,128]{2,1,0:T(8,128)S(1)}, u32[]{:S(2)}, u32[]{:S(2)}) collective-permute-start(f32[27,32,128]{2,1,0:T(8,128)S(1)} %fusion.2), channel_id=1, source_target_pairs={{0,2},{1,7},{2,4},{3,1},{4,6},{5,3},{6,0},{7,5},{8,10},{9,15},{10,... | collective-permute-start | bytes 1327112 | tf_op jit(solution)/shard_map/ppermute | solution.py:372
  30.5 13.3 %collective-permute-start.5 = (f32[27,32,128]{2,1,0:T(8,128)S(1)}, f32[27,32,128]{2,1,0:T(8,128)S(1)}, u32[]{:S(2)}, u32[]{:S(2)}) collective-permute-start(f32[27,32,128]{2,1,0:T(8,128)S(1)} %fusion.1), channel_id=1, source_target_pairs={{0,2},{1,7},{2,4},{3,1},{4,6},{5,3},{6,0},{7,5},{8,10},{9,15},{10,... | collective-permute-start | bytes 1327112 | tf_op jit(solution)/shard_map/ppermute | solution.py:372
  39.0 4.7 %collective-permute-start.2 = (f32[27,32,128]{2,1,0:T(8,128)S(1)}, f32[27,32,128]{2,1,0:T(8,128)S(1)}, u32[]{:S(2)}, u32[]{:S(2)}) collective-permute-start(f32[27,32,128]{2,1,0:T(8,128)S(1)} %collective-permute-done.1), channel_id=1, source_target_pairs={{0,1},{1,0},{2,3},{3,2},{4,5},{5,4},{6,7},{7,6},{8,9},{9,8},{10,11... | collective-permute-start | bytes 1327112 | tf_op jit(solution)/shard_map/ppermute | solution.py:375
  44.1 46.0 %copy-start = (f32[32,1024]{1,0:T(8,128)S(1)}, f32[32,1024]{1,0:T(8,128)}, u32[]{:S(2)}) copy-start(f32[32,1024]{1,0:T(8,128)} %nadir.1) | copy-start | bytes 393220
  44.1 12.5 %collective-permute-start.6 = (f32[23,32,128]{2,1,0:T(8,128)S(1)}, f32[23,32,128]{2,1,0:T(8,128)S(1)}, u32[]{:S(2)}, u32[]{:S(2)}) collective-permute-start(f32[23,32,128]{2,1,0:T(8,128)S(1)} %solve.1.rest_4_), channel_id=1, source_target_pairs={{0,1},{1,0},{2,3},{3,2},{4,5},{5,4},{6,7},{7,6},{8,9},{9,8},{10,11... | collective-permute-start | bytes 1130504 | tf_op jit(solution)/shard_map/ppermute | solution.py:375
  44.2 12.1 %collective-permute-start.12 = (f32[21,32,128]{2,1,0:T(8,128)S(1)}, f32[21,32,128]{2,1,0:T(8,128)S(1)}, u32[]{:S(2)}, u32[]{:S(2)}) collective-permute-start(f32[21,32,128]{2,1,0:T(8,128)S(1)} %slice.36), channel_id=1, source_target_pairs={{0,2},{1,7},{2,4},{3,1},{4,6},{5,3},{6,0},{7,5},{8,10},{9,15},{10,... | collective-permute-start | bytes 1032200 | tf_op jit(solution)/shard_map/ppermute | solution.py:372
  56.4 19.8 %collective-permute-start.14 = (f32[21,32,128]{2,1,0:T(8,128)S(1)}, f32[21,32,128]{2,1,0:T(8,128)S(1)}, u32[]{:S(2)}, u32[]{:S(2)}) collective-permute-start(f32[21,32,128]{2,1,0:T(8,128)S(1)} %collective-permute-done.12.rest_5_), channel_id=1, source_target_pairs={{0,2},{1,7},{2,4},{3,1},{4,6},{5,3},{6,0},{7,5},{8,10},{9,15},{10,... | collective-permute-start | bytes 1032200 | tf_op jit(solution)/shard_map/ppermute | solution.py:372
  56.6 20.2 %collective-permute-start.13 = (f32[21,32,128]{2,1,0:T(8,128)S(1)}, f32[21,32,128]{2,1,0:T(8,128)S(1)}, u32[]{:S(2)}, u32[]{:S(2)}) collective-permute-start(f32[21,32,128]{2,1,0:T(8,128)S(1)} %slice.37), channel_id=1, source_target_pairs={{0,2},{1,7},{2,4},{3,1},{4,6},{5,3},{6,0},{7,5},{8,10},{9,15},{10,... | collective-permute-start | bytes 1032200 | tf_op jit(solution)/shard_map/ppermute | solution.py:372
  59.1 17.2 %collective-permute-start.7 = (f32[2,32,128]{2,1,0:T(8,128)S(1)}, f32[2,32,128]{2,1,0:T(8,128)S(1)}, u32[]{:S(2)}, u32[]{:S(2)}) collective-permute-start(f32[2,32,128]{2,1,0:T(8,128)S(1)} %pad_maximum_fusion), channel_id=1, source_target_pairs={{0,8},{2,10},{4,12},{6,14},{8,16},{9,1},{10,18},{11,3},{12,20},{13... | collective-permute-start | bytes 98312 | tf_op jit(solution)/shard_map/ppermute | solution.py:401
  62.5 27.6 %collective-permute-start.15 = (f32[21,32,128]{2,1,0:T(8,128)S(1)}, f32[21,32,128]{2,1,0:T(8,128)S(1)}, u32[]{:S(2)}, u32[]{:S(2)}) collective-permute-start(f32[21,32,128]{2,1,0:T(8,128)S(1)} %collective-permute-done.12.rest_5_), channel_id=1, source_target_pairs={{0,1},{1,0},{2,3},{3,2},{4,5},{5,4},{6,7},{7,6},{8,9},{9,8},{10,11... | collective-permute-start | bytes 1032200 | tf_op jit(solution)/shard_map/ppermute | solution.py:375
  76.2 1.2 %collective-permute-start.8 = (f32[2,32,128]{2,1,0:T(8,128)S(1)}, f32[2,32,128]{2,1,0:T(8,128)S(1)}, u32[]{:S(2)}, u32[]{:S(2)}) collective-permute-start(f32[2,32,128]{2,1,0:T(8,128)S(1)} %collective-permute-done.7), channel_id=1, source_target_pairs={{0,1},{1,0},{2,3},{3,2},{4,5},{5,4},{6,7},{7,6},{8,9},{9,8},{10,11... | collective-permute-start | bytes 98312 | tf_op jit(solution)/shard_map/ppermute | solution.py:375
  76.2 13.9 %collective-permute-start.17 = (f32[21,32,128]{2,1,0:T(8,128)S(1)}, f32[21,32,128]{2,1,0:T(8,128)S(1)}, u32[]{:S(2)}, u32[]{:S(2)}) collective-permute-start(f32[21,32,128]{2,1,0:T(8,128)S(1)} %collective-permute-done.14.rest_7_), channel_id=1, source_target_pairs={{0,1},{1,0},{2,3},{3,2},{4,5},{5,4},{6,7},{7,6},{8,9},{9,8},{10,11... | collective-permute-start | bytes 1032200 | tf_op jit(solution)/shard_map/ppermute | solution.py:375
  76.8 13.3 %collective-permute-start.16 = (f32[21,32,128]{2,1,0:T(8,128)S(1)}, f32[21,32,128]{2,1,0:T(8,128)S(1)}, u32[]{:S(2)}, u32[]{:S(2)}) collective-permute-start(f32[21,32,128]{2,1,0:T(8,128)S(1)} %collective-permute-done.13.rest_6_), channel_id=1, source_target_pairs={{0,1},{1,0},{2,3},{3,2},{4,5},{5,4},{6,7},{7,6},{8,9},{9,8},{10,11... | collective-permute-start | bytes 1032200 | tf_op jit(solution)/shard_map/ppermute | solution.py:375
  77.4 7.9 %collective-permute-start.9 = (f32[4,32,128]{2,1,0:T(8,128)S(1)}, f32[4,32,128]{2,1,0:T(8,128)S(1)}, u32[]{:S(2)}, u32[]{:S(2)}) collective-permute-start(f32[4,32,128]{2,1,0:T(8,128)S(1)} %constant_dynamic-update-slice_fusion.rest_0_), channel_id=1, source_target_pairs={{0,2},{1,7},{2,4},{3,1},{4,6},{5,3},{6,0},{7,5},{8,10},{9,15},{10,... | collective-permute-start | bytes 196616 | tf_op jit(solution)/shard_map/ppermute | solution.py:372
  81.9 8.2 %collective-permute-start.11 = (f32[4,32,128]{2,1,0:T(8,128)S(1)}, f32[4,32,128]{2,1,0:T(8,128)S(1)}, u32[]{:S(2)}, u32[]{:S(2)}) collective-permute-start(f32[4,32,128]{2,1,0:T(8,128)S(1)} %constant_dynamic-update-slice_fusion.rest_0_), channel_id=1, source_target_pairs={{0,4},{1,5},{2,6},{3,7},{4,0},{5,1},{6,2},{7,3},{8,12},{9,13},{10,... | collective-permute-start | bytes 196616 | tf_op jit(solution)/shard_map/ppermute | solution.py:405
  85.4 4.8 %collective-permute-start.10 = (f32[4,32,128]{2,1,0:T(8,128)S(1)}, f32[4,32,128]{2,1,0:T(8,128)S(1)}, u32[]{:S(2)}, u32[]{:S(2)}) collective-permute-start(f32[4,32,128]{2,1,0:T(8,128)S(1)} %collective-permute-done.9.rest_1_), channel_id=1, source_target_pairs={{0,1},{1,0},{2,3},{3,2},{4,5},{5,4},{6,7},{7,6},{8,9},{9,8},{10,11... | collective-permute-start | bytes 196616 | tf_op jit(solution)/shard_map/ppermute | solution.py:375

commit v5 on v4

--- a/solution.py
+++ b/solution.py
@@ -295,7 +295,7 @@
 
 
 def correct_kernel(refl, kernels, nadir, *rest):
-    (halo, *ends, beyond), pieces, (out, strip) = rest[:4], rest[4:-2], rest[-2:]
+    (halo, beyond), pieces, (out, strip) = rest[:2], rest[2:-2], rest[-2:]
     step = pl.program_id(0)
     parts = pl.num_programs(0)
     dates, bands, rows, _ = out.shape
@@ -306,6 +306,7 @@
         strip[0] = jnp.zeros(strip.shape[1:], jnp.float32)
         strip[parts + 1] = jnp.zeros(strip.shape[1:], jnp.float32)
         place, core, way = ring_place()
+        ends = (pieces[3], pieces[7])
         for (by, flip), piece, (source, at, sent_by) in zip(
             (
                 (0, 0), (-way, 0), (-way, 1), (-2 * way, 0),
@@ -313,10 +314,10 @@
             ),
             pieces,
             (
-                (halo, (0, 3), core), (ends[0], (0, 3), core),
-                (ends[0], (1, 2), core), (beyond, (0, 3), core),
-                (halo, (1, 2), core), (ends[1], (0, 3), 1 - core),
-                (ends[1], (1, 2), 1 - core), (beyond, (1, 2), core),
+                (halo, (0, 3), core), (ends[0], (planes, planes + 3), core),
+                (ends[0], (planes + 1, planes + 2), core), (beyond, (0, 3), core),
+                (halo, (1, 2), core), (ends[1], (planes, planes + 3), 1 - core),
+                (ends[1], (planes + 1, planes + 2), 1 - core), (beyond, (1, 2), core),
             ),
         ):
             spot = part_at(place + by, 1 - core if flip else core, ring) + 1
@@ -400,15 +401,13 @@
     edges = jnp.concatenate([own[planes : planes + 1], partner[planes + 1 :]], 0)
     edges = lax.ppermute(edges, ("rows", "dates"), pairs)
     halo = jnp.concatenate([edges, swap(edges)], 0)
-    relayed = onward(behind)
-    halo_behind = onward(halo)
+    relayed = onward(jnp.concatenate([behind, halo], 0))
     halo_far = lax.ppermute(
         halo, "dates", [(i, (i + devices // 2) % devices) for i in range(devices)]
     )
     pieces = (own, behind, behind_partner, relayed, partner)
     pieces += (swap(behind), swap(behind_partner), swap(relayed))
-    halos = (halo, halo_behind, swap(halo_behind), halo_far)
-    return correct(held[0], kernels, nadir_sun, halos, pieces)
+    return correct(held[0], kernels, nadir_sun, (halo, halo_far), pieces)
 
 
 def solution(mesh):

time: 95.4 us -> 95.8 us (level)
  the two profiles are of different devices: /device:TPU:36 before, /device:TPU:6 now
where the time goes in v5:
time: 95.8 us
  starting transfers between devices  45.6 us (48%)
  waiting for transfers between devices  38.5 us (40%)
  Pallas kernels  11.2 us (12%)
    ppermute x6, waiting for transfers between devices, onward(): return lax.ppermute(x, 'dates', pairs)  24.1 us
    ppermute x6, starting transfers between devices, onward(): return lax.ppermute(x, 'dates', pairs)  19.2 us
    ppermute x8, starting transfers between devices, swap(): return lax.ppermute(x, 'dates', [(i, i ^ 1) for i in range(devices)])  16.8 us
    ppermute x1, starting transfers between devices, per_device(): lax.ppermute(halo, 'dates', [(i, (i + devices // 2) % devices) for i in r...  6.14 us
    ppermute x1, waiting for transfers between devices, per_device(): edges = lax.ppermute(edges, ('rows', 'dates'), pairs)  5.71 us
    pallas_call x1, Pallas kernels, correct(): pl.pallas_call(correct_kernel, grid=(parts,), in_specs=[VMEM] * (3 + len(...  5.12 us
    ppermute x8, waiting for transfers between devices, swap(): return lax.ppermute(x, 'dates', [(i, i ^ 1) for i in range(devices)])  4.48 us
    ppermute x1, waiting for transfers between devices, per_device(): lax.ppermute(halo, 'dates', [(i, (i + devices // 2) % devices) for i in r...  4.26 us
  transfers between devices with their start and end apart: 16, of which 10 were waited for; matrix products, arithmetic and copies ran while one was open for 0% of the time, Pallas kernels for 1%

profile of v5, /device:TPU:6, one launch (start us, length us, event | category | flops | bytes accessed | tf_op | source)
XLA Modules:
  0.0 95.8 jit_solution(15503497566755615525)
XLA Ops:
  0.0 3.2 %far_sums.1 = (f32[1,27,32,128]{3,2,1,0:T(8,128)S(1)}, f32[1,27,32,128]{3,2,1,0:T(8,128)S(1)}, f32[8,4,2,32,128]{4,3,2,1,0:T(8,128)S(1)}, f32[4,7,32,1024]{3,2,1...) custom-call(f32[4,7,32,1024]{3,2,1,0:T(8,128)} %refs_0_.1, ...), custom_call_target="tpu_custom_call" | custom-call | tf_op jit(solution)/shard_map/far_sums/pallas_call | solution.py:216
  3.2 1.3 %shard_map.64 = (f32[3,27,32,128]{3,2,1,0:T(8,128)S(1)}, f32[8,4,2,32,128]{4,3,2,1,0:T(8,128)S(1)}) custom-call(f32[4,7,32,1024]{3,2,1,0:T(8,128)S(1)} %get-tuple-element.17.refl, f32[4,32,1024]{2,1,0:T(8,128)S(1)} %get-tuple-element.18.sun, f32[4,32,1024]{2,1,0:T(8,128)S(1)} %get-tuple-element.19.view, ...), custom_call_target="tpu_custom_call", output_to_operand_aliasing={{1}: (5, {})} | custom-call | tf_op jit(solution)/shard_map/pallas_call | solution.py:230
  4.5 0.1 collective-permute-start
  4.6 0.5 collective-permute-start.3
  5.1 3.2 %collective-permute-done.3 = f32[1,27,32,128]{3,2,1,0:T(8,128)S(1)} collective-permute-done((f32[1,27,32,128]{3,2,1,0:T(8,128)S(1)}, f32[1,27,32,128]{3,2,1,0:T(8,128)S(1)}, u32[]{:S(2)}, u32[]{:S(2)}) %collective-permute-start.3) | collective-permute-done | bytes 442400 | tf_op jit(solution)/shard_map/ppermute | solution.py:376
  8.3 0.1 add_bitcast_fusion
  8.3 3.3 %collective-permute-start.4 = (f32[27,32,128]{2,1,0:T(8,128)S(1)}, f32[27,32,128]{2,1,0:T(8,128)S(1)}, u32[]{:S(2)}, u32[]{:S(2)}) collective-permute-start(f32[27,32,128]{2,1,0:T(8,128)S(1)} %add_bitcast_fusion), channel_id=1, source_target_pairs={{0,2},{1,7},{2,4},{3,1},{4,6},{5,3},{6,0},{7,5},{8,10},{9,15},{10,... | collective-permute-start | bytes 1327112 | tf_op jit(solution)/shard_map/ppermute | solution.py:373
  11.7 1.3 %shard_map.65 = (f32[3,27,32,128]{3,2,1,0:T(8,128)S(1)}, f32[8,4,2,32,128]{4,3,2,1,0:T(8,128)S(1)}) custom-call(f32[4,7,32,1024]{3,2,1,0:T(8,128)S(1)} %get-tuple-element.17.refl, f32[4,32,1024]{2,1,0:T(8,128)S(1)} %get-tuple-element.18.sun, f32[4,32,1024]{2,1,0:T(8,128)S(1)} %get-tuple-element.19.view, ...), custom_call_target="tpu_custom_call", output_to_operand_aliasing={{1}: (5, {})} | custom-call | tf_op jit(solution)/shard_map/pallas_call | solution.py:230
  13.0 0.0 collective-permute-done.own_b
  13.0 0.1 fusion.2
  13.0 4.6 %collective-permute-start.1 = (f32[27,32,128]{2,1,0:T(8,128)S(1)}, f32[27,32,128]{2,1,0:T(8,128)S(1)}, u32[]{:S(2)}, u32[]{:S(2)}) collective-permute-start(f32[27,32,128]{2,1,0:T(8,128)S(1)} %fusion.2), channel_id=1, source_target_pairs={{0,2},{1,7},{2,4},{3,1},{4,6},{5,3},{6,0},{7,5},{8,10},{9,15},{10,... | collective-permute-start | bytes 1327112 | tf_op jit(solution)/shard_map/ppermute | solution.py:373
  17.6 4.9 %collective-permute-done.4 = f32[27,32,128]{2,1,0:T(8,128)S(1)} collective-permute-done((f32[27,32,128]{2,1,0:T(8,128)S(1)}, f32[27,32,128]{2,1,0:T(8,128)S(1)}, u32[]{:S(2)}, u32[]{:S(2)}) %collective-permute-start.4) | collective-permute-done | bytes 442400 | tf_op jit(solution)/shard_map/ppermute | solution.py:373
  22.5 0.1 fusion.1
  22.6 1.7 %collective-permute-start.5 = (f32[27,32,128]{2,1,0:T(8,128)S(1)}, f32[27,32,128]{2,1,0:T(8,128)S(1)}, u32[]{:S(2)}, u32[]{:S(2)}) collective-permute-start(f32[27,32,128]{2,1,0:T(8,128)S(1)} %fusion.1), channel_id=1, source_target_pairs={{0,2},{1,7},{2,4},{3,1},{4,6},{5,3},{6,0},{7,5},{8,10},{9,15},{10,... | collective-permute-start | bytes 1327112 | tf_op jit(solution)/shard_map/ppermute | solution.py:373
  24.3 4.9 %collective-permute-done.1 = f32[27,32,128]{2,1,0:T(8,128)S(1)} collective-permute-done((f32[27,32,128]{2,1,0:T(8,128)S(1)}, f32[27,32,128]{2,1,0:T(8,128)S(1)}, u32[]{:S(2)}, u32[]{:S(2)}) %collective-permute-start.1) | collective-permute-done | bytes 442400 | tf_op jit(solution)/shard_map/ppermute | solution.py:373
  29.3 7.3 %collective-permute-start.2 = (f32[27,32,128]{2,1,0:T(8,128)S(1)}, f32[27,32,128]{2,1,0:T(8,128)S(1)}, u32[]{:S(2)}, u32[]{:S(2)}) collective-permute-start(f32[27,32,128]{2,1,0:T(8,128)S(1)} %collective-permute-done.1), channel_id=1, source_target_pairs={{0,1},{1,0},{2,3},{3,2},{4,5},{5,4},{6,7},{7,6},{8,9},{9,8},{10,11... | collective-permute-start | bytes 1327112 | tf_op jit(solution)/shard_map/ppermute | solution.py:376
  36.6 0.1 collective-permute-done.5.far
  36.7 1.3 %collective-permute-done.2.near = f32[27,32,128]{2,1,0:T(8,128)S(1)} collective-permute-done((f32[27,32,128]{2,1,0:T(8,128)S(1)}, f32[27,32,128]{2,1,0:T(8,128)S(1)}, u32[]{:S(2)}, u32[]{:S(2)}) %collective-permute-start.2) | collective-permute-done | bytes 442400 | tf_op jit(solution)/shard_map/ppermute | solution.py:376
  38.0 0.3 solve.1.rest_2_
  38.3 0.0 copy-start
  38.3 5.6 %collective-permute-start.6 = (f32[23,32,128]{2,1,0:T(8,128)S(1)}, f32[23,32,128]{2,1,0:T(8,128)S(1)}, u32[]{:S(2)}, u32[]{:S(2)}) collective-permute-start(f32[23,32,128]{2,1,0:T(8,128)S(1)} %solve.1.rest_2_), channel_id=1, source_target_pairs={{0,1},{1,0},{2,3},{3,2},{4,5},{5,4},{6,7},{7,6},{8,9},{9,8},{10,11... | collective-permute-start | bytes 1130504 | tf_op jit(solution)/shard_map/ppermute | solution.py:376
  43.9 2.2 %collective-permute-start.10 = (f32[21,32,128]{2,1,0:T(8,128)S(1)}, f32[21,32,128]{2,1,0:T(8,128)S(1)}, u32[]{:S(2)}, u32[]{:S(2)}) collective-permute-start(f32[21,32,128]{2,1,0:T(8,128)S(1)} %slice.36), channel_id=1, source_target_pairs={{0,2},{1,7},{2,4},{3,1},{4,6},{5,3},{6,0},{7,5},{8,10},{9,15},{10,... | collective-permute-start | bytes 1032200 | tf_op jit(solution)/shard_map/ppermute | solution.py:373
  46.1 0.0 collective-permute-done.6.rest_6_
  46.1 3.5 %collective-permute-start.7 = (f32[2,32,128]{2,1,0:T(8,128)S(1)}, f32[2,32,128]{2,1,0:T(8,128)S(1)}, u32[]{:S(2)}, u32[]{:S(2)}) collective-permute-start(f32[2,32,128]{2,1,0:T(8,128)S(1)} %pad_maximum_fusion.1), channel_id=1, source_target_pairs={{0,8},{2,10},{4,12},{6,14},{8,16},{9,1},{10,18},{11,3},{12,20},{13... | collective-permute-start | bytes 98312 | tf_op jit(solution)/shard_map/ppermute | solution.py:402
  49.6 5.7 %collective-permute-done.7 = f32[2,32,128]{2,1,0:T(8,128)S(1)} collective-permute-done((f32[2,32,128]{2,1,0:T(8,128)S(1)}, f32[2,32,128]{2,1,0:T(8,128)S(1)}, u32[]{:S(2)}, u32[]{:S(2)}) %collective-permute-start.7) | collective-permute-done | bytes 32800 | tf_op jit(solution)/shard_map/ppermute | solution.py:402
  55.3 0.0 collective-permute-start.8
  55.3 2.2 %collective-permute-done.10.rest_3_ = f32[21,32,128]{2,1,0:T(8,128)S(1)} collective-permute-done((f32[21,32,128]{2,1,0:T(8,128)S(1)}, f32[21,32,128]{2,1,0:T(8,128)S(1)}, u32[]{:S(2)}, u32[]{:S(2)}) %collective-permute-start.10) | collective-permute-done | bytes 344096 | tf_op jit(solution)/shard_map/ppermute | solution.py:373
  57.6 0.0 collective-permute-done.8
  57.6 5.3 %collective-permute-start.12 = (f32[25,32,128]{2,1,0:T(8,128)S(1)}, f32[25,32,128]{2,1,0:T(8,128)S(1)}, u32[]{:S(2)}, u32[]{:S(2)}) collective-permute-start(f32[25,32,128]{2,1,0:T(8,128)S(1)} %pad_maximum_fusion), channel_id=1, source_target_pairs={{0,2},{1,7},{2,4},{3,1},{4,6},{5,3},{6,0},{7,5},{8,10},{9,15},{10,... | collective-permute-start | bytes 1228808 | tf_op jit(solution)/shard_map/ppermute | solution.py:373
  63.0 2.1 %collective-permute-start.11 = (f32[21,32,128]{2,1,0:T(8,128)S(1)}, f32[21,32,128]{2,1,0:T(8,128)S(1)}, u32[]{:S(2)}, u32[]{:S(2)}) collective-permute-start(f32[21,32,128]{2,1,0:T(8,128)S(1)} %slice.37), channel_id=1, source_target_pairs={{0,2},{1,7},{2,4},{3,1},{4,6},{5,3},{6,0},{7,5},{8,10},{9,15},{10,... | collective-permute-start | bytes 1032200 | tf_op jit(solution)/shard_map/ppermute | solution.py:373
  65.1 4.5 %collective-permute-done.12.rest_5_ = f32[25,32,128]{2,1,0:T(8,128)S(1)} collective-permute-done((f32[25,32,128]{2,1,0:T(8,128)S(1)}, f32[25,32,128]{2,1,0:T(8,128)S(1)}, u32[]{:S(2)}, u32[]{:S(2)}) %collective-permute-start.12) | collective-permute-done | bytes 409632 | tf_op jit(solution)/shard_map/ppermute | solution.py:373
  69.6 3.3 %collective-permute-start.15 = (f32[25,32,128]{2,1,0:T(8,128)S(1)}, f32[25,32,128]{2,1,0:T(8,128)S(1)}, u32[]{:S(2)}, u32[]{:S(2)}) collective-permute-start(f32[25,32,128]{2,1,0:T(8,128)S(1)} %collective-permute-done.12.rest_5_), channel_id=1, source_target_pairs={{0,1},{1,0},{2,3},{3,2},{4,5},{5,4},{6,7},{7,6},{8,9},{9,8},{10,11... | collective-permute-start | bytes 1228808 | tf_op jit(solution)/shard_map/ppermute | solution.py:376
  72.9 0.0 collective-permute-start.13
  72.9 7.3 %collective-permute-done.11.rest_4_ = f32[21,32,128]{2,1,0:T(8,128)S(1)} collective-permute-done((f32[21,32,128]{2,1,0:T(8,128)S(1)}, f32[21,32,128]{2,1,0:T(8,128)S(1)}, u32[]{:S(2)}, u32[]{:S(2)}) %collective-permute-start.11) | collective-permute-done | bytes 344096 | tf_op jit(solution)/shard_map/ppermute | solution.py:373
  80.2 0.0 collective-permute-start.14
  80.2 6.1 %collective-permute-start.9 = (f32[4,32,128]{2,1,0:T(8,128)S(1)}, f32[4,32,128]{2,1,0:T(8,128)S(1)}, u32[]{:S(2)}, u32[]{:S(2)}) collective-permute-start(f32[4,32,128]{2,1,0:T(8,128)S(1)} %constant_dynamic-update-slice_fusion.rest_0_), channel_id=1, source_target_pairs={{0,4},{1,5},{2,6},{3,7},{4,0},{5,1},{6,2},{7,3},{8,12},{9,13},{10,... | collective-permute-start | bytes 196616 | tf_op jit(solution)/shard_map/ppermute | solution.py:405
  86.3 4.3 %collective-permute-done.9.rest_1_ = f32[4,32,128]{2,1,0:T(8,128)S(1)} collective-permute-done((f32[4,32,128]{2,1,0:T(8,128)S(1)}, f32[4,32,128]{2,1,0:T(8,128)S(1)}, u32[]{:S(2)}, u32[]{:S(2)}) %collective-permute-start.9) | collective-permute-done | bytes 65568 | tf_op jit(solution)/shard_map/ppermute | solution.py:405
  90.6 0.0 collective-permute-done.13.rest_7_
  90.6 0.0 collective-permute-done.14.rest_8_
  90.6 0.0 collective-permute-done.15.rest_9_
  90.6 0.0 copy-done
  90.6 5.1 %correct.1 = f32[4,7,32,1024]{3,2,1,0:T(8,128)} custom-call(f32[4,7,32,1024]{3,2,1,0:T(8,128)S(1)} %get-tuple-element.17.refl, f32[8,4,2,32,128]{4,3,2,1,0:T(8,128)S(1)} %get-tuple-element.24.kernels, f32[32,1024]{1,0:T(8,128)S(1)} %copy-done, f32[4,32,128]{2,1,0:T(8,128)S(1)} %constant_dynamic-update-slice_fusion.rest_0_, ...), custom_call_target="tpu_custom_call" | custom-call | tf_op jit(solution)/shard_map/correct/pallas_call | solution.py:355
  (8 shorter events, 0.1 us)
Async XLA Ops:
  4.5 8.5 %collective-permute-start = (f32[3,27,32,128]{3,2,1,0:T(8,128)S(1)}, f32[3,27,32,128]{3,2,1,0:T(8,128)S(1)}, u32[]{:S(2)}, u32[]{:S(2)}) collective-permute-start(f32[3,27,32,128]{3,2,1,0:T(8,128)S(1)} %get-tuple-element.26), channel_id=1, source_target_pairs={{0,1},{1,0},{2,3},{3,2},{4,5},{5,4},{6,7},{7,6},{8,9},{9,8},{10,11... | collective-permute-start | bytes 3981320 | tf_op jit(solution)/shard_map/ppermute | solution.py:376
  4.6 3.7 %collective-permute-start.3 = (f32[1,27,32,128]{3,2,1,0:T(8,128)S(1)}, f32[1,27,32,128]{3,2,1,0:T(8,128)S(1)}, u32[]{:S(2)}, u32[]{:S(2)}) collective-permute-start(f32[1,27,32,128]{3,2,1,0:T(8,128)S(1)} %get-tuple-element.28), channel_id=1, source_target_pairs={{0,1},{1,0},{2,3},{3,2},{4,5},{5,4},{6,7},{7,6},{8,9},{9,8},{10,11... | collective-permute-start | bytes 1327112 | tf_op jit(solution)/shard_map/ppermute | solution.py:376
  8.3 14.2 %collective-permute-start.4 = (f32[27,32,128]{2,1,0:T(8,128)S(1)}, f32[27,32,128]{2,1,0:T(8,128)S(1)}, u32[]{:S(2)}, u32[]{:S(2)}) collective-permute-start(f32[27,32,128]{2,1,0:T(8,128)S(1)} %add_bitcast_fusion), channel_id=1, source_target_pairs={{0,2},{1,7},{2,4},{3,1},{4,6},{5,3},{6,0},{7,5},{8,10},{9,15},{10,... | collective-permute-start | bytes 1327112 | tf_op jit(solution)/shard_map/ppermute | solution.py:373
  13.0 16.2 %collective-permute-start.1 = (f32[27,32,128]{2,1,0:T(8,128)S(1)}, f32[27,32,128]{2,1,0:T(8,128)S(1)}, u32[]{:S(2)}, u32[]{:S(2)}) collective-permute-start(f32[27,32,128]{2,1,0:T(8,128)S(1)} %fusion.2), channel_id=1, source_target_pairs={{0,2},{1,7},{2,4},{3,1},{4,6},{5,3},{6,0},{7,5},{8,10},{9,15},{10,... | collective-permute-start | bytes 1327112 | tf_op jit(solution)/shard_map/ppermute | solution.py:373
  22.6 14.0 %collective-permute-start.5 = (f32[27,32,128]{2,1,0:T(8,128)S(1)}, f32[27,32,128]{2,1,0:T(8,128)S(1)}, u32[]{:S(2)}, u32[]{:S(2)}) collective-permute-start(f32[27,32,128]{2,1,0:T(8,128)S(1)} %fusion.1), channel_id=1, source_target_pairs={{0,2},{1,7},{2,4},{3,1},{4,6},{5,3},{6,0},{7,5},{8,10},{9,15},{10,... | collective-permute-start | bytes 1327112 | tf_op jit(solution)/shard_map/ppermute | solution.py:373
  29.3 8.7 %collective-permute-start.2 = (f32[27,32,128]{2,1,0:T(8,128)S(1)}, f32[27,32,128]{2,1,0:T(8,128)S(1)}, u32[]{:S(2)}, u32[]{:S(2)}) collective-permute-start(f32[27,32,128]{2,1,0:T(8,128)S(1)} %collective-permute-done.1), channel_id=1, source_target_pairs={{0,1},{1,0},{2,3},{3,2},{4,5},{5,4},{6,7},{7,6},{8,9},{9,8},{10,11... | collective-permute-start | bytes 1327112 | tf_op jit(solution)/shard_map/ppermute | solution.py:376
  38.3 52.3 %copy-start = (f32[32,1024]{1,0:T(8,128)S(1)}, f32[32,1024]{1,0:T(8,128)}, u32[]{:S(2)}) copy-start(f32[32,1024]{1,0:T(8,128)} %nadir.1) | copy-start | bytes 393220
  38.3 7.8 %collective-permute-start.6 = (f32[23,32,128]{2,1,0:T(8,128)S(1)}, f32[23,32,128]{2,1,0:T(8,128)S(1)}, u32[]{:S(2)}, u32[]{:S(2)}) collective-permute-start(f32[23,32,128]{2,1,0:T(8,128)S(1)} %solve.1.rest_2_), channel_id=1, source_target_pairs={{0,1},{1,0},{2,3},{3,2},{4,5},{5,4},{6,7},{7,6},{8,9},{9,8},{10,11... | collective-permute-start | bytes 1130504 | tf_op jit(solution)/shard_map/ppermute | solution.py:376
  43.9 13.6 %collective-permute-start.10 = (f32[21,32,128]{2,1,0:T(8,128)S(1)}, f32[21,32,128]{2,1,0:T(8,128)S(1)}, u32[]{:S(2)}, u32[]{:S(2)}) collective-permute-start(f32[21,32,128]{2,1,0:T(8,128)S(1)} %slice.36), channel_id=1, source_target_pairs={{0,2},{1,7},{2,4},{3,1},{4,6},{5,3},{6,0},{7,5},{8,10},{9,15},{10,... | collective-permute-start | bytes 1032200 | tf_op jit(solution)/shard_map/ppermute | solution.py:373
  46.1 9.2 %collective-permute-start.7 = (f32[2,32,128]{2,1,0:T(8,128)S(1)}, f32[2,32,128]{2,1,0:T(8,128)S(1)}, u32[]{:S(2)}, u32[]{:S(2)}) collective-permute-start(f32[2,32,128]{2,1,0:T(8,128)S(1)} %pad_maximum_fusion.1), channel_id=1, source_target_pairs={{0,8},{2,10},{4,12},{6,14},{8,16},{9,1},{10,18},{11,3},{12,20},{13... | collective-permute-start | bytes 98312 | tf_op jit(solution)/shard_map/ppermute | solution.py:402
  55.3 2.2 %collective-permute-start.8 = (f32[2,32,128]{2,1,0:T(8,128)S(1)}, f32[2,32,128]{2,1,0:T(8,128)S(1)}, u32[]{:S(2)}, u32[]{:S(2)}) collective-permute-start(f32[2,32,128]{2,1,0:T(8,128)S(1)} %collective-permute-done.7), channel_id=1, source_target_pairs={{0,1},{1,0},{2,3},{3,2},{4,5},{5,4},{6,7},{7,6},{8,9},{9,8},{10,11... | collective-permute-start | bytes 98312 | tf_op jit(solution)/shard_map/ppermute | solution.py:376
  57.6 12.0 %collective-permute-start.12 = (f32[25,32,128]{2,1,0:T(8,128)S(1)}, f32[25,32,128]{2,1,0:T(8,128)S(1)}, u32[]{:S(2)}, u32[]{:S(2)}) collective-permute-start(f32[25,32,128]{2,1,0:T(8,128)S(1)} %pad_maximum_fusion), channel_id=1, source_target_pairs={{0,2},{1,7},{2,4},{3,1},{4,6},{5,3},{6,0},{7,5},{8,10},{9,15},{10,... | collective-permute-start | bytes 1228808 | tf_op jit(solution)/shard_map/ppermute | solution.py:373
  63.0 17.2 %collective-permute-start.11 = (f32[21,32,128]{2,1,0:T(8,128)S(1)}, f32[21,32,128]{2,1,0:T(8,128)S(1)}, u32[]{:S(2)}, u32[]{:S(2)}) collective-permute-start(f32[21,32,128]{2,1,0:T(8,128)S(1)} %slice.37), channel_id=1, source_target_pairs={{0,2},{1,7},{2,4},{3,1},{4,6},{5,3},{6,0},{7,5},{8,10},{9,15},{10,... | collective-permute-start | bytes 1032200 | tf_op jit(solution)/shard_map/ppermute | solution.py:373
  69.6 21.0 %collective-permute-start.15 = (f32[25,32,128]{2,1,0:T(8,128)S(1)}, f32[25,32,128]{2,1,0:T(8,128)S(1)}, u32[]{:S(2)}, u32[]{:S(2)}) collective-permute-start(f32[25,32,128]{2,1,0:T(8,128)S(1)} %collective-permute-done.12.rest_5_), channel_id=1, source_target_pairs={{0,1},{1,0},{2,3},{3,2},{4,5},{5,4},{6,7},{7,6},{8,9},{9,8},{10,11... | collective-permute-start | bytes 1228808 | tf_op jit(solution)/shard_map/ppermute | solution.py:376
  72.9 17.8 %collective-permute-start.13 = (f32[21,32,128]{2,1,0:T(8,128)S(1)}, f32[21,32,128]{2,1,0:T(8,128)S(1)}, u32[]{:S(2)}, u32[]{:S(2)}) collective-permute-start(f32[21,32,128]{2,1,0:T(8,128)S(1)} %collective-permute-done.10.rest_3_), channel_id=1, source_target_pairs={{0,1},{1,0},{2,3},{3,2},{4,5},{5,4},{6,7},{7,6},{8,9},{9,8},{10,11... | collective-permute-start | bytes 1032200 | tf_op jit(solution)/shard_map/ppermute | solution.py:376
  80.2 10.4 %collective-permute-start.14 = (f32[21,32,128]{2,1,0:T(8,128)S(1)}, f32[21,32,128]{2,1,0:T(8,128)S(1)}, u32[]{:S(2)}, u32[]{:S(2)}) collective-permute-start(f32[21,32,128]{2,1,0:T(8,128)S(1)} %collective-permute-done.11.rest_4_), channel_id=1, source_target_pairs={{0,1},{1,0},{2,3},{3,2},{4,5},{5,4},{6,7},{7,6},{8,9},{9,8},{10,11... | collective-permute-start | bytes 1032200 | tf_op jit(solution)/shard_map/ppermute | solution.py:376
  80.2 10.4 %collective-permute-start.9 = (f32[4,32,128]{2,1,0:T(8,128)S(1)}, f32[4,32,128]{2,1,0:T(8,128)S(1)}, u32[]{:S(2)}, u32[]{:S(2)}) collective-permute-start(f32[4,32,128]{2,1,0:T(8,128)S(1)} %constant_dynamic-update-slice_fusion.rest_0_), channel_id=1, source_target_pairs={{0,4},{1,5},{2,6},{3,7},{4,0},{5,1},{6,2},{7,3},{8,12},{9,13},{10,... | collective-permute-start | bytes 196616 | tf_op jit(solution)/shard_map/ppermute | solution.py:405
